TPU v7x, 256 devices: a whole 4x4x8 slice. The times are simulated.
256 devices in a mesh: row: 16 (over z, core), col: 16 (over x, y).
Axes of the slice: x: 4, y: 4, z: 8, core: 2. Of those that a mesh axis runs over, the one named last changes fastest.
Arguments:
- inputs: bfloat16 [3, 64, 128, 2048], P(None, None, 'row', 'col'), may hold values from -6 to 6
- gate_pre: bfloat16 [3, 256, 128, 2048], P(None, None, 'row', 'col'), may hold values from -8 to 8
- cotangent: bfloat16 [3, 64, 128, 2048], P(None, None, 'row', 'col'), may hold values from -6 to 6
- hidden_init: bfloat16 [64, 128, 2048], P(None, 'row', 'col'), may hold values from -6 to 6
- cell_init: float32 [64, 128, 2048], P(None, 'row', 'col'), may hold values from -6 to 6
- land_mask: int32 [128, 2048], P('row', 'col'), may hold values 0 or 1
- kernel: bfloat16 [256, 1152], replicated, may hold values from -0.1875 to 0.1875
Outputs:
- grad_inputs: bfloat16 [3, 64, 128, 2048], P(None, None, 'row', 'col')
- grad_hidden: float32 [64, 128, 2048], P(None, 'row', 'col')
- grad_cell: float32 [64, 128, 2048], P(None, 'row', 'col')
- grad_kernel: float32 [256, 1152], P('row', 'col')
- grad_bias: float32 [256], P(('row', 'col'))
Inputs may be any that keep to these rules, and one draw needn't show every extreme that they name: `land_mask`: 1 marks a land cell.
All inputs are finite; a program needn't handle non-finite values. No bound on the sum of `land_mask` on one device may be relied on, other than what follows from the above.
Results may differ from a plain program's by a relative error of at most 0.005.
Values may be sent and summed in bfloat16 or wider, within the bound.
No kernel may reach another device: no remote copies, remote signals or barrier semaphores. Data moves between devices by JAX's collectives and lax.ppermute only.
A program may use at most 64 MiB of HBM per device.

v0:
```python
import math

import jax
import jax.numpy as jnp
from jax import lax
from jax.sharding import PartitionSpec as P


def with_halo(block, sides, width):
    for axis, dim in sides:
        count = lax.axis_size(axis)
        forward = [(i, i + 1) for i in range(count - 1)]
        backward = [(target, source) for source, target in forward]
        low = lax.ppermute(
            lax.slice_in_dim(block, block.shape[dim] - width, None, axis=dim), axis, forward
        )
        high = lax.ppermute(lax.slice_in_dim(block, 0, width, axis=dim), axis, backward)
        block = jnp.concatenate([low, block, high], axis=dim)
    return block


def gate_parts(pre, hidden):
    return (
        jax.nn.sigmoid(pre[:hidden]),
        jax.nn.sigmoid(pre[hidden : 2 * hidden]),
        jax.nn.sigmoid(pre[2 * hidden : 3 * hidden]),
        jnp.tanh(pre[3 * hidden :]),
    )


def kernel_terms(grads, padded, rows, cols):
    flat = grads.reshape(grads.shape[0], rows * cols)
    blocks = []
    for offset in range(9):
        upper, left = (offset // 3, offset % 3)
        window = padded[:, upper : upper + rows, left : left + cols].reshape(
            padded.shape[0], rows * cols
        )
        blocks.append(
            lax.dot_general(
                flat, window, (((1,), (1,)), ((), ())), preferred_element_type=jnp.float32
            )
        )
    return jnp.concatenate(blocks, axis=1)


def transposed(kernel, padded_grads, rows, cols, width):
    total = jnp.zeros((width, rows * cols), jnp.float32)
    for offset in range(9):
        upper, left = (offset // 3, offset % 3)
        window = padded_grads[:, 2 - upper : 2 - upper + rows, 2 - left : 2 - left + cols]
        window = window.reshape(padded_grads.shape[0], rows * cols)
        piece = kernel[:, offset * width : (offset + 1) * width]
        total = total + lax.dot_general(
            piece, window, (((0,), (0,)), ((), ())), preferred_element_type=jnp.float32
        )
    return total


def reduce_grads(kernel_part, bias_part):
    row_kernel, row_bias = (
        lax.psum_scatter(kernel_part, "row", scatter_dimension=0, tiled=True),
        lax.psum_scatter(bias_part, "row", scatter_dimension=0, tiled=True),
    )
    return (
        lax.psum_scatter(row_kernel, "col", scatter_dimension=1, tiled=True),
        lax.psum_scatter(row_bias, "col", scatter_dimension=0, tiled=True),
    )


def shards(inputs, gate_pre, cotangent, hidden_init, cell_init, land_mask, kernel):
    steps = inputs.shape[0]
    width_in = inputs.shape[1]
    hidden = hidden_init.shape[0]
    width = width_in + hidden
    rows, cols = land_mask.shape
    mask = land_mask.astype(jnp.float32)
    scale = 1.0 / math.sqrt(rows * cols * lax.axis_size("row") * lax.axis_size("col"))
    states = [cell_init]
    layers = []
    hidden_now = hidden_init
    acts = []
    for step in range(steps):
        gates = gate_parts(gate_pre[step].astype(jnp.float32), hidden)
        acts.append(gates)
        layers.append(jnp.concatenate([inputs[step], hidden_now], axis=0))
        new_cell = gates[1] * states[-1] + gates[0] * gates[3]
        states.append(new_cell)
        hidden_now = (mask * gates[2] * jnp.tanh(new_cell)).astype(jnp.bfloat16)
    grad_h = jnp.zeros((hidden, rows, cols), jnp.float32)
    grad_c = jnp.zeros((hidden, rows, cols), jnp.float32)
    kernel_total = None
    bias_total = None
    outs = [None] * steps
    for step in reversed(range(steps)):
        gin, gfor, gout, gcand = acts[step]
        tanh_cell = jnp.tanh(states[step + 1])
        error = mask * (grad_h + cotangent[step].astype(jnp.float32))
        grad_c = grad_c + error * gout * (1.0 - tanh_cell * tanh_cell)
        grads = jnp.concatenate(
            [
                grad_c * gcand * gin * (1.0 - gin),
                grad_c * states[step] * gfor * (1.0 - gfor),
                error * tanh_cell * gout * (1.0 - gout),
                grad_c * gin * (1.0 - gcand * gcand),
            ],
            axis=0,
        ).astype(jnp.bfloat16)
        grad_c = grad_c * gfor
        padded_grads = with_halo(grads, (("row", 1), ("col", 2)), 1)
        padded = with_halo(layers[step], (("row", 1), ("col", 2)), 1)
        kernel_part = scale * kernel_terms(grads, padded, rows, cols)
        bias_part = scale * jnp.sum(grads.astype(jnp.float32), axis=(1, 2))
        reduced_kernel, reduced_bias = reduce_grads(kernel_part, bias_part)
        if kernel_total is None:
            kernel_total, bias_total = (reduced_kernel, reduced_bias)
        else:
            kernel_total = kernel_total + reduced_kernel
            bias_total = bias_total + reduced_bias
        back = transposed(kernel, padded_grads, rows, cols, width)
        outs[step] = back[:width_in].reshape(width_in, rows, cols).astype(jnp.bfloat16)
        grad_h = back[width_in:].reshape(hidden, rows, cols)
    return (jnp.stack(outs), grad_h, grad_c, kernel_total, bias_total)


def solution(mesh):
    placed = (
        P(None, None, "row", "col"),
        P(None, None, "row", "col"),
        P(None, None, "row", "col"),
        P(None, "row", "col"),
        P(None, "row", "col"),
        P("row", "col"),
        P(),
    )
    return jax.shard_map(
        shards,
        mesh=mesh,
        in_specs=placed,
        out_specs=(
            P(None, None, "row", "col"),
            P(None, "row", "col"),
            P(None, "row", "col"),
            P("row", "col"),
            P(("row", "col")),
        ),
        check_vma=False,
    )
```

profile of v0, /device:TPU:1, one launch (start us, length us, event | category | flops | bytes accessed | tf_op | source)
XLA Modules:
  0.0 381.5 jit_solution(3137953251659456467)
XLA Ops:
  13.9 5.1 %collective-permute-start.1 = (bf16[256,1,128]{2,0,1:T(8,128)(2,1)}, bf16[256,1,128]{2,0,1:T(8,128)(2,1)}, u32[]{:S(2)}, u32[]{:S(2)}) collective-permute-start(bf16[256,1,128]{2,0,1:T(8,128)(2,1)} %get-tuple-element.91), channel_id=1, source_target_pairs={{16,0},{32,16},{48,32},{64,48},{80,64},{96,80},{112,96},{128,112},... | collective-permute-start | bytes 196616 | tf_op jit(solution)/shard_map/ppermute | solution.py:17
  21.8 3.0 collective-permute-start.21
  24.8 2.5 collective-permute-start.20
  28.1 2.4 collective-permute-start.13
  35.6 3.3 collective-permute-start.12
  41.9 3.8 collective-permute-start.16
  49.3 4.6 %collective-permute-start.14 = (bf16[128,10,1]{2,0,1:T(8,128)(2,1)S(1)}, bf16[128,10,1]{2,0,1:T(8,128)(2,1)S(1)}, u32[]{:S(2)}, u32[]{:S(2)}) collective-permute-start(bf16[128,10,1]{2,0,1:T(8,128)(2,1)S(1)} %get-tuple-element.105), channel_id=1, source_target_pairs={{0,1},{1,2},{2,3},{3,4},{4,5},{5,6},{6,7},{7,8},{8,9},{9,10},{10,1... | collective-permute-start | bytes 7688 | tf_op jit(solution)/shard_map/ppermute | solution.py:14
  54.2 9.1 %collective-permute-done.15 = bf16[128,10,1]{2,0,1:T(8,128)(2,1)S(1)} collective-permute-done((bf16[128,10,1]{2,0,1:T(8,128)(2,1)S(1)}, bf16[128,10,1]{2,0,1:T(8,128)(2,1)S(1)}, u32[]{:S(2)}, u32[]{:S(2)}) %collective-permute-start.15) | collective-permute-done | bytes 2592 | tf_op jit(solution)/shard_map/ppermute | solution.py:17
  63.3 3.0 collective-permute-start.22
  73.6 4.0 %collective-permute-start.18 = (bf16[128,10,1]{2,0,1:T(8,128)(2,1)S(1)}, bf16[128,10,1]{2,0,1:T(8,128)(2,1)S(1)}, u32[]{:S(2)}, u32[]{:S(2)}) collective-permute-start(bf16[128,10,1]{2,0,1:T(8,128)(2,1)S(1)} %get-tuple-element.101), channel_id=1, source_target_pairs={{0,1},{1,2},{2,3},{3,4},{4,5},{5,6},{6,7},{7,8},{8,9},{9,10},{10,1... | collective-permute-start | bytes 7688 | tf_op jit(solution)/shard_map/ppermute | solution.py:14
  77.6 2.3 pad_maximum_fusion.8
  79.9 4.2 %collective-permute-done.18 = bf16[128,10,1]{2,0,1:T(8,128)(2,1)S(1)} collective-permute-done((bf16[128,10,1]{2,0,1:T(8,128)(2,1)S(1)}, bf16[128,10,1]{2,0,1:T(8,128)(2,1)S(1)}, u32[]{:S(2)}, u32[]{:S(2)}) %collective-permute-start.18) | collective-permute-done | bytes 2592 | tf_op jit(solution)/shard_map/ppermute | solution.py:14
  90.5 2.1 copy.89
  92.6 6.3 %collective-permute-start.3 = (bf16[256,10,1]{0,1,2:T(8,128)(2,1)}, bf16[256,10,1]{0,1,2:T(8,128)(2,1)}, u32[]{:S(2)}, u32[]{:S(2)}) collective-permute-start(bf16[256,10,1]{0,1,2:T(8,128)(2,1)} %copy.89), channel_id=1, source_target_pairs={{0,1},{1,2},{2,3},{3,4},{4,5},{5,6},{6,7},{7,8},{8,9},{9,10},{10,1... | collective-permute-start | bytes 15368 | tf_op jit(solution)/shard_map/ppermute | solution.py:14
  108.7 3.2 pad_maximum_fusion
  113.2 2.1 copy.91
  122.5 2.1 copy.98
  124.6 2.0 copy.100
  136.3 3.4 collective-permute-start.5
  139.7 3.4 collective-permute-start.4
  150.4 4.6 %collective-permute-start.7 = (bf16[256,10,1]{0,1,2:T(8,128)(2,1)S(1)}, bf16[256,10,1]{0,1,2:T(8,128)(2,1)S(1)}, u32[]{:S(2)}, u32[]{:S(2)}) collective-permute-start(bf16[256,10,1]{0,1,2:T(8,128)(2,1)S(1)} %copy.107), channel_id=1, source_target_pairs={{0,1},{1,2},{2,3},{3,4},{4,5},{5,6},{6,7},{7,8},{8,9},{9,10},{10,1... | collective-permute-start | bytes 15368 | tf_op jit(solution)/shard_map/ppermute | solution.py:14
  157.1 2.2 fusion.157
  162.6 3.0 pad_maximum_fusion.1
  166.9 2.1 copy.109
  174.7 2.1 copy.118
  188.0 3.6 collective-permute-start.8
  199.9 24.0 %all-reduce.1 = f32[256]{0:T(256)S(1)} all-reduce(f32[256]{0:T(256)S(1)} %add_multiply_fusion.1), channel_id=12, replica_groups=mesh['row'=16,'col'=16] {'row'}, use_global_device_ids=true, to_apply=%region_7.0.clone | all-reduce | flops 256 | bytes 2048
  224.1 33.4 %all-reduce.2 = f32[16]{0:T(128)S(1)} all-reduce(f32[16]{0:T(128)S(1)} %dynamic-slice.3), channel_id=13, replica_groups=mesh['row'=16,'col'=16] {'col'}, use_global_device_ids=true, to_apply=%region_8.0.clone | all-reduce | flops 16 | bytes 128
  261.3 4.2 %collective-permute-start.11 = (bf16[256,10,1]{0,1,2:T(8,128)(2,1)S(1)}, bf16[256,10,1]{0,1,2:T(8,128)(2,1)S(1)}, u32[]{:S(2)}, u32[]{:S(2)}) collective-permute-start(bf16[256,10,1]{0,1,2:T(8,128)(2,1)S(1)} %copy.126), channel_id=1, source_target_pairs={{0,1},{1,2},{2,3},{3,4},{4,5},{5,6},{6,7},{7,8},{8,9},{9,10},{10,1... | collective-permute-start | bytes 15368 | tf_op jit(solution)/shard_map/ppermute | solution.py:14
  268.1 2.7 pad_maximum_fusion.2
  281.7 10.6 %reduce-scatter.7.cloned.1.call-done = f32[16,1152]{1,0:T(8,128)} async-done(((f32[256,1152]{1,0:T(8,128)}), f32[16,1152]{1,0:T(8,128)}) %reduce-scatter.7.cloned.1.call-update) | async-done | bytes 73744
  295.8 77.4 %reduce-scatter.9.cloned.1.call-done = f32[16,72]{0,1:T(8,128)} async-done(((f32[16,1152]{0,1:T(8,128)}), f32[16,72]{0,1:T(8,128)}) %reduce-scatter.9.cloned.1.call-update) | async-done | bytes 4624
  (356 shorter events, 123.1 us)
Async XLA Ops:
  7.2 285.1 %reduce-scatter.7.cloned.1.call-start = ((), (), s32[]{:S(2)}) async-start(), calls=%async_computation.2 | async-start | bytes 1253376
  12.7 86.3 %copy-start.2 = (bf16[64,8,128]{2,0,1:T(8,128)(2,1)}, bf16[64,8,128]{2,0,1:T(8,128)(2,1)S(1)}, u32[]{:S(2)}) copy-start(bf16[64,8,128]{2,0,1:T(8,128)(2,1)S(1)} %get-tuple-element.65) | copy-start | bytes 393220
  12.7 86.3 %copy-start.3 = (bf16[64,8,128]{2,0,1:T(8,128)(2,1)}, bf16[64,8,128]{2,0,1:T(8,128)(2,1)S(1)}, u32[]{:S(2)}) copy-start(bf16[64,8,128]{2,0,1:T(8,128)(2,1)S(1)} %get-tuple-element.66) | copy-start | bytes 393220
  12.7 86.3 %copy-start.4 = (bf16[64,8,128]{2,0,1:T(8,128)(2,1)}, bf16[64,8,128]{2,0,1:T(8,128)(2,1)S(1)}, u32[]{:S(2)}) copy-start(bf16[64,8,128]{2,0,1:T(8,128)(2,1)S(1)} %get-tuple-element.67) | copy-start | bytes 393220
  13.9 71.6 %collective-permute-start.1 = (bf16[256,1,128]{2,0,1:T(8,128)(2,1)}, bf16[256,1,128]{2,0,1:T(8,128)(2,1)}, u32[]{:S(2)}, u32[]{:S(2)}) collective-permute-start(bf16[256,1,128]{2,0,1:T(8,128)(2,1)} %get-tuple-element.91), channel_id=1, source_target_pairs={{16,0},{32,16},{48,32},{64,48},{80,64},{96,80},{112,96},{128,112},... | collective-permute-start | bytes 196616 | tf_op jit(solution)/shard_map/ppermute | solution.py:17
  19.0 66.5 %collective-permute-start = (bf16[256,1,128]{2,0,1:T(8,128)(2,1)}, bf16[256,1,128]{2,0,1:T(8,128)(2,1)}, u32[]{:S(2)}, u32[]{:S(2)}) collective-permute-start(bf16[256,1,128]{2,0,1:T(8,128)(2,1)} %get-tuple-element.90), channel_id=1, source_target_pairs={{0,16},{16,32},{32,48},{48,64},{64,80},{80,96},{96,112},{112,128},... | collective-permute-start | bytes 196616 | tf_op jit(solution)/shard_map/ppermute | solution.py:14
  21.0 56.6 %copy-start.25 = (bf16[64,8,128]{2,0,1:T(8,128)(2,1)}, bf16[64,8,128]{2,0,1:T(8,128)(2,1)S(1)}, u32[]{:S(2)}) copy-start(bf16[64,8,128]{2,0,1:T(8,128)(2,1)S(1)} %copy.141) | copy-start | bytes 393220
  21.1 56.5 %copy-start.27 = (bf16[64,8,128]{2,0,1:T(8,128)(2,1)}, bf16[64,8,128]{2,0,1:T(8,128)(2,1)S(1)}, u32[]{:S(2)}) copy-start(bf16[64,8,128]{2,0,1:T(8,128)(2,1)S(1)} %get-tuple-element.118) | copy-start | bytes 393220
  21.8 13.8 %collective-permute-start.21 = (bf16[128,1,128]{2,0,1:T(8,128)(2,1)}, bf16[128,1,128]{2,0,1:T(8,128)(2,1)}, u32[]{:S(2)}, u32[]{:S(2)}) collective-permute-start(bf16[128,1,128]{2,0,1:T(8,128)(2,1)} %get-tuple-element.115), channel_id=1, source_target_pairs={{16,0},{32,16},{48,32},{64,48},{80,64},{96,80},{112,96},{128,112},... | collective-permute-start | bytes 98312 | tf_op jit(solution)/shard_map/ppermute | solution.py:17
  24.8 14.1 %collective-permute-start.20 = (bf16[128,1,128]{2,0,1:T(8,128)(2,1)}, bf16[128,1,128]{2,0,1:T(8,128)(2,1)}, u32[]{:S(2)}, u32[]{:S(2)}) collective-permute-start(bf16[128,1,128]{2,0,1:T(8,128)(2,1)} %get-tuple-element.114), channel_id=1, source_target_pairs={{0,16},{16,32},{32,48},{48,64},{64,80},{80,96},{96,112},{112,128},... | collective-permute-start | bytes 98312 | tf_op jit(solution)/shard_map/ppermute | solution.py:14
  28.1 13.8 %collective-permute-start.13 = (bf16[128,1,128]{2,0,1:T(8,128)(2,1)}, bf16[128,1,128]{2,0,1:T(8,128)(2,1)}, u32[]{:S(2)}, u32[]{:S(2)}) collective-permute-start(bf16[128,1,128]{2,0,1:T(8,128)(2,1)} %get-tuple-element.113), channel_id=1, source_target_pairs={{16,0},{32,16},{48,32},{64,48},{80,64},{96,80},{112,96},{128,112},... | collective-permute-start | bytes 98312 | tf_op jit(solution)/shard_map/ppermute | solution.py:17
  35.6 10.1 %collective-permute-start.12 = (bf16[128,1,128]{2,0,1:T(8,128)(2,1)}, bf16[128,1,128]{2,0,1:T(8,128)(2,1)S(1)}, u32[]{:S(2)}, u32[]{:S(2)}) collective-permute-start(bf16[128,1,128]{2,0,1:T(8,128)(2,1)} %get-tuple-element.112), channel_id=1, source_target_pairs={{0,16},{16,32},{32,48},{48,64},{64,80},{80,96},{96,112},{112,128},... | collective-permute-start | bytes 98312 | tf_op jit(solution)/shard_map/ppermute | solution.py:14
  39.0 9.0 %collective-permute-start.17 = (bf16[128,1,128]{2,0,1:T(8,128)(2,1)}, bf16[128,1,128]{2,0,1:T(8,128)(2,1)S(1)}, u32[]{:S(2)}, u32[]{:S(2)}) collective-permute-start(bf16[128,1,128]{2,0,1:T(8,128)(2,1)} %get-tuple-element.111), channel_id=1, source_target_pairs={{16,0},{32,16},{48,32},{64,48},{80,64},{96,80},{112,96},{128,112},... | collective-permute-start | bytes 98312 | tf_op jit(solution)/shard_map/ppermute | solution.py:17
  41.9 7.4 %collective-permute-start.16 = (bf16[128,1,128]{2,0,1:T(8,128)(2,1)S(1)}, bf16[128,1,128]{2,0,1:T(8,128)(2,1)S(1)}, u32[]{:S(2)}, u32[]{:S(2)}) collective-permute-start(bf16[128,1,128]{2,0,1:T(8,128)(2,1)S(1)} %copy-done.74), channel_id=1, source_target_pairs={{0,16},{16,32},{32,48},{48,64},{64,80},{80,96},{96,112},{112,128},... | collective-permute-start | bytes 98312 | tf_op jit(solution)/shard_map/ppermute | solution.py:14
  45.7 27.9 %collective-permute-start.23 = (bf16[128,10,1]{2,0,1:T(8,128)(2,1)S(1)}, bf16[128,10,1]{2,0,1:T(8,128)(2,1)S(1)}, u32[]{:S(2)}, u32[]{:S(2)}) collective-permute-start(bf16[128,10,1]{2,0,1:T(8,128)(2,1)S(1)} %get-tuple-element.108), channel_id=1, source_target_pairs={{1,0},{2,1},{3,2},{4,3},{5,4},{6,5},{7,6},{8,7},{9,8},{10,9},{11,1... | collective-permute-start | bytes 7688 | tf_op jit(solution)/shard_map/ppermute | solution.py:17
  48.0 36.1 %copy-start.57 = (bf16[128,1,128]{2,0,1:T(8,128)(2,1)}, bf16[128,1,128]{2,0,1:T(8,128)(2,1)S(1)}, u32[]{:S(2)}) copy-start(bf16[128,1,128]{2,0,1:T(8,128)(2,1)S(1)} %collective-permute-done.17) | copy-start | bytes 98308
  48.0 15.3 %collective-permute-start.15 = (bf16[128,10,1]{2,0,1:T(8,128)(2,1)S(1)}, bf16[128,10,1]{2,0,1:T(8,128)(2,1)S(1)}, u32[]{:S(2)}, u32[]{:S(2)}) collective-permute-start(bf16[128,10,1]{2,0,1:T(8,128)(2,1)S(1)} %get-tuple-element.104), channel_id=1, source_target_pairs={{1,0},{2,1},{3,2},{4,3},{5,4},{6,5},{7,6},{8,7},{9,8},{10,9},{11,1... | collective-permute-start | bytes 7688 | tf_op jit(solution)/shard_map/ppermute | solution.py:17
  49.3 17.0 %collective-permute-start.14 = (bf16[128,10,1]{2,0,1:T(8,128)(2,1)S(1)}, bf16[128,10,1]{2,0,1:T(8,128)(2,1)S(1)}, u32[]{:S(2)}, u32[]{:S(2)}) collective-permute-start(bf16[128,10,1]{2,0,1:T(8,128)(2,1)S(1)} %get-tuple-element.105), channel_id=1, source_target_pairs={{0,1},{1,2},{2,3},{3,4},{4,5},{5,6},{6,7},{7,8},{8,9},{9,10},{10,1... | collective-permute-start | bytes 7688 | tf_op jit(solution)/shard_map/ppermute | solution.py:14
  63.3 14.3 %collective-permute-start.22 = (bf16[128,10,1]{2,0,1:T(8,128)(2,1)S(1)}, bf16[128,10,1]{2,0,1:T(8,128)(2,1)S(1)}, u32[]{:S(2)}, u32[]{:S(2)}) collective-permute-start(bf16[128,10,1]{2,0,1:T(8,128)(2,1)S(1)} %get-tuple-element.109), channel_id=1, source_target_pairs={{0,1},{1,2},{2,3},{3,4},{4,5},{5,6},{6,7},{7,8},{8,9},{9,10},{10,1... | collective-permute-start | bytes 7688 | tf_op jit(solution)/shard_map/ppermute | solution.py:14
  66.3 13.5 %collective-permute-start.19 = (bf16[128,10,1]{2,0,1:T(8,128)(2,1)S(1)}, bf16[128,10,1]{2,0,1:T(8,128)(2,1)S(1)}, u32[]{:S(2)}, u32[]{:S(2)}) collective-permute-start(bf16[128,10,1]{2,0,1:T(8,128)(2,1)S(1)} %get-tuple-element.100), channel_id=1, source_target_pairs={{1,0},{2,1},{3,2},{4,3},{5,4},{6,5},{7,6},{8,7},{9,8},{10,9},{11,1... | collective-permute-start | bytes 7688 | tf_op jit(solution)/shard_map/ppermute | solution.py:17
  73.6 10.6 %collective-permute-start.18 = (bf16[128,10,1]{2,0,1:T(8,128)(2,1)S(1)}, bf16[128,10,1]{2,0,1:T(8,128)(2,1)S(1)}, u32[]{:S(2)}, u32[]{:S(2)}) collective-permute-start(bf16[128,10,1]{2,0,1:T(8,128)(2,1)S(1)} %get-tuple-element.101), channel_id=1, source_target_pairs={{0,1},{1,2},{2,3},{3,4},{4,5},{5,6},{6,7},{7,8},{8,9},{9,10},{10,1... | collective-permute-start | bytes 7688 | tf_op jit(solution)/shard_map/ppermute | solution.py:14
  89.2 15.8 %collective-permute-start.2 = (bf16[256,10,1]{0,1,2:T(8,128)(2,1)S(1)}, bf16[256,10,1]{0,1,2:T(8,128)(2,1)}, u32[]{:S(2)}, u32[]{:S(2)}) collective-permute-start(bf16[256,10,1]{0,1,2:T(8,128)(2,1)S(1)} %copy.85), channel_id=1, source_target_pairs={{1,0},{2,1},{3,2},{4,3},{5,4},{6,5},{7,6},{8,7},{9,8},{10,9},{11,1... | collective-permute-start | bytes 15368 | tf_op jit(solution)/shard_map/ppermute | solution.py:17
  92.6 14.3 %collective-permute-start.3 = (bf16[256,10,1]{0,1,2:T(8,128)(2,1)}, bf16[256,10,1]{0,1,2:T(8,128)(2,1)}, u32[]{:S(2)}, u32[]{:S(2)}) collective-permute-start(bf16[256,10,1]{0,1,2:T(8,128)(2,1)} %copy.89), channel_id=1, source_target_pairs={{0,1},{1,2},{2,3},{3,4},{4,5},{5,6},{6,7},{7,8},{8,9},{9,10},{10,1... | collective-permute-start | bytes 15368 | tf_op jit(solution)/shard_map/ppermute | solution.py:14
  136.3 11.2 %collective-permute-start.5 = (bf16[256,1,128]{2,0,1:T(8,128)(2,1)S(1)}, bf16[256,1,128]{2,0,1:T(8,128)(2,1)S(1)}, u32[]{:S(2)}, u32[]{:S(2)}) collective-permute-start(bf16[256,1,128]{2,0,1:T(8,128)(2,1)S(1)} %get-tuple-element.87), channel_id=1, source_target_pairs={{16,0},{32,16},{48,32},{64,48},{80,64},{96,80},{112,96},{128,112},... | collective-permute-start | bytes 196616 | tf_op jit(solution)/shard_map/ppermute | solution.py:17
  139.7 7.8 %collective-permute-start.4 = (bf16[256,1,128]{2,0,1:T(8,128)(2,1)S(1)}, bf16[256,1,128]{2,0,1:T(8,128)(2,1)S(1)}, u32[]{:S(2)}, u32[]{:S(2)}) collective-permute-start(bf16[256,1,128]{2,0,1:T(8,128)(2,1)S(1)} %get-tuple-element.86), channel_id=1, source_target_pairs={{0,16},{16,32},{32,48},{48,64},{64,80},{80,96},{96,112},{112,128},... | collective-permute-start | bytes 196616 | tf_op jit(solution)/shard_map/ppermute | solution.py:14
  148.8 11.5 %collective-permute-start.6 = (bf16[256,10,1]{0,1,2:T(8,128)(2,1)S(1)}, bf16[256,10,1]{0,1,2:T(8,128)(2,1)S(1)}, u32[]{:S(2)}, u32[]{:S(2)}) collective-permute-start(bf16[256,10,1]{0,1,2:T(8,128)(2,1)S(1)} %copy.103), channel_id=1, source_target_pairs={{1,0},{2,1},{3,2},{4,3},{5,4},{6,5},{7,6},{8,7},{9,8},{10,9},{11,1... | collective-permute-start | bytes 15368 | tf_op jit(solution)/shard_map/ppermute | solution.py:17
  150.4 11.0 %collective-permute-start.7 = (bf16[256,10,1]{0,1,2:T(8,128)(2,1)S(1)}, bf16[256,10,1]{0,1,2:T(8,128)(2,1)S(1)}, u32[]{:S(2)}, u32[]{:S(2)}) collective-permute-start(bf16[256,10,1]{0,1,2:T(8,128)(2,1)S(1)} %copy.107), channel_id=1, source_target_pairs={{0,1},{1,2},{2,3},{3,4},{4,5},{5,6},{6,7},{7,8},{8,9},{9,10},{10,1... | collective-permute-start | bytes 15368 | tf_op jit(solution)/shard_map/ppermute | solution.py:14
  186.1 72.5 %collective-permute-start.9 = (bf16[256,1,128]{2,0,1:T(8,128)(2,1)S(1)}, bf16[256,1,128]{2,0,1:T(8,128)(2,1)S(1)}, u32[]{:S(2)}, u32[]{:S(2)}) collective-permute-start(bf16[256,1,128]{2,0,1:T(8,128)(2,1)S(1)} %get-tuple-element.83), channel_id=1, source_target_pairs={{16,0},{32,16},{48,32},{64,48},{80,64},{96,80},{112,96},{128,112},... | collective-permute-start | bytes 196616 | tf_op jit(solution)/shard_map/ppermute | solution.py:17
  188.0 70.6 %collective-permute-start.8 = (bf16[256,1,128]{2,0,1:T(8,128)(2,1)S(1)}, bf16[256,1,128]{2,0,1:T(8,128)(2,1)S(1)}, u32[]{:S(2)}, u32[]{:S(2)}) collective-permute-start(bf16[256,1,128]{2,0,1:T(8,128)(2,1)S(1)} %get-tuple-element.82), channel_id=1, source_target_pairs={{0,16},{16,32},{32,48},{48,64},{64,80},{80,96},{96,112},{112,128},... | collective-permute-start | bytes 196616 | tf_op jit(solution)/shard_map/ppermute | solution.py:14
  224.0 149.2 %reduce-scatter.9.cloned.1.call-start = ((), (), s32[]{:S(2)}) async-start(), calls=%async_computation.3 | async-start | bytes 626688
  259.6 7.7 %collective-permute-start.10 = (bf16[256,10,1]{0,1,2:T(8,128)(2,1)S(1)}, bf16[256,10,1]{0,1,2:T(8,128)(2,1)S(1)}, u32[]{:S(2)}, u32[]{:S(2)}) collective-permute-start(bf16[256,10,1]{0,1,2:T(8,128)(2,1)S(1)} %copy.122), channel_id=1, source_target_pairs={{1,0},{2,1},{3,2},{4,3},{5,4},{6,5},{7,6},{8,7},{9,8},{10,9},{11,1... | collective-permute-start | bytes 15368 | tf_op jit(solution)/shard_map/ppermute | solution.py:17
  261.3 6.4 %collective-permute-start.11 = (bf16[256,10,1]{0,1,2:T(8,128)(2,1)S(1)}, bf16[256,10,1]{0,1,2:T(8,128)(2,1)S(1)}, u32[]{:S(2)}, u32[]{:S(2)}) collective-permute-start(bf16[256,10,1]{0,1,2:T(8,128)(2,1)S(1)} %copy.126), channel_id=1, source_target_pairs={{0,1},{1,2},{2,3},{3,4},{4,5},{5,6},{6,7},{7,8},{8,9},{9,10},{10,1... | collective-permute-start | bytes 15368 | tf_op jit(solution)/shard_map/ppermute | solution.py:14
  (73 other events, 335.6 us)
Sparse Core Ops, SparseCore 0:
  224.2 68.0 reduce-scatter.6
  295.7 77.4 reduce-scatter.8
where the time goes:
time: 385 us; the launch traced here: 382 us
  waiting for transfers between devices  101 us (26%)
  local copies, waits for them, and re-layouts  79.4 us (21%)
  starting transfers between devices  71 us (18%)
  blocking collectives  57.4 us (15%)
  matrix products  29.7 us (8%)
  other arithmetic  26 us (7%)
  between operations  16.5 us (4%)
    unnamed x4, waiting for transfers between devices  88 us
    unnamed x2, blocking collectives  57.4 us
    ppermute x12, starting transfers between devices, with_halo(): lax.ppermute(lax.slice_in_dim(block, block.shape[dim] - width, None, axis...  45.5 us
    slice x30, local copies, waits for them, and re-layouts, transposed(): padded_grads[:, 2 - upper:2 - upper + rows, 2 - left:2 - left + cols]  33.8 us
    ppermute x12, starting transfers between devices, with_halo(): lax.ppermute(lax.slice_in_dim(block, 0, width, axis=dim), axis, backward)  25.4 us
    unnamed x176, local copies, waits for them, and re-layouts  20.4 us
    concatenate x15, other arithmetic, with_halo(): block = jnp.concatenate([low, block, high], axis=dim)  19.4 us
    dot_general x27, matrix products, transposed(): lax.dot_general(piece, window, (((0,), (0,)), ((), ())), preferred_elemen...  18.9 us
  transfers between devices with their start and end apart: 26, of which 4 were waited for; matrix products, arithmetic and copies ran while one was open for 17% of the time, Pallas kernels for 0%

commit v1 on v0

v1 whole, which is shorter than its diff:
```python
import functools
import math

import jax
import jax.numpy as jnp
from jax import lax
from jax.experimental import pallas as pl
from jax.experimental.pallas import tpu as pltpu
from jax.sharding import PartitionSpec as P

INTERPRET = False
F32 = jnp.float32
BF16 = jnp.bfloat16
ROWS = 8
LANES = 128
SLABS = ROWS + 2
CH = 64
Q = 4 * CH
W = 2 * CH


def call(body, out_shape, in_specs=None, out_specs=None, scratch=(), aliases=None):
    kwargs = {}
    if in_specs is not None:
        kwargs["in_specs"] = in_specs
    if out_specs is not None:
        kwargs["out_specs"] = out_specs
    return pl.pallas_call(
        body,
        out_shape=out_shape,
        scratch_shapes=list(scratch),
        input_output_aliases=aliases or {},
        interpret=INTERPRET,
        grid=(1,),
        **kwargs,
    )


def whole():
    return pl.BlockSpec(memory_space=pltpu.VMEM)


def at_step(step, shape):
    return pl.BlockSpec((1,) + shape, lambda i: (step,) + (0,) * len(shape))


def sigmoid(x):
    return 0.5 * jnp.tanh(0.5 * x) + 0.5


def lane_ids(rows):
    return lax.broadcasted_iota(jnp.int32, (rows, LANES), 1)


def parity(axis):
    return lax.rem(lax.axis_index(axis), 2)


def edge_flags(axis):
    index = lax.axis_index(axis)
    low = jnp.where(index > 0, 1.0, 0.0).astype(F32)
    high = jnp.where(index < lax.axis_size(axis) - 1, 1.0, 0.0).astype(F32)
    return low, high


def gate_grads(pre, part, cot, dh, mask, cell_before, tanh_cell, dc):
    gin, gfor, gout, gcand = pre
    error = mask * (cot if dh is None else dh + cot)
    eo = error * gout
    grad = eo * (1.0 - tanh_cell * tanh_cell)
    if dc is not None:
        grad = dc + grad
    gi = grad * gin
    part[0] = gi * gcand * (1.0 - gin)
    df = grad * gfor
    part[1] = df * cell_before * (1.0 - gfor)
    part[2] = eo * tanh_cell * (1.0 - gout)
    part[3] = gi * (1.0 - gcand * gcand)
    return df


def emit_grads(scr, a_ref, p0_ref, p1_ref, ql_ref, qr_ref):
    par = parity("row")
    step = 32
    lanes = lane_ids(step)
    for k in range(Q // step):
        own = pl.ds(k * step, step)
        ql = jnp.zeros((step, LANES), F32)
        qr = jnp.zeros((step, LANES), F32)
        for r in range(ROWS):
            row = scr[pl.ds(k * step * ROWS + r, step, stride=ROWS), :]
            a_ref[own, r * LANES : (r + 1) * LANES] = row.astype(BF16)
            ql = jnp.where(lanes == r + 1, pltpu.roll(row, r + 1, 1), ql)
            qr = jnp.where(lanes == r + 1, pltpu.roll(row, r + 2, 1), qr)
        ql_ref[own, :] = ql.astype(BF16)
        qr_ref[own, :] = qr.astype(BF16)
    top = a_ref[:, 0:LANES]
    bottom = a_ref[:, (ROWS - 1) * LANES :]

    @pl.when(par == 0)
    def _():
        p0_ref[...] = bottom
        p1_ref[...] = top

    @pl.when(par == 1)
    def _():
        p0_ref[...] = top
        p1_ref[...] = bottom


def forward_kernel(pre_ref, cot_ref, h_ref_unused, c0_ref, mask_ref, c1_ref, c2_ref, h1_ref, h2_ref, dc_ref, a_ref, p0_ref, p1_ref, ql_ref, qr_ref, scr):
    del h_ref_unused
    step = 4
    mask = mask_ref[...].astype(F32)[None]

    def chunk(j, carry):
        base = j * step

        def gate(t, g):
            return pre_ref[t, pl.ds(g * CH + base, step)].astype(F32)

        own = pl.ds(base, step)
        cell = c0_ref[own]
        for t, (c_ref, h_ref) in enumerate(((c1_ref, h1_ref), (c2_ref, h2_ref))):
            cell = sigmoid(gate(t, 1)) * cell + sigmoid(gate(t, 0)) * jnp.tanh(gate(t, 3))
            c_ref[own] = cell
            h_ref[own] = (mask * sigmoid(gate(t, 2)) * jnp.tanh(cell)).astype(BF16)
        pre = (sigmoid(gate(2, 0)), sigmoid(gate(2, 1)), sigmoid(gate(2, 2)), jnp.tanh(gate(2, 3)))
        tanh_cell = jnp.tanh(pre[1] * cell + pre[0] * pre[3])
        part = [None] * 4
        dc_ref[own] = gate_grads(pre, part, cot_ref[0, own].astype(F32), None, mask, cell, tanh_cell, None)
        for g in range(4):
            scr[pl.ds((g * CH + base) * ROWS, step * ROWS), :] = part[g].reshape(step * ROWS, LANES)
        return carry

    lax.fori_loop(0, CH // step, chunk, 0)
    emit_grads(scr, a_ref, p0_ref, p1_ref, ql_ref, qr_ref)


def halo_rows(r0_ref, r1_ref, own):
    par = parity("row").astype(F32)
    low, high = edge_flags("row")
    first, second = r0_ref[own, :].astype(F32), r1_ref[own, :].astype(F32)
    above = second * ((1.0 - par) * low) + first * (par * low)
    below = first * ((1.0 - par) * high) + second * (par * high)
    return above, below


def corner_kernel(r0_ref, r1_ref, ql_ref, qr_ref, c0_ref, c1_ref):
    par = parity("col").astype(F32)
    step = 32
    lanes = lane_ids(step)
    for k in range(Q // step):
        own = pl.ds(k * step, step)
        above, below = halo_rows(r0_ref, r1_ref, own)
        left = jnp.where(lanes == 0, above, ql_ref[own, :].astype(F32))
        left = jnp.where(lanes == SLABS - 1, pltpu.roll(below, SLABS - 1, 1), left)
        right = jnp.where(lanes == 0, pltpu.roll(above, 1, 1), qr_ref[own, :].astype(F32))
        right = jnp.where(lanes == SLABS - 1, pltpu.roll(below, SLABS, 1), right)
        c0_ref[own, :] = (right * (1.0 - par) + left * par).astype(BF16)
        c1_ref[own, :] = (left * (1.0 - par) + right * par).astype(BF16)


def build_windows(a_ref, r0_ref, r1_ref, c0_ref, c1_ref, b_ref):
    par = parity("col").astype(F32)
    low, high = edge_flags("col")
    step = 32
    lanes = lane_ids(step)
    for k in range(Q // step):
        own = pl.ds(k * step, step)
        above, below = halo_rows(r0_ref, r1_ref, own)
        first, second = c0_ref[own, :].astype(F32), c1_ref[own, :].astype(F32)
        left = second * ((1.0 - par) * low) + first * (par * low)
        right = first * ((1.0 - par) * high) + second * (par * high)
        for s in range(SLABS):
            if s == 0:
                row = above
            elif s == SLABS - 1:
                row = below
            else:
                row = a_ref[own, (s - 1) * LANES : s * LANES].astype(F32)
            span = slice(s * LANES, (s + 1) * LANES)
            minus = jnp.where(lanes == LANES - 1, pltpu.roll(right, LANES - 1 - s, 1), pltpu.roll(row, LANES - 1, 1))
            plus = jnp.where(lanes == 0, pltpu.roll(left, (LANES - s) % LANES, 1), pltpu.roll(row, 1, 1))
            b_ref[pl.ds(k * step, step), span] = minus.astype(BF16)
            b_ref[pl.ds(Q + k * step, step), span] = row.astype(BF16)
            b_ref[pl.ds(2 * Q + k * step, step), span] = plus.astype(BF16)


def convolve(w_ref, b_ref, y3, scr):
    y3[...] = lax.dot_general(w_ref[...], b_ref[...], (((1,), (0,)), ((), ())), preferred_element_type=F32)
    for r in range(ROWS):
        total = y3[0:W, (r + 2) * LANES : (r + 3) * LANES]
        total = total + y3[W : 2 * W, (r + 1) * LANES : (r + 2) * LANES]
        total = total + y3[2 * W : 3 * W, r * LANES : (r + 1) * LANES]
        scr[pl.ds(r, W, stride=ROWS), :] = total


def backward_kernel(has_gi, *refs):
    if has_gi:
        refs = refs[1:]
    (a_in, r0_ref, r1_ref, k0_ref, k1_ref, w_ref, pre_ref, cot_ref, before_ref, cell_ref, mask_ref, dc_in,
     gi_ref, b_ref, dc_ref, a_ref, p0_ref, p1_ref, ql_ref, qr_ref, y3, yscr, scr) = refs
    build_windows(a_in, r0_ref, r1_ref, k0_ref, k1_ref, b_ref)
    convolve(w_ref, b_ref, y3, yscr)
    step = 4
    mask = mask_ref[...].astype(F32)[None]

    def chunk(j, carry):
        base = j * step
        own = pl.ds(base, step)

        def gate(g):
            return pre_ref[0, pl.ds(g * CH + base, step)].astype(F32)

        gi_ref[0, own] = yscr[pl.ds(base * ROWS, step * ROWS), :].reshape(step, ROWS, LANES).astype(BF16)
        dh = yscr[pl.ds((CH + base) * ROWS, step * ROWS), :].reshape(step, ROWS, LANES)
        pre = (sigmoid(gate(0)), sigmoid(gate(1)), sigmoid(gate(2)), jnp.tanh(gate(3)))
        part = [None] * 4
        dc_ref[own] = gate_grads(pre, part, cot_ref[0, own].astype(F32), dh, mask, before_ref[own], jnp.tanh(cell_ref[own]), dc_in[own])
        for g in range(4):
            scr[pl.ds((g * CH + base) * ROWS, step * ROWS), :] = part[g].reshape(step * ROWS, LANES)
        return carry

    lax.fori_loop(0, CH // step, chunk, 0)
    emit_grads(scr, a_ref, p0_ref, p1_ref, ql_ref, qr_ref)


def last_kernel(gi_in, a_in, r0_ref, r1_ref, k0_ref, k1_ref, w_ref, gi_ref, b_ref, dh_ref, y3, yscr):
    del gi_in
    build_windows(a_in, r0_ref, r1_ref, k0_ref, k1_ref, b_ref)
    convolve(w_ref, b_ref, y3, yscr)
    gi_ref[0] = yscr[0 : CH * ROWS, :].reshape(CH, ROWS, LANES).astype(BF16)
    dh_ref[...] = yscr[CH * ROWS :, :].reshape(CH, ROWS, LANES)


ZROWS = 3 * W + 16


def kernel_grads(x_ref, h_ref, b_ref, z3, tmp):
    tmp[0 : CH * ROWS, :] = x_ref[0].astype(F32).reshape(CH * ROWS, LANES)
    tmp[CH * ROWS :, :] = h_ref[...].astype(F32).reshape(CH * ROWS, LANES)
    zero = jnp.zeros((W, LANES), BF16)
    for u in range(3):
        for s in range(SLABS):
            if not 0 <= s - 2 + u < ROWS:
                z3[u * W : (u + 1) * W, s * LANES : (s + 1) * LANES] = zero
    for r in range(ROWS):
        row = tmp[pl.ds(r, W, stride=ROWS), :].astype(BF16)
        for u in range(3):
            s = r + 2 - u
            z3[u * W : (u + 1) * W, s * LANES : (s + 1) * LANES] = row
    row_id = lax.broadcasted_iota(jnp.int32, (16, SLABS * LANES), 0)
    lane_id = lax.broadcasted_iota(jnp.int32, (16, SLABS * LANES), 1)
    inside = (row_id == 0) & (lane_id >= LANES) & (lane_id < (SLABS - 1) * LANES)
    z3[3 * W :, :] = jnp.where(inside, 1.0, 0.0).astype(BF16)
    dims = (((1,), (1,)), ((), ()))
    for v in range(3):
        span = 3 * W + 16 if v == 1 else 3 * W
        got = lax.dot_general(z3[0:span, :], b_ref[v * Q : (v + 1) * Q, :], dims, preferred_element_type=F32)
        for u in range(3):
            yield u * 3 + v, got[u * W : (u + 1) * W]
        if v == 1:
            yield 9, got[3 * W :]


def accumulate_kernel(has_acc, *refs):
    if has_acc:
        acc_ref, x_ref, h_ref, b_ref, out_ref, z3, tmp = refs
    else:
        x_ref, h_ref, b_ref, out_ref, z3, tmp = refs
    for tap, got in kernel_grads(x_ref, h_ref, b_ref, z3, tmp):
        rows = slice(tap * W, tap * W + got.shape[0])
        out_ref[rows, :] = acc_ref[rows, :] + got if has_acc else got


def send_kernel(blocks, scale, acc_ref, x_ref, h_ref, b_ref, out_ref, z3, tmp, total):
    for tap, got in kernel_grads(x_ref, h_ref, b_ref, z3, tmp):
        rows = slice(tap * W, tap * W + got.shape[0])
        total[rows, :] = (acc_ref[rows, :] + got) * scale
    bias = total[9 * W : 9 * W + 8, :]
    high = jnp.broadcast_to(bias[0:1], (8, Q)).astype(BF16).astype(F32)
    low = jnp.broadcast_to(bias[0:1], (8, Q)) - high
    ids = lax.broadcasted_iota(jnp.int32, (8, Q), 0)
    tail = jnp.where(ids == 0, high, jnp.where(ids == 1, low, 0.0))
    size = 9 * W // blocks
    for c in range(blocks):
        body = jnp.concatenate([total[c * size : (c + 1) * size, :], tail], axis=0)
        out_ref[c * (size + 8) : (c + 1) * (size + 8), :] = body.astype(BF16)


def fold_kernel(blocks, in_ref, out_ref):
    size = in_ref.shape[0] // blocks
    total = in_ref[0:size, :].astype(F32)
    for c in range(1, blocks):
        total = total + in_ref[c * size : (c + 1) * size, :].astype(F32)
    out_ref[...] = total.T


def even_swap(count):
    return [(i, i ^ 1) for i in range(count)]


def odd_swap(count):
    return [(i, (i + 1) % count if i % 2 else (i - 1) % count) for i in range(count)]


def swaps(first, second, axis):
    count = lax.axis_size(axis)
    return lax.ppermute(first, axis, even_swap(count)), lax.ppermute(second, axis, odd_swap(count))


def struct(shape, dtype):
    return jax.ShapeDtypeStruct(shape, dtype)


def shards(inputs, gate_pre, cotangent, hidden_init, cell_init, land_mask, kernel):
    field = (CH, ROWS, LANES)
    nrow, ncol = lax.axis_size("row"), lax.axis_size("col")
    scale = 1.0 / math.sqrt(ROWS * LANES * nrow * ncol)
    weights = kernel.reshape(Q, 3, 3, W).transpose(1, 3, 2, 0).reshape(3 * W, 3 * Q)
    edge = struct((Q, LANES), BF16)
    grads_out = (struct((Q, ROWS * LANES), BF16), edge, edge, edge, edge)
    scr = pltpu.VMEM((Q * ROWS, LANES), F32)
    y3, yscr = pltpu.VMEM((3 * W, SLABS * LANES), F32), pltpu.VMEM((W * ROWS, LANES), F32)
    z3, tmp = pltpu.VMEM((ZROWS, SLABS * LANES), BF16), pltpu.VMEM((W * ROWS, LANES), F32)

    c1, c2, h1, h2, dc, a, p0, p1, ql, qr = call(
        forward_kernel,
        (struct(field, F32), struct(field, F32), struct(field, BF16), struct(field, BF16), struct(field, F32)) + grads_out,
        in_specs=[whole(), at_step(2, field), whole(), whole(), whole()],
        out_specs=[whole()] * 10,
        scratch=[scr],
    )(gate_pre, cotangent, hidden_init, cell_init, land_mask)

    cells = [cell_init, c1, c2]
    hiddens = [hidden_init, h1, h2]
    gi_shape = struct((3,) + field, BF16)
    windows = struct((3 * Q, SLABS * LANES), BF16)
    acc_shape = struct((9 * W + 16, Q), F32)
    gi = acc = None
    for t in (2, 1, 0):
        r0, r1 = swaps(p0, p1, "row")
        k0, k1 = call(corner_kernel, (edge, edge), in_specs=[whole()] * 4, out_specs=[whole()] * 2)(r0, r1, ql, qr)
        k0, k1 = swaps(k0, k1, "col")
        if t > 0:
            head = [] if gi is None else [gi]
            gi, b, dc, a_next, p0, p1, ql, qr = call(
                functools.partial(backward_kernel, gi is not None),
                (gi_shape, windows, struct(field, F32)) + grads_out,
                in_specs=[pl.BlockSpec(memory_space=pl.ANY)] * len(head)
                + [whole()] * 6
                + [at_step(t - 1, (Q, ROWS, LANES)), at_step(t - 1, field)]
                + [whole()] * 4,
                out_specs=[at_step(t, field)] + [whole()] * 7,
                scratch=[y3, yscr, scr],
                aliases={0: 0} if head else {},
            )(*head, a, r0, r1, k0, k1, weights, gate_pre, cotangent, cells[t - 1], cells[t], land_mask, dc)
            a = a_next
            head = [] if acc is None else [acc]
            acc = call(
                functools.partial(accumulate_kernel, acc is not None),
                acc_shape,
                in_specs=[whole()] * len(head) + [at_step(t, field), whole(), whole()],
                out_specs=whole(),
                scratch=[z3, tmp],
                aliases={0: 0} if head else {},
            )(*head, inputs, hiddens[t], b)
        else:
            gi, b, grad_hidden = call(
                last_kernel,
                (gi_shape, windows, struct(field, F32)),
                in_specs=[pl.BlockSpec(memory_space=pl.ANY)] + [whole()] * 6,
                out_specs=[at_step(0, field), whole(), whole()],
                scratch=[y3, yscr],
                aliases={0: 0},
            )(gi, a, r0, r1, k0, k1, weights)
            size = 9 * W // ncol + 8
            send = call(
                functools.partial(send_kernel, ncol, scale),
                struct((ncol * size, Q), BF16),
                in_specs=[whole(), at_step(0, field), whole(), whole()],
                out_specs=whole(),
                scratch=[z3, tmp, pltpu.VMEM((9 * W + 16, Q), F32)],
            )(acc, inputs, hiddens[0], b)
    got = lax.all_to_all(send, "col", 0, 0, tiled=True)
    folded = call(functools.partial(fold_kernel, ncol), struct((Q, size), F32), in_specs=[whole()], out_specs=whole())(got)
    got = lax.all_to_all(folded, "row", 0, 0, tiled=True)
    total = got.reshape(nrow, Q // nrow, size).sum(0)
    bias = total[:, size - 8] + total[:, size - 7]
    count = Q // nrow // ncol
    grad_bias = lax.dynamic_slice_in_dim(bias, lax.axis_index("col") * count, count)
    return (gi, grad_hidden, dc, total[:, : size - 8], grad_bias)


def solution(mesh):
    placed = (
        P(None, None, "row", "col"),
        P(None, None, "row", "col"),
        P(None, None, "row", "col"),
        P(None, "row", "col"),
        P(None, "row", "col"),
        P("row", "col"),
        P(),
    )
    return jax.shard_map(
        shards,
        mesh=mesh,
        in_specs=placed,
        out_specs=(
            P(None, None, "row", "col"),
            P(None, "row", "col"),
            P(None, "row", "col"),
            P("row", "col"),
            P(("row", "col")),
        ),
        check_vma=False,
    )
```

time: 385 us -> 117 us (0.30)
  waiting for transfers between devices: 101 us -> 25 us
  local copies, waits for them, and re-layouts: 79.4 us -> 6.05 us
  blocking collectives: 57.4 us -> 15.3 us
  starting transfers between devices: 71 us -> 30.8 us
  Pallas kernels: 0 us -> 37.8 us
  matrix products: 29.7 us -> 0 us
  other arithmetic: 26 us -> 1.19 us
  between operations: 16.5 us -> 0.7 us
    unnamed x4 -> x0, waiting for transfers between devices: 88 us -> none
    unnamed x2 -> x0, blocking collectives: 57.4 us -> none
    ppermute x24 -> x12, starting transfers between devices: 70.9 us -> 22.7 us  [the longest x6 11.9 us: swaps(): lax.ppermute(second, axis, odd_swap(count))]
    slice x48 -> x1, local copies, waits for them, and re-layouts: 44.2 us -> 0.07 us  [shards(): bias = total[:, size - 8] + total[:, size - 7]]
    pallas_call x0 -> x11, Pallas kernels: none -> 37.8 us  [the longest x2 10.9 us: shards(): call(functools.partial(backward_kernel, gi is not None), (gi_shape, windo...]
    dot_general x54 -> x0, matrix products: 29.7 us -> none  [the longest x27 18.9 us: transposed(): lax.dot_general(piece, window, (((0,), (0,)), ((), ())), preferred_elemen...]
    concatenate x15 -> x0, other arithmetic: 19.4 us -> none  [with_halo(): block = jnp.concatenate([low, block, high], axis=dim)]
    unnamed x176 -> x30, local copies, waits for them, and re-layouts: 20.4 us -> 4.95 us
  transfers between devices with their start and end apart: 26 -> 13, of which waited for: 4 -> 9; matrix products, arithmetic and copies ran while one was open for 17% -> 1% of each run, Pallas kernels for 0% -> 7%
where the time goes in v1:
time: 117 us
  Pallas kernels  37.8 us (32%)
  starting transfers between devices  30.8 us (26%)
  waiting for transfers between devices  25 us (21%)
  blocking collectives  15.3 us (13%)
  local copies, waits for them, and re-layouts  6.05 us (5%)
  other arithmetic  1.19 us (1%)
    all_to_all x1, blocking collectives, shards(): got = lax.all_to_all(send, 'col', 0, 0, tiled=True)  15.3 us
    ppermute x6, waiting for transfers between devices, swaps(): lax.ppermute(second, axis, odd_swap(count))  12.8 us
    ppermute x6, starting transfers between devices, swaps(): lax.ppermute(second, axis, odd_swap(count))  11.9 us
    pallas_call x2, Pallas kernels, shards(): call(functools.partial(backward_kernel, gi is not None), (gi_shape, windo...  10.9 us
    ppermute x6, starting transfers between devices, swaps(): lax.ppermute(first, axis, even_swap(count))  10.8 us
    all_to_all x1, waiting for transfers between devices, shards(): got = lax.all_to_all(folded, 'row', 0, 0, tiled=True)  8.89 us
    all_to_all x1, starting transfers between devices, shards(): got = lax.all_to_all(folded, 'row', 0, 0, tiled=True)  8.16 us
    pallas_call x2, Pallas kernels, shards(): call(functools.partial(accumulate_kernel, acc is not None), acc_shape, in...  7.86 us
  transfers between devices with their start and end apart: 13, of which 9 were waited for; matrix products, arithmetic and copies ran while one was open for 1% of the time, Pallas kernels for 7%

profile of v1, /device:TPU:1, one launch (start us, length us, event | category | flops | bytes accessed | tf_op | source)
XLA Modules:
  0.0 116.8 jit_solution(10893459027230361004)
XLA Ops:
  0.6 4.2 %shard_map.110 = (f32[64,8,128]{2,1,0:T(8,128)}, f32[64,8,128]{2,1,0:T(8,128)}, bf16[64,8,128]{2,1,0:T(8,128)(2,1)}, bf16[64,8,128]{2,1,0:T(8,128)(2,1)}, f32[64...) custom-call(bf16[3,256,8,128]{3,2,1,0:T(8,128)(2,1)} %refs_7_.3, ...), custom_call_target="tpu_custom_call" | custom-call | tf_op jit(solution)/shard_map/pallas_call | solution.py:328
  4.8 3.2 %collective-permute-start = (bf16[256,128]{1,0:T(8,128)(2,1)}, bf16[256,128]{1,0:T(8,128)(2,1)S(1)}, u32[]{:S(2)}, u32[]{:S(2)}) collective-permute-start(bf16[256,128]{1,0:T(8,128)(2,1)} %get-tuple-element.41), channel_id=1, source_target_pairs={{0,16},{16,0},{32,48},{48,32},{64,80},{80,64},{96,112},{112,96},{1... | collective-permute-start | bytes 196616 | tf_op jit(solution)/shard_map/ppermute | solution.py:310
  8.0 1.1 collective-permute-done.r0_ref.refs_1_
  9.1 2.8 %collective-permute-done.1.r1_ref.refs_2_ = bf16[256,128]{1,0:T(8,128)(2,1)S(1)} collective-permute-done((bf16[256,128]{1,0:T(8,128)(2,1)}, bf16[256,128]{1,0:T(8,128)(2,1)S(1)}, u32[]{:S(2)}, u32[]{:S(2)}) %collective-permute-start.1) | collective-permute-done | bytes 65568 | tf_op jit(solution)/shard_map/ppermute | solution.py:310
  11.9 0.6 copy-done.2
  12.6 1.8 %shard_map.111 = (bf16[256,128]{1,0:T(8,128)(2,1)}, bf16[256,128]{1,0:T(8,128)(2,1)}) custom-call(bf16[256,128]{1,0:T(8,128)(2,1)} %copy-done.1, bf16[256,128]{1,0:T(8,128)(2,1)} %copy-done.2, bf16[256,128]{1,0:T(8,128)(2,1)} %get-tuple-element.43.ql_ref, bf16[256,128]{1,0:T(8,128)(2,1)} %get-tuple-element.44.qr_ref), custom_call_target="tpu_custom_call" | custom-call | tf_op jit(solution)/shard_map/pallas_call | solution.py:344
  14.3 3.7 %collective-permute-start.3 = (bf16[256,128]{1,0:T(8,128)(2,1)}, bf16[256,128]{1,0:T(8,128)(2,1)S(1)}, u32[]{:S(2)}, u32[]{:S(2)}) collective-permute-start(bf16[256,128]{1,0:T(8,128)(2,1)} %get-tuple-element.46), channel_id=1, source_target_pairs={{0,15},{1,2},{2,1},{3,4},{4,3},{5,6},{6,5},{7,8},{8,7},{9,10},{10,... | collective-permute-start | bytes 196616 | tf_op jit(solution)/shard_map/ppermute | solution.py:310
  18.8 0.9 copy.18
  19.7 1.3 %collective-permute-done.3.refs_4_ = bf16[256,128]{1,0:T(8,128)(2,1)S(1)} collective-permute-done((bf16[256,128]{1,0:T(8,128)(2,1)}, bf16[256,128]{1,0:T(8,128)(2,1)S(1)}, u32[]{:S(2)}, u32[]{:S(2)}) %collective-permute-start.3) | collective-permute-done | bytes 65568 | tf_op jit(solution)/shard_map/ppermute | solution.py:310
  21.6 5.5 %shard_map.112 = (bf16[3,64,8,128]{3,2,1,0:T(8,128)(2,1)}, bf16[768,1280]{1,0:T(8,128)(2,1)}, f32[64,8,128]{2,1,0:T(8,128)}, bf16[256,1024]{1,0:T(8,128)(2,1)}, ...) custom-call(bf16[256,1024]{1,0:T(8,128)(2,1)} %get-tuple-element.40.re, ...), custom_call_target="tpu_custom_call" | custom-call | tf_op jit(solution)/shard_map/pallas_call | solution.py:348
  27.1 5.3 %collective-permute-start.4 = (bf16[256,128]{1,0:T(8,128)(2,1)}, bf16[256,128]{1,0:T(8,128)(2,1)S(1)}, u32[]{:S(2)}, u32[]{:S(2)}) collective-permute-start(bf16[256,128]{1,0:T(8,128)(2,1)} %get-tuple-element.52), channel_id=1, source_target_pairs={{0,16},{16,0},{32,48},{48,32},{64,80},{80,64},{96,112},{112,96},{1... | collective-permute-start | bytes 196616 | tf_op jit(solution)/shard_map/ppermute | solution.py:310
  32.4 1.1 collective-permute-done.4.r0_ref.refs_2_
  33.5 3.1 %collective-permute-done.5.r1_ref.refs_3_ = bf16[256,128]{1,0:T(8,128)(2,1)S(1)} collective-permute-done((bf16[256,128]{1,0:T(8,128)(2,1)}, bf16[256,128]{1,0:T(8,128)(2,1)S(1)}, u32[]{:S(2)}, u32[]{:S(2)}) %collective-permute-start.5) | collective-permute-done | bytes 65568 | tf_op jit(solution)/shard_map/ppermute | solution.py:310
  37.2 1.8 %shard_map.113 = (bf16[256,128]{1,0:T(8,128)(2,1)}, bf16[256,128]{1,0:T(8,128)(2,1)}) custom-call(bf16[256,128]{1,0:T(8,128)(2,1)} %copy-done.3, bf16[256,128]{1,0:T(8,128)(2,1)} %copy-done.4, bf16[256,128]{1,0:T(8,128)(2,1)} %get-tuple-element.54.ql_ref, bf16[256,128]{1,0:T(8,128)(2,1)} %get-tuple-element.55.qr_ref), custom_call_target="tpu_custom_call" | custom-call | tf_op jit(solution)/shard_map/pallas_call | solution.py:344
  39.0 4.1 %collective-permute-start.7 = (bf16[256,128]{1,0:T(8,128)(2,1)}, bf16[256,128]{1,0:T(8,128)(2,1)S(1)}, u32[]{:S(2)}, u32[]{:S(2)}) collective-permute-start(bf16[256,128]{1,0:T(8,128)(2,1)} %get-tuple-element.57), channel_id=1, source_target_pairs={{0,15},{1,2},{2,1},{3,4},{4,3},{5,6},{6,5},{7,8},{8,7},{9,10},{10,... | collective-permute-start | bytes 196616 | tf_op jit(solution)/shard_map/ppermute | solution.py:310
  43.1 2.5 %collective-permute-done.7.refs_5_ = bf16[256,128]{1,0:T(8,128)(2,1)S(1)} collective-permute-done((bf16[256,128]{1,0:T(8,128)(2,1)}, bf16[256,128]{1,0:T(8,128)(2,1)S(1)}, u32[]{:S(2)}, u32[]{:S(2)}) %collective-permute-start.7) | collective-permute-done | bytes 65568 | tf_op jit(solution)/shard_map/ppermute | solution.py:310
  46.3 5.5 %shard_map.114 = (bf16[3,64,8,128]{3,2,1,0:T(8,128)(2,1)}, bf16[768,1280]{1,0:T(8,128)(2,1)}, f32[64,8,128]{2,1,0:T(8,128)}, bf16[256,1024]{1,0:T(8,128)(2,1)}, ...) custom-call(bf16[3,64,8,128]{3,2,1,0:T(8,128)(2,1)} %get-tuple-eleme, ...), custom_call_target="tpu_custom_call", output_to_operand_aliasing={{0}: (0, {})} | custom-call | tf_op jit(solution)/shard_map/pallas_call | solution.py:348
  51.7 2.2 %collective-permute-start.8 = (bf16[256,128]{1,0:T(8,128)(2,1)}, bf16[256,128]{1,0:T(8,128)(2,1)S(1)}, u32[]{:S(2)}, u32[]{:S(2)}) collective-permute-start(bf16[256,128]{1,0:T(8,128)(2,1)} %get-tuple-element.61), channel_id=1, source_target_pairs={{0,16},{16,0},{32,48},{48,32},{64,80},{80,64},{96,112},{112,96},{1... | collective-permute-start | bytes 196616 | tf_op jit(solution)/shard_map/ppermute | solution.py:310
  53.9 1.1 collective-permute-done.8.r0_ref
  55.1 3.1 %collective-permute-done.9.r1_ref = bf16[256,128]{1,0:T(8,128)(2,1)S(1)} collective-permute-done((bf16[256,128]{1,0:T(8,128)(2,1)}, bf16[256,128]{1,0:T(8,128)(2,1)S(1)}, u32[]{:S(2)}, u32[]{:S(2)}) %collective-permute-start.9) | collective-permute-done | bytes 65568 | tf_op jit(solution)/shard_map/ppermute | solution.py:310
  58.1 0.6 copy-done.6
  58.8 1.8 %shard_map.115 = (bf16[256,128]{1,0:T(8,128)(2,1)}, bf16[256,128]{1,0:T(8,128)(2,1)}) custom-call(bf16[256,128]{1,0:T(8,128)(2,1)} %copy-done.5, bf16[256,128]{1,0:T(8,128)(2,1)} %copy-done.6, bf16[256,128]{1,0:T(8,128)(2,1)} %get-tuple-element.63.ql_ref, bf16[256,128]{1,0:T(8,128)(2,1)} %get-tuple-element.64.qr_ref), custom_call_target="tpu_custom_call" | custom-call | tf_op jit(solution)/shard_map/pallas_call | solution.py:344
  60.5 4.1 %collective-permute-start.11 = (bf16[256,128]{1,0:T(8,128)(2,1)}, bf16[256,128]{1,0:T(8,128)(2,1)S(1)}, u32[]{:S(2)}, u32[]{:S(2)}) collective-permute-start(bf16[256,128]{1,0:T(8,128)(2,1)} %get-tuple-element.66), channel_id=1, source_target_pairs={{0,15},{1,2},{2,1},{3,4},{4,3},{5,6},{6,5},{7,8},{8,7},{9,10},{10,... | collective-permute-start | bytes 196616 | tf_op jit(solution)/shard_map/ppermute | solution.py:310
  64.6 3.8 %shard_map.117.refs_0_ = f32[1168,256]{1,0:T(8,128)} custom-call(bf16[3,64,8,128]{3,2,1,0:T(8,128)(2,1)} %x_ref.1, bf16[64,8,128]{2,1,0:T(8,128)(2,1)} %get-tuple-element.70.refs_1_, bf16[768,1280]{1,0:T(8,128)(2,1)} %get-tuple-element.71.refs_2_), custom_call_target="tpu_custom_call" | custom-call | tf_op jit(solution)/shard_map/pallas_call | solution.py:361
  68.4 4.1 %shard_map.118.acc_ref = f32[1168,256]{1,0:T(8,128)} custom-call(f32[1168,256]{1,0:T(8,128)} %shard_map.117.refs_0_, bf16[3,64,8,128]{3,2,1,0:T(8,128)(2,1)} %x_ref.1, bf16[64,8,128]{2,1,0:T(8,128)(2,1)} %get-tuple-element.72.refs_2_, bf16[768,1280]{1,0:T(8,128)(2,1)} %get-tuple-element.73.refs_3_), custom_call_target="tpu_custom_call", output_to_operand_aliasing={{}: (0, {})} | custom-call | tf_op jit(solution)/shard_map/pallas_call | solution.py:361
  73.2 3.7 %shard_map.116 = (bf16[3,64,8,128]{3,2,1,0:T(8,128)(2,1)}, bf16[768,1280]{1,0:T(8,128)(2,1)}, f32[64,8,128]{2,1,0:T(8,128)}) custom-call(bf16[3,64,8,128]{3,2,1,0:T(8,128)(2,1)} %get-tuple-element.59.gi_in, bf16[256,1024]{1,0:T(8,128)(2,1)} %get-tuple-element.60.a_in, bf16[256,128]{1,0:T(8,128)(2,1)} %copy-done.5, ...), custom_call_target="tpu_custom_call", output_to_operand_aliasing={{0}: (0, {})} | custom-call | tf_op jit(solution)/shard_map/pallas_call | solution.py:370
  76.9 3.9 %shard_map.119 = bf16[1280,256]{1,0:T(8,128)(2,1)} custom-call(f32[1168,256]{1,0:T(8,128)} %shard_map.118.acc_ref, bf16[3,64,8,128]{3,2,1,0:T(8,128)(2,1)} %x_ref.1, bf16[64,8,128]{2,1,0:T(8,128)(2,1)} %h_ref.1, bf16[768,1280]{1,0:T(8,128)(2,1)} %get-tuple-element.74.b_ref), custom_call_target="tpu_custom_call" | custom-call | tf_op jit(solution)/shard_map/pallas_call | solution.py:379
  80.8 15.3 %all_to_all.20 = bf16[16,80,256]{2,1,0:T(8,128)(2,1)} all-to-all(bf16[16,80,256]{2,1,0:T(8,128)(2,1)} %bitcast.16), channel_id=1, replica_groups=mesh['row'=16,'col'=16] {'col'}, dimensions={0} | all-to-all | bytes 1310720 | tf_op jit(solution)/shard_map/all_to_all | solution.py:386
  96.1 1.9 %shard_map.120 = f32[256,80]{1,0:T(8,128)} custom-call(bf16[1280,256]{1,0:T(8,128)(2,1)} %bitcast.15), custom_call_target="tpu_custom_call" | custom-call | tf_op jit(solution)/shard_map/pallas_call | solution.py:387
  98.0 8.2 %all-to-all-start.1 = ((f32[16,16,80]{2,1,0:T(8,128)}), f32[16,16,80]{2,1,0:T(8,128)S(1)}, u32[]{:S(2)}, u32[]{:S(2)}) async-start(f32[16,16,80]{2,1,0:T(8,128)} %bitcast.18), calls=%async_computation.1 | async-start | bytes 262144 | tf_op jit(solution)/shard_map/all_to_all | solution.py:388
  106.2 8.9 %all-to-all-done.1 = f32[16,16,80]{2,1,0:T(8,128)S(1)} async-done(((f32[16,16,80]{2,1,0:T(8,128)}), f32[16,16,80]{2,1,0:T(8,128)S(1)}, u32[]{:S(2)}, u32[]{:S(2)}) %all-to-all-start.1) | async-done | bytes 81952 | tf_op jit(solution)/shard_map/all_to_all | solution.py:388
  115.7 1.2 fusion.1
  (41 shorter events, 3.9 us)
Async XLA Ops:
  0.6 17.4 %copy-start = (bf16[256,1152]{1,0:T(8,128)(2,1)S(1)}, bf16[256,1152]{1,0:T(8,128)(2,1)}, u32[]{:S(2)}) copy-start(bf16[256,1152]{1,0:T(8,128)(2,1)} %param.13) | copy-start | bytes 1769476
  4.8 4.3 %collective-permute-start = (bf16[256,128]{1,0:T(8,128)(2,1)}, bf16[256,128]{1,0:T(8,128)(2,1)S(1)}, u32[]{:S(2)}, u32[]{:S(2)}) collective-permute-start(bf16[256,128]{1,0:T(8,128)(2,1)} %get-tuple-element.41), channel_id=1, source_target_pairs={{0,16},{16,0},{32,48},{48,32},{64,80},{80,64},{96,112},{112,96},{1... | collective-permute-start | bytes 196616 | tf_op jit(solution)/shard_map/ppermute | solution.py:310
  8.0 3.9 %collective-permute-start.1 = (bf16[256,128]{1,0:T(8,128)(2,1)}, bf16[256,128]{1,0:T(8,128)(2,1)S(1)}, u32[]{:S(2)}, u32[]{:S(2)}) collective-permute-start(bf16[256,128]{1,0:T(8,128)(2,1)} %get-tuple-element.42), channel_id=1, source_target_pairs={{0,240},{16,32},{32,16},{48,64},{64,48},{80,96},{96,80},{112,128},... | collective-permute-start | bytes 196616 | tf_op jit(solution)/shard_map/ppermute | solution.py:310
  9.1 2.8 %copy-start.1 = (bf16[256,128]{1,0:T(8,128)(2,1)}, bf16[256,128]{1,0:T(8,128)(2,1)S(1)}, u32[]{:S(2)}) copy-start(bf16[256,128]{1,0:T(8,128)(2,1)S(1)} %collective-permute-done.r0_ref.refs_1_) | copy-start | bytes 196612
  11.9 0.6 copy-start.2
  14.3 5.4 %collective-permute-start.2 = (bf16[256,128]{1,0:T(8,128)(2,1)}, bf16[256,128]{1,0:T(8,128)(2,1)S(1)}, u32[]{:S(2)}, u32[]{:S(2)}) collective-permute-start(bf16[256,128]{1,0:T(8,128)(2,1)} %get-tuple-element.45), channel_id=1, source_target_pairs={{0,1},{1,0},{2,3},{3,2},{4,5},{5,4},{6,7},{7,6},{8,9},{9,8},{10,11... | collective-permute-start | bytes 196616 | tf_op jit(solution)/shard_map/ppermute | solution.py:310
  14.3 6.6 %collective-permute-start.3 = (bf16[256,128]{1,0:T(8,128)(2,1)}, bf16[256,128]{1,0:T(8,128)(2,1)S(1)}, u32[]{:S(2)}, u32[]{:S(2)}) collective-permute-start(bf16[256,128]{1,0:T(8,128)(2,1)} %get-tuple-element.46), channel_id=1, source_target_pairs={{0,15},{1,2},{2,1},{3,4},{4,3},{5,6},{6,5},{7,8},{8,7},{9,10},{10,... | collective-permute-start | bytes 196616 | tf_op jit(solution)/shard_map/ppermute | solution.py:310
  19.7 1.3 %copy-start.8 = (bf16[256,128]{1,0:T(8,128)(2,1)}, bf16[256,128]{1,0:T(8,128)(2,1)S(1)}, u32[]{:S(2)}) copy-start(bf16[256,128]{1,0:T(8,128)(2,1)S(1)} %collective-permute-done.2.refs_3_) | copy-start | bytes 196612
  21.0 0.6 copy-start.9
  27.1 6.5 %collective-permute-start.4 = (bf16[256,128]{1,0:T(8,128)(2,1)}, bf16[256,128]{1,0:T(8,128)(2,1)S(1)}, u32[]{:S(2)}, u32[]{:S(2)}) collective-permute-start(bf16[256,128]{1,0:T(8,128)(2,1)} %get-tuple-element.52), channel_id=1, source_target_pairs={{0,16},{16,0},{32,48},{48,32},{64,80},{80,64},{96,112},{112,96},{1... | collective-permute-start | bytes 196616 | tf_op jit(solution)/shard_map/ppermute | solution.py:310
  32.4 4.2 %collective-permute-start.5 = (bf16[256,128]{1,0:T(8,128)(2,1)}, bf16[256,128]{1,0:T(8,128)(2,1)S(1)}, u32[]{:S(2)}, u32[]{:S(2)}) collective-permute-start(bf16[256,128]{1,0:T(8,128)(2,1)} %get-tuple-element.53), channel_id=1, source_target_pairs={{0,240},{16,32},{32,16},{48,64},{64,48},{80,96},{96,80},{112,128},... | collective-permute-start | bytes 196616 | tf_op jit(solution)/shard_map/ppermute | solution.py:310
  33.5 3.1 %copy-start.3 = (bf16[256,128]{1,0:T(8,128)(2,1)}, bf16[256,128]{1,0:T(8,128)(2,1)S(1)}, u32[]{:S(2)}) copy-start(bf16[256,128]{1,0:T(8,128)(2,1)S(1)} %collective-permute-done.4.r0_ref.refs_2_) | copy-start | bytes 196612
  36.6 0.6 copy-start.4
  39.0 4.1 %collective-permute-start.6 = (bf16[256,128]{1,0:T(8,128)(2,1)}, bf16[256,128]{1,0:T(8,128)(2,1)S(1)}, u32[]{:S(2)}, u32[]{:S(2)}) collective-permute-start(bf16[256,128]{1,0:T(8,128)(2,1)} %get-tuple-element.56), channel_id=1, source_target_pairs={{0,1},{1,0},{2,3},{3,2},{4,5},{5,4},{6,7},{7,6},{8,9},{9,8},{10,11... | collective-permute-start | bytes 196616 | tf_op jit(solution)/shard_map/ppermute | solution.py:310
  39.0 6.6 %collective-permute-start.7 = (bf16[256,128]{1,0:T(8,128)(2,1)}, bf16[256,128]{1,0:T(8,128)(2,1)S(1)}, u32[]{:S(2)}, u32[]{:S(2)}) collective-permute-start(bf16[256,128]{1,0:T(8,128)(2,1)} %get-tuple-element.57), channel_id=1, source_target_pairs={{0,15},{1,2},{2,1},{3,4},{4,3},{5,6},{6,5},{7,8},{8,7},{9,10},{10,... | collective-permute-start | bytes 196616 | tf_op jit(solution)/shard_map/ppermute | solution.py:310
  43.1 2.6 %copy-start.10 = (bf16[256,128]{1,0:T(8,128)(2,1)}, bf16[256,128]{1,0:T(8,128)(2,1)S(1)}, u32[]{:S(2)}) copy-start(bf16[256,128]{1,0:T(8,128)(2,1)S(1)} %collective-permute-done.6.refs_4_) | copy-start | bytes 196612
  45.6 0.6 copy-start.11
  51.7 3.3 %collective-permute-start.8 = (bf16[256,128]{1,0:T(8,128)(2,1)}, bf16[256,128]{1,0:T(8,128)(2,1)S(1)}, u32[]{:S(2)}, u32[]{:S(2)}) collective-permute-start(bf16[256,128]{1,0:T(8,128)(2,1)} %get-tuple-element.61), channel_id=1, source_target_pairs={{0,16},{16,0},{32,48},{48,32},{64,80},{80,64},{96,112},{112,96},{1... | collective-permute-start | bytes 196616 | tf_op jit(solution)/shard_map/ppermute | solution.py:310
  53.9 4.2 %collective-permute-start.9 = (bf16[256,128]{1,0:T(8,128)(2,1)}, bf16[256,128]{1,0:T(8,128)(2,1)S(1)}, u32[]{:S(2)}, u32[]{:S(2)}) collective-permute-start(bf16[256,128]{1,0:T(8,128)(2,1)} %get-tuple-element.62), channel_id=1, source_target_pairs={{0,240},{16,32},{32,16},{48,64},{64,48},{80,96},{96,80},{112,128},... | collective-permute-start | bytes 196616 | tf_op jit(solution)/shard_map/ppermute | solution.py:310
  55.1 3.1 %copy-start.5 = (bf16[256,128]{1,0:T(8,128)(2,1)}, bf16[256,128]{1,0:T(8,128)(2,1)S(1)}, u32[]{:S(2)}) copy-start(bf16[256,128]{1,0:T(8,128)(2,1)S(1)} %collective-permute-done.8.r0_ref) | copy-start | bytes 196612
  58.1 0.6 copy-start.6
  60.5 12.0 %collective-permute-start.10 = (bf16[256,128]{1,0:T(8,128)(2,1)}, bf16[256,128]{1,0:T(8,128)(2,1)S(1)}, u32[]{:S(2)}, u32[]{:S(2)}) collective-permute-start(bf16[256,128]{1,0:T(8,128)(2,1)} %get-tuple-element.65), channel_id=1, source_target_pairs={{0,1},{1,0},{2,3},{3,2},{4,5},{5,4},{6,7},{7,6},{8,9},{9,8},{10,11... | collective-permute-start | bytes 196616 | tf_op jit(solution)/shard_map/ppermute | solution.py:310
  60.5 12.0 %collective-permute-start.11 = (bf16[256,128]{1,0:T(8,128)(2,1)}, bf16[256,128]{1,0:T(8,128)(2,1)S(1)}, u32[]{:S(2)}, u32[]{:S(2)}) collective-permute-start(bf16[256,128]{1,0:T(8,128)(2,1)} %get-tuple-element.66), channel_id=1, source_target_pairs={{0,15},{1,2},{2,1},{3,4},{4,3},{5,6},{6,5},{7,8},{8,7},{9,10},{10,... | collective-permute-start | bytes 196616 | tf_op jit(solution)/shard_map/ppermute | solution.py:310
  72.5 0.6 copy-start.12
  72.5 0.7 copy-start.13
  98.0 17.0 %all-to-all-start.1 = ((f32[16,16,80]{2,1,0:T(8,128)}), f32[16,16,80]{2,1,0:T(8,128)S(1)}, u32[]{:S(2)}, u32[]{:S(2)}) async-start(f32[16,16,80]{2,1,0:T(8,128)} %bitcast.18), calls=%async_computation.1 | async-start | bytes 262144 | tf_op jit(solution)/shard_map/all_to_all | solution.py:388
  115.1 1.8 %copy-start.7 = (f32[16,80]{1,0:T(8,128)}, f32[16,80]{1,0:T(8,128)S(1)}, u32[]{:S(2)}) copy-start(f32[16,80]{1,0:T(8,128)S(1)} %reduce_sum.9) | copy-start | bytes 15364

commit v2 on v1

v2 whole, which is shorter than its diff:
```python
import functools
import math

import jax
import jax.numpy as jnp
from jax import lax
from jax.experimental import pallas as pl
from jax.experimental.pallas import tpu as pltpu
from jax.sharding import PartitionSpec as P

INTERPRET = False
VMEM_LIMIT = 24 << 20
F32 = jnp.float32
BF16 = jnp.bfloat16
ROWS = 8
LANES = 128
SLABS = ROWS + 2
CH = 64
Q = 4 * CH
W = 2 * CH


def call(body, out_shape, in_specs=None, out_specs=None, scratch=(), aliases=None):
    kwargs = {}
    if in_specs is not None:
        kwargs["in_specs"] = in_specs
    if out_specs is not None:
        kwargs["out_specs"] = out_specs
    return pl.pallas_call(
        body,
        out_shape=out_shape,
        scratch_shapes=list(scratch),
        input_output_aliases=aliases or {},
        interpret=INTERPRET,
        grid=(1,),
        compiler_params=pltpu.CompilerParams(vmem_limit_bytes=VMEM_LIMIT),
        **kwargs,
    )


def whole():
    return pl.BlockSpec(memory_space=pltpu.VMEM)


def at_step(step, shape):
    return pl.BlockSpec((1,) + shape, lambda i: (step,) + (0,) * len(shape))


def in_hbm(x):
    return x if INTERPRET else pltpu.with_memory_space_constraint(x, pltpu.MemorySpace.HBM)


def sigmoid(x):
    return 0.5 * jnp.tanh(0.5 * x) + 0.5


def lane_ids(rows):
    return lax.broadcasted_iota(jnp.int32, (rows, LANES), 1)


def parity(axis):
    return lax.rem(lax.axis_index(axis), 2)


def edge_flags(axis):
    index = lax.axis_index(axis)
    low = jnp.where(index > 0, 1.0, 0.0).astype(F32)
    high = jnp.where(index < lax.axis_size(axis) - 1, 1.0, 0.0).astype(F32)
    return low, high


def gate_grads(pre, part, cot, dh, mask, cell_before, tanh_cell, dc):
    gin, gfor, gout, gcand = pre
    error = mask * (cot if dh is None else dh + cot)
    eo = error * gout
    grad = eo * (1.0 - tanh_cell * tanh_cell)
    if dc is not None:
        grad = dc + grad
    gi = grad * gin
    part[0] = gi * gcand * (1.0 - gin)
    df = grad * gfor
    part[1] = df * cell_before * (1.0 - gfor)
    part[2] = eo * tanh_cell * (1.0 - gout)
    part[3] = gi * (1.0 - gcand * gcand)
    return df


def emit_grads(scr, a_ref, p0_ref, p1_ref, ql_ref, qr_ref):
    par = parity("row")
    step = 32
    lanes = lane_ids(step)
    for k in range(Q // step):
        own = pl.ds(k * step, step)
        ql = jnp.zeros((step, LANES), F32)
        qr = jnp.zeros((step, LANES), F32)
        for r in range(ROWS):
            row = scr[pl.ds(k * step * ROWS + r, step, stride=ROWS), :]
            a_ref[own, r * LANES : (r + 1) * LANES] = row.astype(BF16)
            ql = jnp.where(lanes == r + 1, pltpu.roll(row, r + 1, 1), ql)
            qr = jnp.where(lanes == r + 1, pltpu.roll(row, r + 2, 1), qr)
        ql_ref[own, :] = ql.astype(BF16)
        qr_ref[own, :] = qr.astype(BF16)
    top = a_ref[:, 0:LANES]
    bottom = a_ref[:, (ROWS - 1) * LANES :]

    @pl.when(par == 0)
    def _():
        p0_ref[...] = bottom
        p1_ref[...] = top

    @pl.when(par == 1)
    def _():
        p0_ref[...] = top
        p1_ref[...] = bottom


def forward_kernel(pre_hbm, cot_hbm, c0_hbm, mask_hbm, c1_ref, c2_ref, h1_ref, h2_ref, dc_ref, a_ref, p0_ref, p1_ref, ql_ref, qr_ref, scr, pre_ref, cot_ref, c0_ref, mask_ref, sems):
    copies = [
        pltpu.make_async_copy(src, dst, sems.at[n])
        for n, (src, dst) in enumerate(
            [(c0_hbm, c0_ref), (mask_hbm, mask_ref)]
            + [(pre_hbm.at[t], pre_ref.at[t]) for t in range(3)]
            + [(cot_hbm.at[2], cot_ref)]
        )
    ]
    for copy in (copies[2], copies[0], copies[1], copies[3], copies[4], copies[5]):
        copy.start()
    step = 4

    def gate(t, g, base):
        return pre_ref[t, pl.ds(g * CH + base, step)].astype(F32)

    copies[0].wait()
    copies[1].wait()
    mask = mask_ref[...].astype(F32)[None]
    for t, (before_ref, c_ref, h_ref) in enumerate(((c0_ref, c1_ref, h1_ref), (c1_ref, c2_ref, h2_ref))):
        copies[2 + t].wait()

        def advance(j, carry):
            base = j * step
            own = pl.ds(base, step)
            cell = sigmoid(gate(t, 1, base)) * before_ref[own] + sigmoid(gate(t, 0, base)) * jnp.tanh(gate(t, 3, base))
            c_ref[own] = cell
            h_ref[own] = (mask * sigmoid(gate(t, 2, base)) * jnp.tanh(cell)).astype(BF16)
            return carry

        lax.fori_loop(0, CH // step, advance, 0)
    copies[4].wait()
    copies[5].wait()

    def chunk(j, carry):
        base = j * step
        own = pl.ds(base, step)
        cell = c2_ref[own]
        pre = (sigmoid(gate(2, 0, base)), sigmoid(gate(2, 1, base)), sigmoid(gate(2, 2, base)), jnp.tanh(gate(2, 3, base)))
        tanh_cell = jnp.tanh(pre[1] * cell + pre[0] * pre[3])
        part = [None] * 4
        dc_ref[own] = gate_grads(pre, part, cot_ref[own].astype(F32), None, mask, cell, tanh_cell, None)
        for g in range(4):
            scr[pl.ds((g * CH + base) * ROWS, step * ROWS), :] = part[g].reshape(step * ROWS, LANES)
        return carry

    lax.fori_loop(0, CH // step, chunk, 0)
    emit_grads(scr, a_ref, p0_ref, p1_ref, ql_ref, qr_ref)


def weights_kernel(k_ref, w_ref):
    for u in range(3):
        for v in range(3):
            tap = (3 * u + v) * W
            w_ref[u * W : (u + 1) * W, v * Q : (v + 1) * Q] = k_ref[:, tap : tap + W].astype(F32).T.astype(BF16)


def halo_rows(r0_ref, r1_ref, own):
    par = parity("row").astype(F32)
    low, high = edge_flags("row")
    first, second = r0_ref[own, :].astype(F32), r1_ref[own, :].astype(F32)
    above = second * ((1.0 - par) * low) + first * (par * low)
    below = first * ((1.0 - par) * high) + second * (par * high)
    return above, below


def corner_kernel(r0_ref, r1_ref, ql_ref, qr_ref, c0_ref, c1_ref):
    par = parity("col").astype(F32)
    step = 32
    lanes = lane_ids(step)
    for k in range(Q // step):
        own = pl.ds(k * step, step)
        above, below = halo_rows(r0_ref, r1_ref, own)
        left = jnp.where(lanes == 0, above, ql_ref[own, :].astype(F32))
        left = jnp.where(lanes == SLABS - 1, pltpu.roll(below, SLABS - 1, 1), left)
        right = jnp.where(lanes == 0, pltpu.roll(above, 1, 1), qr_ref[own, :].astype(F32))
        right = jnp.where(lanes == SLABS - 1, pltpu.roll(below, SLABS, 1), right)
        c0_ref[own, :] = (right * (1.0 - par) + left * par).astype(BF16)
        c1_ref[own, :] = (left * (1.0 - par) + right * par).astype(BF16)


def interior_kernel(a_ref, w_ref, b_ref, y_ref, y3):
    step = 32
    lanes = lane_ids(step)
    for k in range(Q // step):
        for r in range(ROWS):
            span = slice(r * LANES, (r + 1) * LANES)
            block = a_ref[pl.ds(k * step, step), span]
            row = block.astype(F32)
            minus = jnp.where(lanes == LANES - 1, 0.0, pltpu.roll(row, LANES - 1, 1))
            plus = jnp.where(lanes == 0, 0.0, pltpu.roll(row, 1, 1))
            b_ref[pl.ds(k * step, step), span] = minus.astype(BF16)
            b_ref[pl.ds(Q + k * step, step), span] = block
            b_ref[pl.ds(2 * Q + k * step, step), span] = plus.astype(BF16)
    y3[...] = lax.dot_general(w_ref[...], b_ref[...], (((1,), (0,)), ((), ())), preferred_element_type=F32)
    for r in range(ROWS):
        total = y3[W : 2 * W, r * LANES : (r + 1) * LANES]
        if r < ROWS - 1:
            total = total + y3[0:W, (r + 1) * LANES : (r + 2) * LANES]
        if r > 0:
            total = total + y3[2 * W : 3 * W, (r - 1) * LANES : r * LANES]
        y_ref[:, r * LANES : (r + 1) * LANES] = total


def build_halo(r0_ref, r1_ref, c0_ref, c1_ref, b_ref):
    par = parity("col").astype(F32)
    low, high = edge_flags("col")
    step = 32
    lanes = lane_ids(step)
    inside = (lanes >= 1) & (lanes <= ROWS)
    last = SLABS - 1
    for k in range(Q // step):
        own = pl.ds(k * step, step)
        above, below = halo_rows(r0_ref, r1_ref, own)
        first, second = c0_ref[own, :].astype(F32), c1_ref[own, :].astype(F32)
        left = second * ((1.0 - par) * low) + first * (par * low)
        right = first * ((1.0 - par) * high) + second * (par * high)
        for n, (row, s) in enumerate(((above, 0), (below, last))):
            span = slice(n * LANES, (n + 1) * LANES)
            minus = jnp.where(lanes == LANES - 1, pltpu.roll(right, LANES - 1 - s, 1), pltpu.roll(row, LANES - 1, 1))
            plus = jnp.where(lanes == 0, pltpu.roll(left, (LANES - s) % LANES, 1), pltpu.roll(row, 1, 1))
            b_ref[pl.ds(k * step, step), span] = minus.astype(BF16)
            b_ref[pl.ds(Q + k * step, step), span] = row.astype(BF16)
            b_ref[pl.ds(2 * Q + k * step, step), span] = plus.astype(BF16)
        span = slice(2 * LANES, 3 * LANES)
        b_ref[pl.ds(k * step, step), span] = jnp.where(inside, right, 0.0).astype(BF16)
        b_ref[pl.ds(Q + k * step, step), span] = jnp.zeros((step, LANES), BF16)
        b_ref[pl.ds(2 * Q + k * step, step), span] = pltpu.roll(jnp.where(inside, left, 0.0), LANES // 2, 1).astype(BF16)


def finish_y(w_ref, b_ref, y_ref, y3, scr):
    y3[...] = lax.dot_general(w_ref[...], b_ref[...], (((1,), (0,)), ((), ())), preferred_element_type=F32)
    step = 32
    lanes = lane_ids(step)
    for k in range(W // step):
        side = 0.0
        for u in range(3):
            piece = y3[pl.ds(u * W + k * step, step), 2 * LANES :]
            side = side + (piece if u == 2 else pltpu.roll(piece, LANES + u - 2, 1))
        for r in range(ROWS):
            total = y_ref[pl.ds(k * step, step), r * LANES : (r + 1) * LANES]
            if r == 0:
                total = total + y3[pl.ds(2 * W + k * step, step), 0:LANES]
            if r == ROWS - 1:
                total = total + y3[pl.ds(k * step, step), LANES : 2 * LANES]
            right = jnp.where(lanes == LANES - 1, pltpu.roll(side, LANES - 1 - r, 1), 0.0)
            left = jnp.where(lanes == 0, pltpu.roll(side, LANES // 2 - r, 1), right)
            scr[pl.ds(k * step * ROWS + r, step, stride=ROWS), :] = total + left


def backward_kernel(has_gi, *refs):
    if has_gi:
        refs = refs[1:]
    (r0_ref, r1_ref, k0_ref, k1_ref, w_ref, y_ref, pre_ref, cot_ref, before_ref, cell_ref, mask_ref, dc_in,
     gi_ref, b_ref, dc_ref, a_ref, p0_ref, p1_ref, ql_ref, qr_ref, y3, yscr, scr) = refs
    build_halo(r0_ref, r1_ref, k0_ref, k1_ref, b_ref)
    finish_y(w_ref, b_ref, y_ref, y3, yscr)
    step = 4
    mask = mask_ref[...].astype(F32)[None]

    def chunk(j, carry):
        base = j * step
        own = pl.ds(base, step)

        def gate(g):
            return pre_ref[0, pl.ds(g * CH + base, step)].astype(F32)

        gi_ref[0, own] = yscr[pl.ds(base * ROWS, step * ROWS), :].reshape(step, ROWS, LANES).astype(BF16)
        dh = yscr[pl.ds((CH + base) * ROWS, step * ROWS), :].reshape(step, ROWS, LANES)
        pre = (sigmoid(gate(0)), sigmoid(gate(1)), sigmoid(gate(2)), jnp.tanh(gate(3)))
        part = [None] * 4
        dc_ref[own] = gate_grads(pre, part, cot_ref[0, own].astype(F32), dh, mask, before_ref[own], jnp.tanh(cell_ref[own]), dc_in[own])
        for g in range(4):
            scr[pl.ds((g * CH + base) * ROWS, step * ROWS), :] = part[g].reshape(step * ROWS, LANES)
        return carry

    lax.fori_loop(0, CH // step, chunk, 0)
    emit_grads(scr, a_ref, p0_ref, p1_ref, ql_ref, qr_ref)


def last_kernel(gi_in, w_ref, y_ref, b_ref, gi_ref, dh_ref, y3, yscr):
    del gi_in
    finish_y(w_ref, b_ref, y_ref, y3, yscr)
    gi_ref[0] = yscr[0 : CH * ROWS, :].reshape(CH, ROWS, LANES).astype(BF16)
    dh_ref[...] = yscr[CH * ROWS :, :].reshape(CH, ROWS, LANES)


ZROWS = 3 * W + 16
CELLS = ROWS * LANES
CONTRACT_LANES = (((1,), (1,)), ((), ()))


def stack_fields(x_ref, h_ref, tmp):
    tmp[0 : CH * ROWS, :] = x_ref[0].astype(F32).reshape(CH * ROWS, LANES)
    tmp[CH * ROWS :, :] = h_ref[...].astype(F32).reshape(CH * ROWS, LANES)


def taps(z3, b_ref, bias):
    for v in range(3):
        span = ZROWS if bias and v == 1 else 3 * W
        got = lax.dot_general(z3[0:span, :], b_ref[v * Q : (v + 1) * Q, :], CONTRACT_LANES, preferred_element_type=F32)
        for u in range(3):
            yield u * 3 + v, got[u * W : (u + 1) * W]
        if bias and v == 1:
            yield 9, got[3 * W :]


def interior_taps(tmp, b_ref, z3):
    zero = jnp.zeros((W, LANES), BF16)
    z3[0:W, 0:LANES] = zero
    z3[2 * W : 3 * W, CELLS - LANES :] = zero
    for r in range(ROWS):
        row = tmp[pl.ds(r, W, stride=ROWS), :].astype(BF16)
        for u in range(3):
            n = r + 1 - u
            if 0 <= n < ROWS:
                z3[u * W : (u + 1) * W, n * LANES : (n + 1) * LANES] = row
    ids = lax.broadcasted_iota(jnp.int32, (16, CELLS), 0)
    z3[3 * W :, :] = jnp.where(ids == 0, 1.0, 0.0).astype(BF16)
    yield from taps(z3, b_ref, True)


def halo_taps(tmp, b_ref, zh):
    zero = jnp.zeros((W, LANES), BF16)
    zh[0:W, 0:LANES] = zero
    zh[W : 2 * W, 0:LANES] = zero
    zh[2 * W :, 0:LANES] = tmp[pl.ds(0, W, stride=ROWS), :].astype(BF16)
    zh[0:W, LANES : 2 * LANES] = tmp[pl.ds(ROWS - 1, W, stride=ROWS), :].astype(BF16)
    zh[W : 2 * W, LANES : 2 * LANES] = zero
    zh[2 * W :, LANES : 2 * LANES] = zero
    step = 32
    lanes = lane_ids(step)
    half = LANES // 2
    for k in range(W // step):
        side = jnp.zeros((step, LANES), F32)
        for r in range(ROWS):
            row = tmp[pl.ds(k * step * ROWS + r, step, stride=ROWS), :]
            side = jnp.where(lanes == r, pltpu.roll(row, r + 1, 1), side)
            side = jnp.where(lanes == half + r, pltpu.roll(row, half + r, 1), side)
        for u in range(3):
            zh[pl.ds(u * W + k * step, step), 2 * LANES :] = (side if u == 2 else pltpu.roll(side, 2 - u, 1)).astype(BF16)
    yield from taps(zh, b_ref, False)


def accumulate_kernel(has_acc, with_halo, *refs):
    refs = list(refs)
    acc_ref = refs.pop(0) if has_acc else None
    x_ref, h_ref, b_ref = refs[:3]
    out_ref, z3, zh, tmp = refs[-4:]
    stack_fields(x_ref, h_ref, tmp)
    for tap, got in interior_taps(tmp, b_ref, z3):
        rows = slice(tap * W, tap * W + got.shape[0])
        out_ref[rows, :] = acc_ref[rows, :] + got if has_acc else got
    if with_halo:
        for tap, got in halo_taps(tmp, refs[3], zh):
            rows = slice(tap * W, tap * W + got.shape[0])
            out_ref[rows, :] += got


def send_kernel(blocks, scale, acc_ref, x_ref, h_ref, r0_ref, r1_ref, k0_ref, k1_ref, out_ref, b_ref, zh, tmp, total):
    build_halo(r0_ref, r1_ref, k0_ref, k1_ref, b_ref)
    stack_fields(x_ref, h_ref, tmp)
    for tap, got in halo_taps(tmp, b_ref, zh):
        rows = slice(tap * W, tap * W + got.shape[0])
        total[rows, :] = (acc_ref[rows, :] + got) * scale
    bias = acc_ref[9 * W : 9 * W + 8, :] * scale
    high = jnp.broadcast_to(bias[0:1], (8, Q)).astype(BF16).astype(F32)
    low = jnp.broadcast_to(bias[0:1], (8, Q)) - high
    ids = lax.broadcasted_iota(jnp.int32, (8, Q), 0)
    tail = jnp.where(ids == 0, high, jnp.where(ids == 1, low, 0.0))
    size = 9 * W // blocks
    for c in range(blocks):
        body = jnp.concatenate([total[c * size : (c + 1) * size, :], tail], axis=0)
        out_ref[c * (size + 8) : (c + 1) * (size + 8), :] = body.astype(BF16)


def result_kernel(blocks, in_ref, k_ref, bias_ref, scr):
    size = in_ref.shape[0] // blocks
    total = in_ref[0:size, :]
    for c in range(1, blocks):
        total = total + in_ref[c * size : (c + 1) * size, :]
    taps_here = k_ref.shape[1]
    k_ref[...] = total[:, 0:taps_here]
    scr[...] = jnp.broadcast_to(total[:, taps_here : taps_here + 1] + total[:, taps_here + 1 : taps_here + 2], scr.shape)
    count = bias_ref.shape[0]
    bias_ref[...] = scr[pl.ds(lax.axis_index("col") * count, count), 0:1]


def fold_kernel(blocks, in_ref, out_ref):
    size = in_ref.shape[0] // blocks
    total = in_ref[0:size, :].astype(F32)
    for c in range(1, blocks):
        total = total + in_ref[c * size : (c + 1) * size, :].astype(F32)
    out_ref[...] = total.T


def even_swap(count):
    return [(i, i ^ 1) for i in range(count)]


def odd_swap(count):
    return [(i, (i + 1) % count if i % 2 else (i - 1) % count) for i in range(count)]


def swaps(first, second, axis):
    count = lax.axis_size(axis)
    return lax.ppermute(first, axis, even_swap(count)), lax.ppermute(second, axis, odd_swap(count))


def struct(shape, dtype):
    return jax.ShapeDtypeStruct(shape, dtype)


def shards(inputs, gate_pre, cotangent, hidden_init, cell_init, land_mask, kernel):
    field = (CH, ROWS, LANES)
    nrow, ncol = lax.axis_size("row"), lax.axis_size("col")
    scale = 1.0 / math.sqrt(ROWS * LANES * nrow * ncol)
    edge = struct((Q, LANES), BF16)
    grads_out = (struct((Q, CELLS), BF16), edge, edge, edge, edge)
    scr = pltpu.VMEM((Q * ROWS, LANES), F32)
    y3 = pltpu.VMEM((3 * W, 3 * LANES), F32)
    tmp = pltpu.VMEM((W * ROWS, LANES), F32)
    z3, zh = pltpu.VMEM((ZROWS, CELLS), BF16), pltpu.VMEM((3 * W, 3 * LANES), BF16)
    hbm = pl.BlockSpec(memory_space=pltpu.MemorySpace.HBM)

    c1, c2, h1, h2, dc, a, p0, p1, ql, qr = call(
        forward_kernel,
        (struct(field, F32), struct(field, F32), struct(field, BF16), struct(field, BF16), struct(field, F32)) + grads_out,
        in_specs=[hbm] * 4,
        out_specs=[whole()] * 10,
        scratch=[
            scr,
            pltpu.VMEM((3, Q, ROWS, LANES), BF16),
            pltpu.VMEM(field, BF16),
            pltpu.VMEM(field, F32),
            pltpu.VMEM((ROWS, LANES), jnp.int32),
            pltpu.SemaphoreType.DMA((6,)),
        ],
    )(*(in_hbm(x) for x in (gate_pre, cotangent, cell_init, land_mask)))

    cells = [cell_init, c1, c2]
    hiddens = [hidden_init, h1, h2]
    gi_shape = struct((3,) + field, BF16)
    interior, halo = struct((3 * Q, CELLS), BF16), struct((3 * Q, 3 * LANES), BF16)
    acc_shape = struct((ZROWS + 6 * W, Q), F32)

    def accumulate(t, acc, b, bh):
        head = [] if acc is None else [acc]
        rest = [b] if bh is None else [b, bh]
        return call(
            functools.partial(accumulate_kernel, acc is not None, bh is not None),
            acc_shape,
            in_specs=[whole()] * len(head) + [at_step(t, field)] + [whole()] * (1 + len(rest)),
            out_specs=whole(),
            scratch=[z3, zh, tmp],
            aliases={0: 0} if head else {},
        )(*head, inputs, hiddens[t], *rest)

    gi = acc = weights = b = bh = None
    for t in (2, 1, 0):
        r0, r1 = swaps(p0, p1, "row")
        if t == 2:
            weights = call(weights_kernel, struct((3 * W, 3 * Q), BF16), in_specs=[whole()], out_specs=whole())(kernel)
            r0, r1, weights = lax.optimization_barrier((r0, r1, weights))
        else:
            acc = accumulate(t + 1, acc, b, bh)
            r0, r1, acc = lax.optimization_barrier((r0, r1, acc))
        k0, k1 = call(corner_kernel, (edge, edge), in_specs=[whole()] * 4, out_specs=[whole()] * 2)(r0, r1, ql, qr)
        k0, k1 = swaps(k0, k1, "col")
        b, y = call(
            interior_kernel,
            (interior, struct((W, CELLS), F32)),
            in_specs=[whole()] * 2,
            out_specs=[whole()] * 2,
            scratch=[pltpu.VMEM((3 * W, CELLS), F32)],
        )(a, weights)
        if t > 0:
            head = [] if gi is None else [gi]
            gi, bh, dc, a, p0, p1, ql, qr = call(
                functools.partial(backward_kernel, gi is not None),
                (gi_shape, halo, struct(field, F32)) + grads_out,
                in_specs=[pl.BlockSpec(memory_space=pl.ANY)] * len(head)
                + [whole()] * 6
                + [at_step(t - 1, (Q, ROWS, LANES)), at_step(t - 1, field)]
                + [whole()] * 4,
                out_specs=[at_step(t, field)] + [whole()] * 7,
                scratch=[y3, tmp, scr],
                aliases={0: 0} if head else {},
            )(*head, r0, r1, k0, k1, weights, y, gate_pre, cotangent, cells[t - 1], cells[t], land_mask, dc)
    acc = accumulate(0, acc, b, None)
    size = 9 * W // ncol + 8
    send, bh = call(
        functools.partial(send_kernel, ncol, scale),
        (struct((ncol * size, Q), BF16), halo),
        in_specs=[whole(), at_step(0, field)] + [whole()] * 5,
        out_specs=[whole()] * 2,
        scratch=[zh, tmp, pltpu.VMEM((9 * W, Q), F32)],
    )(acc, inputs, hiddens[0], r0, r1, k0, k1)
    got = lax.all_to_all(send, "col", 0, 0, tiled=True)
    folded = call(functools.partial(fold_kernel, ncol), struct((Q, size), F32), in_specs=[whole()], out_specs=whole())(got)
    got = lax.all_to_all(folded, "row", 0, 0, tiled=True)
    y, folded = lax.optimization_barrier((y, folded))
    gi, grad_hidden = call(
        last_kernel,
        (gi_shape, struct(field, F32)),
        in_specs=[pl.BlockSpec(memory_space=pl.ANY)] + [whole()] * 3,
        out_specs=[at_step(0, field), whole()],
        scratch=[y3, tmp],
        aliases={0: 0},
    )(gi, weights, y, bh)
    count = Q // nrow // ncol
    grad_kernel, grad_bias = call(
        functools.partial(result_kernel, nrow),
        (struct((Q // nrow, size - 8), F32), struct((count, 1), F32)),
        in_specs=[whole()],
        out_specs=[whole()] * 2,
        scratch=[pltpu.VMEM((Q // nrow, LANES), F32)],
    )(got)
    return (gi, grad_hidden, dc, grad_kernel, grad_bias.reshape(count))


def solution(mesh):
    placed = (
        P(None, None, "row", "col"),
        P(None, None, "row", "col"),
        P(None, None, "row", "col"),
        P(None, "row", "col"),
        P(None, "row", "col"),
        P("row", "col"),
        P(),
    )
    return jax.shard_map(
        shards,
        mesh=mesh,
        in_specs=placed,
        out_specs=(
            P(None, None, "row", "col"),
            P(None, "row", "col"),
            P(None, "row", "col"),
            P("row", "col"),
            P(("row", "col")),
        ),
        check_vma=False,
    )
```

time: 117 us -> 87.2 us (0.75)
  Pallas kernels: 37.8 us -> 19 us
  local copies, waits for them, and re-layouts: 6.05 us -> 0.04 us
  waiting for transfers between devices: 25 us -> 19.7 us
  other arithmetic: 1.19 us -> 0 us
    pallas_call x6 -> x12, Pallas kernels: 26.4 us -> 14.6 us  [the longest x2 4.87 us: shards(): call(functools.partial(backward_kernel, gi is not None), (gi_shape, halo,...]
    unnamed x30 -> x14, local copies, waits for them, and re-layouts: 4.95 us -> 0.04 us
    pallas_call x3, Pallas kernels: 5.29 us -> 0.53 us  [shards(): call(corner_kernel, (edge, edge), in_specs=[whole()] * 4, out_specs=[whol...]
    ppermute x6, waiting for transfers between devices: 3.34 us -> 0.67 us  [swaps(): lax.ppermute(first, axis, even_swap(count))]
    all_to_all x1, waiting for transfers between devices: 8.89 us -> 7.36 us  [shards(): got = lax.all_to_all(folded, 'row', 0, 0, tiled=True)]
  transfers between devices with their start and end apart: 13 -> 13, of which waited for: 9 -> 8; matrix products, arithmetic and copies ran while one was open for 1% -> 0% of each run, Pallas kernels for 7% -> 9%
where the time goes in v2:
time: 87.2 us; the launch traced here: 86.9 us
  starting transfers between devices  31.8 us (36%)
  waiting for transfers between devices  19.7 us (23%)
  Pallas kernels  19 us (22%)
  blocking collectives  15.6 us (18%)
    all_to_all x1, blocking collectives, shards(): got = lax.all_to_all(send, 'col', 0, 0, tiled=True)  15.6 us
    ppermute x6, starting transfers between devices, swaps(): lax.ppermute(second, axis, odd_swap(count))  12 us
    ppermute x6, waiting for transfers between devices, swaps(): lax.ppermute(second, axis, odd_swap(count))  11.7 us
    ppermute x6, starting transfers between devices, swaps(): lax.ppermute(first, axis, even_swap(count))  10.8 us
    all_to_all x1, starting transfers between devices, shards(): got = lax.all_to_all(folded, 'row', 0, 0, tiled=True)  8.97 us
    all_to_all x1, waiting for transfers between devices, shards(): got = lax.all_to_all(folded, 'row', 0, 0, tiled=True)  7.36 us
    pallas_call x2, Pallas kernels, shards(): call(functools.partial(backward_kernel, gi is not None), (gi_shape, halo,...  4.87 us
    pallas_call x3, Pallas kernels, accumulate(): call(functools.partial(accumulate_kernel, acc is not None, bh is not None...  3.53 us
  transfers between devices with their start and end apart: 13, of which 8 were waited for; matrix products, arithmetic and copies ran while one was open for 0% of the time, Pallas kernels for 9%

profile of v2, /device:TPU:1, one launch (start us, length us, event | category | flops | bytes accessed | tf_op | source)
XLA Modules:
  0.0 86.9 jit_solution(5882003145092533740)
XLA Ops:
  0.6 3.0 %shard_map.110 = (f32[64,8,128]{2,1,0:T(8,128)S(1)}, f32[64,8,128]{2,1,0:T(8,128)S(1)}, bf16[64,8,128]{2,1,0:T(8,128)(2,1)S(1)}, bf16[64,8,128]{2,1,0:T(8,128)(2...) custom-call(bf16[3,256,8,128]{3,2,1,0:T(8,128)(2,1)} %refs_7_.3, ...), custom_call_target="tpu_custom_call" | custom-call | tf_op jit(solution)/shard_map/pallas_call | solution.py:442
  3.7 3.3 %collective-permute-start = (bf16[256,128]{1,0:T(8,128)(2,1)S(1)}, bf16[256,128]{1,0:T(8,128)(2,1)S(1)}, u32[]{:S(2)}, u32[]{:S(2)}) collective-permute-start(bf16[256,128]{1,0:T(8,128)(2,1)S(1)} %get-tuple-element.59), channel_id=1, source_target_pairs={{0,16},{16,0},{32,48},{48,32},{64,80},{80,64},{96,112},{112,96},{1... | collective-permute-start | bytes 196616 | tf_op jit(solution)/shard_map/ppermute | solution.py:423
  7.0 0.2 shard_map.111.w_ref.refs_4_.refs_5_
  7.2 0.7 collective-permute-done.r0_ref.refs_0_
  7.9 2.8 %collective-permute-done.1.r1_ref.refs_1_ = bf16[256,128]{1,0:T(8,128)(2,1)S(1)} collective-permute-done((bf16[256,128]{1,0:T(8,128)(2,1)S(1)}, bf16[256,128]{1,0:T(8,128)(2,1)S(1)}, u32[]{:S(2)}, u32[]{:S(2)}) %collective-permute-start.1) | collective-permute-done | bytes 65568 | tf_op jit(solution)/shard_map/ppermute | solution.py:423
  10.7 0.2 shard_map.112
  11.0 3.7 %collective-permute-start.3 = (bf16[256,128]{1,0:T(8,128)(2,1)S(1)}, bf16[256,128]{1,0:T(8,128)(2,1)S(1)}, u32[]{:S(2)}, u32[]{:S(2)}) collective-permute-start(bf16[256,128]{1,0:T(8,128)(2,1)S(1)} %get-tuple-element.66), channel_id=1, source_target_pairs={{0,15},{1,2},{2,1},{3,4},{4,3},{5,6},{6,5},{7,8},{8,7},{9,10},{10,... | collective-permute-start | bytes 196616 | tf_op jit(solution)/shard_map/ppermute | solution.py:423
  14.6 1.0 %shard_map.113 = (bf16[768,1024]{1,0:T(8,128)(2,1)S(1)}, f32[128,1024]{1,0:T(8,128)S(1)}) custom-call(bf16[256,1024]{1,0:T(8,128)(2,1)S(1)} %get-tuple-element.68.a_ref, bf16[384,768]{1,0:T(8,128)(2,1)S(1)} %shard_map.111.w_ref.refs_4_.refs_5_), custom_call_target="tpu_custom_call" | custom-call | tf_op jit(solution)/shard_map/pallas_call | solution.py:486
  15.6 1.9 %collective-permute-done.3.refs_3_ = bf16[256,128]{1,0:T(8,128)(2,1)S(1)} collective-permute-done((bf16[256,128]{1,0:T(8,128)(2,1)S(1)}, bf16[256,128]{1,0:T(8,128)(2,1)S(1)}, u32[]{:S(2)}, u32[]{:S(2)}) %collective-permute-start.3) | collective-permute-done | bytes 65568 | tf_op jit(solution)/shard_map/ppermute | solution.py:423
  17.5 2.4 %shard_map.114 = (bf16[3,64,8,128]{3,2,1,0:T(8,128)(2,1)}, bf16[768,384]{1,0:T(8,128)(2,1)S(1)}, f32[64,8,128]{2,1,0:T(8,128)S(1)}, bf16[256,1024]{1,0:T(8,128)(...) custom-call(bf16[256,128]{1,0:T(8,128)(2,1)S(1)} %collective-permute, ...), custom_call_target="tpu_custom_call" | custom-call | tf_op jit(solution)/shard_map/pallas_call | solution.py:495
  19.9 5.1 %collective-permute-start.4 = (bf16[256,128]{1,0:T(8,128)(2,1)S(1)}, bf16[256,128]{1,0:T(8,128)(2,1)S(1)}, u32[]{:S(2)}, u32[]{:S(2)}) collective-permute-start(bf16[256,128]{1,0:T(8,128)(2,1)S(1)} %get-tuple-element.74), channel_id=1, source_target_pairs={{0,16},{16,0},{32,48},{48,32},{64,80},{80,64},{96,112},{112,96},{1... | collective-permute-start | bytes 196616 | tf_op jit(solution)/shard_map/ppermute | solution.py:423
  25.0 1.2 %shard_map.115.refs_0_ = f32[1168,256]{1,0:T(8,128)S(1)} custom-call(bf16[3,64,8,128]{3,2,1,0:T(8,128)(2,1)S(1)} %copy-done.1, bf16[64,8,128]{2,1,0:T(8,128)(2,1)S(1)} %get-tuple-element.76.refs_1_, bf16[768,1024]{1,0:T(8,128)(2,1)S(1)} %get-tuple-element.77.refs_2_, bf16[768,384]{1,0:T(8,128)(2,1)S(1)} %get-tuple-element.78.refs_3_), custom_call_target="tpu_custom_call" | custom-call | tf_op jit(solution)/shard_map/pallas_call | solution.py:466
  26.3 2.8 %collective-permute-done.5.r1_ref.refs_2_ = bf16[256,128]{1,0:T(8,128)(2,1)S(1)} collective-permute-done((bf16[256,128]{1,0:T(8,128)(2,1)S(1)}, bf16[256,128]{1,0:T(8,128)(2,1)S(1)}, u32[]{:S(2)}, u32[]{:S(2)}) %collective-permute-start.5) | collective-permute-done | bytes 65568 | tf_op jit(solution)/shard_map/ppermute | solution.py:423
  29.3 4.2 %collective-permute-start.7 = (bf16[256,128]{1,0:T(8,128)(2,1)S(1)}, bf16[256,128]{1,0:T(8,128)(2,1)S(1)}, u32[]{:S(2)}, u32[]{:S(2)}) collective-permute-start(bf16[256,128]{1,0:T(8,128)(2,1)S(1)} %get-tuple-element.84), channel_id=1, source_target_pairs={{0,15},{1,2},{2,1},{3,4},{4,3},{5,6},{6,5},{7,8},{8,7},{9,10},{10,... | collective-permute-start | bytes 196616 | tf_op jit(solution)/shard_map/ppermute | solution.py:423
  33.5 1.0 %shard_map.117 = (bf16[768,1024]{1,0:T(8,128)(2,1)S(1)}, f32[128,1024]{1,0:T(8,128)S(1)}) custom-call(bf16[256,1024]{1,0:T(8,128)(2,1)S(1)} %get-tuple-element.85.a_ref, bf16[384,768]{1,0:T(8,128)(2,1)S(1)} %shard_map.111.w_ref.refs_4_.refs_5_), custom_call_target="tpu_custom_call" | custom-call | tf_op jit(solution)/shard_map/pallas_call | solution.py:486
  34.5 1.3 %collective-permute-done.7.refs_4_ = bf16[256,128]{1,0:T(8,128)(2,1)S(1)} collective-permute-done((bf16[256,128]{1,0:T(8,128)(2,1)S(1)}, bf16[256,128]{1,0:T(8,128)(2,1)S(1)}, u32[]{:S(2)}, u32[]{:S(2)}) %collective-permute-start.7) | collective-permute-done | bytes 65568 | tf_op jit(solution)/shard_map/ppermute | solution.py:423
  35.8 2.5 %shard_map.118 = (bf16[3,64,8,128]{3,2,1,0:T(8,128)(2,1)}, bf16[768,384]{1,0:T(8,128)(2,1)S(1)}, f32[64,8,128]{2,1,0:T(8,128)}, bf16[256,1024]{1,0:T(8,128)(2,1)...) custom-call(bf16[3,64,8,128]{3,2,1,0:T(8,128)(2,1)} %get-tuple-eleme, ...), custom_call_target="tpu_custom_call", output_to_operand_aliasing={{0}: (0, {})} | custom-call | tf_op jit(solution)/shard_map/pallas_call | solution.py:495
  38.3 2.1 %collective-permute-start.8 = (bf16[256,128]{1,0:T(8,128)(2,1)S(1)}, bf16[256,128]{1,0:T(8,128)(2,1)S(1)}, u32[]{:S(2)}, u32[]{:S(2)}) collective-permute-start(bf16[256,128]{1,0:T(8,128)(2,1)S(1)} %get-tuple-element.91), channel_id=1, source_target_pairs={{0,16},{16,0},{32,48},{48,32},{64,80},{80,64},{96,112},{112,96},{1... | collective-permute-start | bytes 196616 | tf_op jit(solution)/shard_map/ppermute | solution.py:423
  40.4 1.4 %shard_map.120.refs_0_ = f32[1168,256]{1,0:T(8,128)S(1)} custom-call(f32[1168,256]{1,0:T(8,128)S(1)} %shard_map.115.refs_0_, bf16[3,64,8,128]{3,2,1,0:T(8,128)(2,1)S(1)} %copy-done.1, bf16[64,8,128]{2,1,0:T(8,128)(2,1)S(1)} %get-tuple-element.94.refs_2_, bf16[768,1024]{1,0:T(8,128)(2,1)S(1)} %get-tuple-element.95.refs_3_, ...), custom_call_target="tpu_custom_call", output_to_operand_aliasing={{}: (0, {})} | custom-call | tf_op jit(solution)/shard_map/pallas_call | solution.py:466
  41.8 2.5 %collective-permute-done.9.r1_ref = bf16[256,128]{1,0:T(8,128)(2,1)S(1)} collective-permute-done((bf16[256,128]{1,0:T(8,128)(2,1)S(1)}, bf16[256,128]{1,0:T(8,128)(2,1)S(1)}, u32[]{:S(2)}, u32[]{:S(2)}) %collective-permute-start.9) | collective-permute-done | bytes 65568 | tf_op jit(solution)/shard_map/ppermute | solution.py:423
  44.4 0.2 shard_map.122
  44.6 4.2 %collective-permute-start.11 = (bf16[256,128]{1,0:T(8,128)(2,1)S(1)}, bf16[256,128]{1,0:T(8,128)(2,1)S(1)}, u32[]{:S(2)}, u32[]{:S(2)}) collective-permute-start(bf16[256,128]{1,0:T(8,128)(2,1)S(1)} %get-tuple-element.104), channel_id=1, source_target_pairs={{0,15},{1,2},{2,1},{3,4},{4,3},{5,6},{6,5},{7,8},{8,7},{9,10},{10,... | collective-permute-start | bytes 196616 | tf_op jit(solution)/shard_map/ppermute | solution.py:423
  48.8 1.0 %shard_map.119 = (bf16[768,1024]{1,0:T(8,128)(2,1)S(1)}, f32[128,1024]{1,0:T(8,128)S(1)}) custom-call(bf16[256,1024]{1,0:T(8,128)(2,1)S(1)} %get-tuple-element.89.a_ref, bf16[384,768]{1,0:T(8,128)(2,1)S(1)} %shard_map.111.w_ref.refs_4_.refs_5_), custom_call_target="tpu_custom_call" | custom-call | tf_op jit(solution)/shard_map/pallas_call | solution.py:486
  49.8 0.9 %shard_map.121.acc_ref = f32[1168,256]{1,0:T(8,128)S(1)} custom-call(f32[1168,256]{1,0:T(8,128)S(1)} %shard_map.120.refs_0_, bf16[3,64,8,128]{3,2,1,0:T(8,128)(2,1)S(1)} %copy-done.1, bf16[64,8,128]{2,1,0:T(8,128)(2,1)S(1)} %copy-done.5, bf16[768,1024]{1,0:T(8,128)(2,1)S(1)} %get-tuple-element.98.refs_3_), custom_call_target="tpu_custom_call", output_to_operand_aliasing={{}: (0, {})} | custom-call | tf_op jit(solution)/shard_map/pallas_call | solution.py:466
  50.7 0.4 collective-permute-done.11.k1_ref
  51.2 0.8 shard_map.123
  52.0 15.6 %all_to_all.22 = bf16[16,80,256]{2,1,0:T(8,128)(2,1)S(1)} all-to-all(bf16[16,80,256]{2,1,0:T(8,128)(2,1)S(1)} %bitcast.6), channel_id=1, replica_groups=mesh['row'=16,'col'=16] {'col'}, dimensions={0} | all-to-all | bytes 1310720 | tf_op jit(solution)/shard_map/all_to_all | solution.py:515
  67.6 0.8 shard_map.124
  68.4 9.0 %all-to-all-start.1 = ((f32[16,16,80]{2,1,0:T(8,128)}), f32[16,16,80]{2,1,0:T(8,128)S(1)}, u32[]{:S(2)}, u32[]{:S(2)}) async-start(f32[16,16,80]{2,1,0:T(8,128)} %bitcast.2), calls=%async_computation.1 | async-start | bytes 262144 | tf_op jit(solution)/shard_map/all_to_all | solution.py:517
  77.4 1.5 %shard_map.125 = (bf16[3,64,8,128]{3,2,1,0:T(8,128)(2,1)}, f32[64,8,128]{2,1,0:T(8,128)}) custom-call(bf16[3,64,8,128]{3,2,1,0:T(8,128)(2,1)} %get-tuple-element.88.gi_in, bf16[384,768]{1,0:T(8,128)(2,1)S(1)} %shard_map.111.w_ref.refs_4_.refs_5_, f32[128,1024]{1,0:T(8,128)S(1)} %get-tuple-element.106.y_ref, ...), custom_call_target="tpu_custom_call", output_to_operand_aliasing={{0}: (0, {})} | custom-call | tf_op jit(solution)/shard_map/pallas_call | solution.py:519
  78.9 7.4 %all-to-all-done.1 = f32[16,16,80]{2,1,0:T(8,128)S(1)} async-done(((f32[16,16,80]{2,1,0:T(8,128)}), f32[16,16,80]{2,1,0:T(8,128)S(1)}, u32[]{:S(2)}, u32[]{:S(2)}) %all-to-all-start.1) | async-done | bytes 81952 | tf_op jit(solution)/shard_map/all_to_all | solution.py:517
  86.3 0.7 shard_map.126
  (26 shorter events, 0.5 us)
Async XLA Ops:
  0.6 6.4 %copy-start.4 = (bf16[256,1152]{1,0:T(8,128)(2,1)S(1)}, bf16[256,1152]{1,0:T(8,128)(2,1)}, u32[]{:S(2)}) copy-start(bf16[256,1152]{1,0:T(8,128)(2,1)} %k_ref.1) | copy-start | bytes 1769476
  3.7 13.8 %copy-start = (bf16[3,256,8,128]{3,2,1,0:T(8,128)(2,1)S(1)}, bf16[3,256,8,128]{3,2,1,0:T(8,128)(2,1)}, u32[]{:S(2)}) copy-start(bf16[3,256,8,128]{3,2,1,0:T(8,128)(2,1)} %refs_7_.3) | copy-start | bytes 4718596
  3.7 13.8 %copy-start.2 = (bf16[3,64,8,128]{3,2,1,0:T(8,128)(2,1)S(1)}, bf16[3,64,8,128]{3,2,1,0:T(8,128)(2,1)}, u32[]{:S(2)}) copy-start(bf16[3,64,8,128]{3,2,1,0:T(8,128)(2,1)} %refs_8_.1) | copy-start | bytes 1179652
  3.7 13.8 %copy-start.6 = (s32[8,128]{1,0:T(8,128)S(1)}, s32[8,128]{1,0:T(8,128)}, u32[]{:S(2)}) copy-start(s32[8,128]{1,0:T(8,128)} %refs_11_.1) | copy-start | bytes 12292
  3.7 4.2 %collective-permute-start = (bf16[256,128]{1,0:T(8,128)(2,1)S(1)}, bf16[256,128]{1,0:T(8,128)(2,1)S(1)}, u32[]{:S(2)}, u32[]{:S(2)}) collective-permute-start(bf16[256,128]{1,0:T(8,128)(2,1)S(1)} %get-tuple-element.59), channel_id=1, source_target_pairs={{0,16},{16,0},{32,48},{48,32},{64,80},{80,64},{96,112},{112,96},{1... | collective-permute-start | bytes 196616 | tf_op jit(solution)/shard_map/ppermute | solution.py:423
  7.0 3.7 %collective-permute-start.1 = (bf16[256,128]{1,0:T(8,128)(2,1)S(1)}, bf16[256,128]{1,0:T(8,128)(2,1)S(1)}, u32[]{:S(2)}, u32[]{:S(2)}) collective-permute-start(bf16[256,128]{1,0:T(8,128)(2,1)S(1)} %get-tuple-element.60), channel_id=1, source_target_pairs={{0,240},{16,32},{32,16},{48,64},{64,48},{80,96},{96,80},{112,128},... | collective-permute-start | bytes 196616 | tf_op jit(solution)/shard_map/ppermute | solution.py:423
  10.9 4.8 %collective-permute-start.2 = (bf16[256,128]{1,0:T(8,128)(2,1)S(1)}, bf16[256,128]{1,0:T(8,128)(2,1)S(1)}, u32[]{:S(2)}, u32[]{:S(2)}) collective-permute-start(bf16[256,128]{1,0:T(8,128)(2,1)S(1)} %get-tuple-element.65), channel_id=1, source_target_pairs={{0,1},{1,0},{2,3},{3,2},{4,5},{5,4},{6,7},{7,6},{8,9},{9,8},{10,11... | collective-permute-start | bytes 196616 | tf_op jit(solution)/shard_map/ppermute | solution.py:423
  11.0 6.5 %collective-permute-start.3 = (bf16[256,128]{1,0:T(8,128)(2,1)S(1)}, bf16[256,128]{1,0:T(8,128)(2,1)S(1)}, u32[]{:S(2)}, u32[]{:S(2)}) collective-permute-start(bf16[256,128]{1,0:T(8,128)(2,1)S(1)} %get-tuple-element.66), channel_id=1, source_target_pairs={{0,15},{1,2},{2,1},{3,4},{4,3},{5,6},{6,5},{7,8},{8,7},{9,10},{10,... | collective-permute-start | bytes 196616 | tf_op jit(solution)/shard_map/ppermute | solution.py:423
  17.5 7.6 %copy-start.1 = (bf16[3,64,8,128]{3,2,1,0:T(8,128)(2,1)S(1)}, bf16[3,64,8,128]{3,2,1,0:T(8,128)(2,1)}, u32[]{:S(2)}) copy-start(bf16[3,64,8,128]{3,2,1,0:T(8,128)(2,1)} %x_ref.1) | copy-start | bytes 1179652
  19.9 6.4 %collective-permute-start.4 = (bf16[256,128]{1,0:T(8,128)(2,1)S(1)}, bf16[256,128]{1,0:T(8,128)(2,1)S(1)}, u32[]{:S(2)}, u32[]{:S(2)}) collective-permute-start(bf16[256,128]{1,0:T(8,128)(2,1)S(1)} %get-tuple-element.74), channel_id=1, source_target_pairs={{0,16},{16,0},{32,48},{48,32},{64,80},{80,64},{96,112},{112,96},{1... | collective-permute-start | bytes 196616 | tf_op jit(solution)/shard_map/ppermute | solution.py:423
  25.0 4.0 %collective-permute-start.5 = (bf16[256,128]{1,0:T(8,128)(2,1)S(1)}, bf16[256,128]{1,0:T(8,128)(2,1)S(1)}, u32[]{:S(2)}, u32[]{:S(2)}) collective-permute-start(bf16[256,128]{1,0:T(8,128)(2,1)S(1)} %get-tuple-element.75), channel_id=1, source_target_pairs={{0,240},{16,32},{32,16},{48,64},{64,48},{80,96},{96,80},{112,128},... | collective-permute-start | bytes 196616 | tf_op jit(solution)/shard_map/ppermute | solution.py:423
  25.0 10.8 %copy-start.3 = (f32[64,8,128]{2,1,0:T(8,128)S(1)}, f32[64,8,128]{2,1,0:T(8,128)}, u32[]{:S(2)}) copy-start(f32[64,8,128]{2,1,0:T(8,128)} %refs_9_.1) | copy-start | bytes 786436
  29.2 5.3 %collective-permute-start.6 = (bf16[256,128]{1,0:T(8,128)(2,1)S(1)}, bf16[256,128]{1,0:T(8,128)(2,1)S(1)}, u32[]{:S(2)}, u32[]{:S(2)}) collective-permute-start(bf16[256,128]{1,0:T(8,128)(2,1)S(1)} %get-tuple-element.83), channel_id=1, source_target_pairs={{0,1},{1,0},{2,3},{3,2},{4,5},{5,4},{6,7},{7,6},{8,9},{9,8},{10,11... | collective-permute-start | bytes 196616 | tf_op jit(solution)/shard_map/ppermute | solution.py:423
  29.3 6.5 %collective-permute-start.7 = (bf16[256,128]{1,0:T(8,128)(2,1)S(1)}, bf16[256,128]{1,0:T(8,128)(2,1)S(1)}, u32[]{:S(2)}, u32[]{:S(2)}) collective-permute-start(bf16[256,128]{1,0:T(8,128)(2,1)S(1)} %get-tuple-element.84), channel_id=1, source_target_pairs={{0,15},{1,2},{2,1},{3,4},{4,3},{5,6},{6,5},{7,8},{8,7},{9,10},{10,... | collective-permute-start | bytes 196616 | tf_op jit(solution)/shard_map/ppermute | solution.py:423
  38.3 3.5 %collective-permute-start.8 = (bf16[256,128]{1,0:T(8,128)(2,1)S(1)}, bf16[256,128]{1,0:T(8,128)(2,1)S(1)}, u32[]{:S(2)}, u32[]{:S(2)}) collective-permute-start(bf16[256,128]{1,0:T(8,128)(2,1)S(1)} %get-tuple-element.91), channel_id=1, source_target_pairs={{0,16},{16,0},{32,48},{48,32},{64,80},{80,64},{96,112},{112,96},{1... | collective-permute-start | bytes 196616 | tf_op jit(solution)/shard_map/ppermute | solution.py:423
  40.4 4.0 %collective-permute-start.9 = (bf16[256,128]{1,0:T(8,128)(2,1)S(1)}, bf16[256,128]{1,0:T(8,128)(2,1)S(1)}, u32[]{:S(2)}, u32[]{:S(2)}) collective-permute-start(bf16[256,128]{1,0:T(8,128)(2,1)S(1)} %get-tuple-element.92), channel_id=1, source_target_pairs={{0,240},{16,32},{32,16},{48,64},{64,48},{80,96},{96,80},{112,128},... | collective-permute-start | bytes 196616 | tf_op jit(solution)/shard_map/ppermute | solution.py:423
  40.4 9.4 %copy-start.5 = (bf16[64,8,128]{2,1,0:T(8,128)(2,1)S(1)}, bf16[64,8,128]{2,1,0:T(8,128)(2,1)}, u32[]{:S(2)}) copy-start(bf16[64,8,128]{2,1,0:T(8,128)(2,1)} %h_ref.1) | copy-start | bytes 393220
  44.5 6.2 %collective-permute-start.10 = (bf16[256,128]{1,0:T(8,128)(2,1)S(1)}, bf16[256,128]{1,0:T(8,128)(2,1)S(1)}, u32[]{:S(2)}, u32[]{:S(2)}) collective-permute-start(bf16[256,128]{1,0:T(8,128)(2,1)S(1)} %get-tuple-element.103), channel_id=1, source_target_pairs={{0,1},{1,0},{2,3},{3,2},{4,5},{5,4},{6,7},{7,6},{8,9},{9,8},{10,11... | collective-permute-start | bytes 196616 | tf_op jit(solution)/shard_map/ppermute | solution.py:423
  44.6 6.5 %collective-permute-start.11 = (bf16[256,128]{1,0:T(8,128)(2,1)S(1)}, bf16[256,128]{1,0:T(8,128)(2,1)S(1)}, u32[]{:S(2)}, u32[]{:S(2)}) collective-permute-start(bf16[256,128]{1,0:T(8,128)(2,1)S(1)} %get-tuple-element.104), channel_id=1, source_target_pairs={{0,15},{1,2},{2,1},{3,4},{4,3},{5,6},{6,5},{7,8},{8,7},{9,10},{10,... | collective-permute-start | bytes 196616 | tf_op jit(solution)/shard_map/ppermute | solution.py:423
  68.4 17.9 %all-to-all-start.1 = ((f32[16,16,80]{2,1,0:T(8,128)}), f32[16,16,80]{2,1,0:T(8,128)S(1)}, u32[]{:S(2)}, u32[]{:S(2)}) async-start(f32[16,16,80]{2,1,0:T(8,128)} %bitcast.2), calls=%async_computation.1 | async-start | bytes 262144 | tf_op jit(solution)/shard_map/all_to_all | solution.py:517

commit v3 on v2

--- a/solution.py
+++ b/solution.py
@@ -42,10 +42,6 @@
     return pl.BlockSpec(memory_space=pltpu.VMEM)
 
 
-def at_step(step, shape):
-    return pl.BlockSpec((1,) + shape, lambda i: (step,) + (0,) * len(shape))
-
-
 def in_hbm(x):
     return x if INTERPRET else pltpu.with_memory_space_constraint(x, pltpu.MemorySpace.HBM)
 
@@ -85,6 +81,20 @@
     return df
 
 
+def by_parity(par, top, bottom, p0_ref, p1_ref, start):
+    rows = slice(start, start + top.shape[0])
+
+    @pl.when(par == 0)
+    def _():
+        p0_ref[rows, :] = bottom
+        p1_ref[rows, :] = top
+
+    @pl.when(par == 1)
+    def _():
+        p0_ref[rows, :] = top
+        p1_ref[rows, :] = bottom
+
+
 def emit_grads(scr, a_ref, p0_ref, p1_ref, ql_ref, qr_ref):
     par = parity("row")
     step = 32
@@ -103,50 +113,38 @@
     top = a_ref[:, 0:LANES]
     bottom = a_ref[:, (ROWS - 1) * LANES :]
 
-    @pl.when(par == 0)
-    def _():
-        p0_ref[...] = bottom
-        p1_ref[...] = top
-
-    @pl.when(par == 1)
-    def _():
-        p0_ref[...] = top
-        p1_ref[...] = bottom
-
-
-def forward_kernel(pre_hbm, cot_hbm, c0_hbm, mask_hbm, c1_ref, c2_ref, h1_ref, h2_ref, dc_ref, a_ref, p0_ref, p1_ref, ql_ref, qr_ref, scr, pre_ref, cot_ref, c0_ref, mask_ref, sems):
-    copies = [
-        pltpu.make_async_copy(src, dst, sems.at[n])
-        for n, (src, dst) in enumerate(
-            [(c0_hbm, c0_ref), (mask_hbm, mask_ref)]
-            + [(pre_hbm.at[t], pre_ref.at[t]) for t in range(3)]
-            + [(cot_hbm.at[2], cot_ref)]
-        )
-    ]
-    for copy in (copies[2], copies[0], copies[1], copies[3], copies[4], copies[5]):
-        copy.start()
+    by_parity(par, top, bottom, p0_ref, p1_ref, 0)
+
+
+def forward_kernel(pre_hbm, cot_hbm, c0_hbm, mask_hbm, c1_ref, c2_ref, dc_ref, a_ref, p0_ref, p1_ref, ql_ref, qr_ref, scr, pre_ref, cot_ref, c0_ref, mask_ref, sems):
+    pairs = [(c0_hbm, c0_ref), (mask_hbm, mask_ref), (cot_hbm.at[2], cot_ref)]
+    for t, g in ((0, 1), (0, 0), (0, 3), (1, 1), (1, 0), (1, 3), (2, 1), (2, 0), (2, 3), (2, 2)):
+        own = pl.ds(g * CH, CH)
+        pairs.append((pre_hbm.at[t, own], pre_ref.at[t, own]))
+    copies = [pltpu.make_async_copy(src, dst, sems.at[n]) for n, (src, dst) in enumerate(pairs)]
+    order = [3, 4, 0, 5, 6, 7, 8, 9, 10, 11, 12, 2, 1]
+    for n in order:
+        copies[n].start()
     step = 4
 
     def gate(t, g, base):
         return pre_ref[t, pl.ds(g * CH + base, step)].astype(F32)
 
     copies[0].wait()
-    copies[1].wait()
-    mask = mask_ref[...].astype(F32)[None]
-    for t, (before_ref, c_ref, h_ref) in enumerate(((c0_ref, c1_ref, h1_ref), (c1_ref, c2_ref, h2_ref))):
-        copies[2 + t].wait()
+    for t, (before_ref, c_ref) in enumerate(((c0_ref, c1_ref), (c1_ref, c2_ref))):
+        for n in range(3 + 3 * t, 6 + 3 * t):
+            copies[n].wait()
 
         def advance(j, carry):
             base = j * step
             own = pl.ds(base, step)
-            cell = sigmoid(gate(t, 1, base)) * before_ref[own] + sigmoid(gate(t, 0, base)) * jnp.tanh(gate(t, 3, base))
-            c_ref[own] = cell
-            h_ref[own] = (mask * sigmoid(gate(t, 2, base)) * jnp.tanh(cell)).astype(BF16)
+            c_ref[own] = sigmoid(gate(t, 1, base)) * before_ref[own] + sigmoid(gate(t, 0, base)) * jnp.tanh(gate(t, 3, base))
             return carry
 
         lax.fori_loop(0, CH // step, advance, 0)
-    copies[4].wait()
-    copies[5].wait()
+    for n in (9, 10, 11, 12, 2, 1):
+        copies[n].wait()
+    mask = mask_ref[...].astype(F32)[None]
 
     def chunk(j, carry):
         base = j * step
@@ -164,6 +162,20 @@
     emit_grads(scr, a_ref, p0_ref, p1_ref, ql_ref, qr_ref)
 
 
+def hidden_kernel(pre_ref, c1_ref, c2_ref, mask_ref, h1_ref, h2_ref):
+    step = 4
+    mask = mask_ref[...].astype(F32)[None]
+    for t, (c_ref, h_ref) in enumerate(((c1_ref, h1_ref), (c2_ref, h2_ref))):
+
+        def chunk(j, carry):
+            own = pl.ds(j * step, step)
+            gout = sigmoid(pre_ref[t, pl.ds(2 * CH + j * step, step)].astype(F32))
+            h_ref[own] = (mask * gout * jnp.tanh(c_ref[own])).astype(BF16)
+            return carry
+
+        lax.fori_loop(0, CH // step, chunk, 0)
+
+
 def weights_kernel(k_ref, w_ref):
     for u in range(3):
         for v in range(3):
@@ -180,7 +192,10 @@
     return above, below
 
 
-def corner_kernel(r0_ref, r1_ref, ql_ref, qr_ref, c0_ref, c1_ref):
+ZLANE = 16
+
+
+def corner_kernel(with_z, r0_ref, r1_ref, ql_ref, qr_ref, c0_ref, c1_ref):
     par = parity("col").astype(F32)
     step = 32
     lanes = lane_ids(step)
@@ -191,8 +206,43 @@
         left = jnp.where(lanes == SLABS - 1, pltpu.roll(below, SLABS - 1, 1), left)
         right = jnp.where(lanes == 0, pltpu.roll(above, 1, 1), qr_ref[own, :].astype(F32))
         right = jnp.where(lanes == SLABS - 1, pltpu.roll(below, SLABS, 1), right)
+        if with_z and k < W // step:
+            above, below = halo_rows(r0_ref, r1_ref, pl.ds(Q + k * step, step))
+            far = ZLANE + SLABS - 1
+            left = jnp.where(lanes == ZLANE, pltpu.roll(above, ZLANE, 1), left)
+            left = jnp.where(lanes == far, pltpu.roll(below, far, 1), left)
+            right = jnp.where(lanes == ZLANE, pltpu.roll(above, ZLANE + 1, 1), right)
+            right = jnp.where(lanes == far, pltpu.roll(below, far + 1, 1), right)
         c0_ref[own, :] = (right * (1.0 - par) + left * par).astype(BF16)
         c1_ref[own, :] = (left * (1.0 - par) + right * par).astype(BF16)
+
+
+def halo_columns(c0_ref, c1_ref, own):
+    par = parity("col").astype(F32)
+    low, high = edge_flags("col")
+    first, second = c0_ref[own, :].astype(F32), c1_ref[own, :].astype(F32)
+    left = second * ((1.0 - par) * low) + first * (par * low)
+    right = first * ((1.0 - par) * high) + second * (par * high)
+    return left, right
+
+
+def z_edges_kernel(x_ref, h_ref, p0_ref, p1_ref, zl_ref, zr_ref, tmp):
+    stack_fields(0, x_ref, h_ref, tmp)
+    top = tmp[pl.ds(0, W, stride=ROWS), :].astype(BF16)
+    bottom = tmp[pl.ds(ROWS - 1, W, stride=ROWS), :].astype(BF16)
+    by_parity(parity("row"), top, bottom, p0_ref, p1_ref, 0)
+    step = 32
+    lanes = lane_ids(step)
+    for k in range(W // step):
+        zl = jnp.zeros((step, LANES), F32)
+        zr = jnp.zeros((step, LANES), F32)
+        for r in range(ROWS):
+            row = tmp[pl.ds(k * step * ROWS + r, step, stride=ROWS), :]
+            lane = ZLANE + r + 1
+            zl = jnp.where(lanes == lane, pltpu.roll(row, lane, 1), zl)
+            zr = jnp.where(lanes == lane, pltpu.roll(row, lane + 1, 1), zr)
+        zl_ref[pl.ds(k * step, step), :] = zl.astype(BF16)
+        zr_ref[pl.ds(k * step, step), :] = zr.astype(BF16)
 
 
 def interior_kernel(a_ref, w_ref, b_ref, y_ref, y3):
@@ -219,8 +269,6 @@
 
 
 def build_halo(r0_ref, r1_ref, c0_ref, c1_ref, b_ref):
-    par = parity("col").astype(F32)
-    low, high = edge_flags("col")
     step = 32
     lanes = lane_ids(step)
     inside = (lanes >= 1) & (lanes <= ROWS)
@@ -228,9 +276,7 @@
     for k in range(Q // step):
         own = pl.ds(k * step, step)
         above, below = halo_rows(r0_ref, r1_ref, own)
-        first, second = c0_ref[own, :].astype(F32), c1_ref[own, :].astype(F32)
-        left = second * ((1.0 - par) * low) + first * (par * low)
-        right = first * ((1.0 - par) * high) + second * (par * high)
+        left, right = halo_columns(c0_ref, c1_ref, own)
         for n, (row, s) in enumerate(((above, 0), (below, last))):
             span = slice(n * LANES, (n + 1) * LANES)
             minus = jnp.where(lanes == LANES - 1, pltpu.roll(right, LANES - 1 - s, 1), pltpu.roll(row, LANES - 1, 1))
@@ -264,9 +310,9 @@
             scr[pl.ds(k * step * ROWS + r, step, stride=ROWS), :] = total + left
 
 
-def backward_kernel(has_gi, *refs):
-    if has_gi:
-        refs = refs[1:]
+def backward_kernel(t, with_z, *refs):
+    edges = refs[:4] if with_z else None
+    refs = refs[4:] if with_z else refs
     (r0_ref, r1_ref, k0_ref, k1_ref, w_ref, y_ref, pre_ref, cot_ref, before_ref, cell_ref, mask_ref, dc_in,
      gi_ref, b_ref, dc_ref, a_ref, p0_ref, p1_ref, ql_ref, qr_ref, y3, yscr, scr) = refs
     build_halo(r0_ref, r1_ref, k0_ref, k1_ref, b_ref)
@@ -279,25 +325,34 @@
         own = pl.ds(base, step)
 
         def gate(g):
-            return pre_ref[0, pl.ds(g * CH + base, step)].astype(F32)
-
-        gi_ref[0, own] = yscr[pl.ds(base * ROWS, step * ROWS), :].reshape(step, ROWS, LANES).astype(BF16)
+            return pre_ref[t, pl.ds(g * CH + base, step)].astype(F32)
+
+        gi_ref[own] = yscr[pl.ds(base * ROWS, step * ROWS), :].reshape(step, ROWS, LANES).astype(BF16)
         dh = yscr[pl.ds((CH + base) * ROWS, step * ROWS), :].reshape(step, ROWS, LANES)
         pre = (sigmoid(gate(0)), sigmoid(gate(1)), sigmoid(gate(2)), jnp.tanh(gate(3)))
         part = [None] * 4
-        dc_ref[own] = gate_grads(pre, part, cot_ref[0, own].astype(F32), dh, mask, before_ref[own], jnp.tanh(cell_ref[own]), dc_in[own])
+        dc_ref[own] = gate_grads(pre, part, cot_ref[t, own].astype(F32), dh, mask, before_ref[own], jnp.tanh(cell_ref[own]), dc_in[own])
         for g in range(4):
             scr[pl.ds((g * CH + base) * ROWS, step * ROWS), :] = part[g].reshape(step * ROWS, LANES)
         return carry
 
     lax.fori_loop(0, CH // step, chunk, 0)
     emit_grads(scr, a_ref, p0_ref, p1_ref, ql_ref, qr_ref)
-
-
-def last_kernel(gi_in, w_ref, y_ref, b_ref, gi_ref, dh_ref, y3, yscr):
-    del gi_in
+    if with_z:
+        z0_ref, z1_ref, zl_ref, zr_ref = edges
+        p0_ref[Q:, :] = z0_ref[...]
+        p1_ref[Q:, :] = z1_ref[...]
+        ql_ref[0:W, :] = (ql_ref[0:W, :].astype(F32) + zl_ref[...].astype(F32)).astype(BF16)
+        qr_ref[0:W, :] = (qr_ref[0:W, :].astype(F32) + zr_ref[...].astype(F32)).astype(BF16)
+
+
+def last_kernel(gi1_ref, gi2_ref, dc_ref, r0_ref, r1_ref, k0_ref, k1_ref, w_ref, y_ref, gi_ref, dh_ref, cell_ref, b_ref, y3, yscr):
+    build_halo(r0_ref, r1_ref, k0_ref, k1_ref, b_ref)
     finish_y(w_ref, b_ref, y_ref, y3, yscr)
     gi_ref[0] = yscr[0 : CH * ROWS, :].reshape(CH, ROWS, LANES).astype(BF16)
+    gi_ref[1] = gi1_ref[...]
+    gi_ref[2] = gi2_ref[...]
+    cell_ref[...] = dc_ref[...]
     dh_ref[...] = yscr[CH * ROWS :, :].reshape(CH, ROWS, LANES)
 
 
@@ -306,8 +361,8 @@
 CONTRACT_LANES = (((1,), (1,)), ((), ()))
 
 
-def stack_fields(x_ref, h_ref, tmp):
-    tmp[0 : CH * ROWS, :] = x_ref[0].astype(F32).reshape(CH * ROWS, LANES)
+def stack_fields(t, x_ref, h_ref, tmp):
+    tmp[0 : CH * ROWS, :] = x_ref[t].astype(F32).reshape(CH * ROWS, LANES)
     tmp[CH * ROWS :, :] = h_ref[...].astype(F32).reshape(CH * ROWS, LANES)
 
 
@@ -358,12 +413,12 @@
     yield from taps(zh, b_ref, False)
 
 
-def accumulate_kernel(has_acc, with_halo, *refs):
+def accumulate_kernel(t, has_acc, with_halo, *refs):
     refs = list(refs)
     acc_ref = refs.pop(0) if has_acc else None
     x_ref, h_ref, b_ref = refs[:3]
     out_ref, z3, zh, tmp = refs[-4:]
-    stack_fields(x_ref, h_ref, tmp)
+    stack_fields(t, x_ref, h_ref, tmp)
     for tap, got in interior_taps(tmp, b_ref, z3):
         rows = slice(tap * W, tap * W + got.shape[0])
         out_ref[rows, :] = acc_ref[rows, :] + got if has_acc else got
@@ -373,20 +428,51 @@
             out_ref[rows, :] += got
 
 
-def send_kernel(blocks, scale, acc_ref, x_ref, h_ref, r0_ref, r1_ref, k0_ref, k1_ref, out_ref, b_ref, zh, tmp, total):
-    build_halo(r0_ref, r1_ref, k0_ref, k1_ref, b_ref)
-    stack_fields(x_ref, h_ref, tmp)
+def z_windows(tmp, r0_ref, r1_ref, k0_ref, k1_ref, zw):
+    step = 32
+    lanes = lane_ids(step)
+    for k in range(W // step):
+        above, below = halo_rows(r0_ref, r1_ref, pl.ds(Q + k * step, step))
+        left, right = halo_columns(k0_ref, k1_ref, pl.ds(k * step, step))
+        for source in range(-1, ROWS + 1):
+            if source < 0:
+                row = above
+            elif source == ROWS:
+                row = below
+            else:
+                row = tmp[pl.ds(k * step * ROWS + source, step, stride=ROWS), :]
+            lane = ZLANE + source + 1
+            shifted = (
+                jnp.where(lanes == 0, pltpu.roll(left, LANES - lane, 1), pltpu.roll(row, 1, 1)),
+                row,
+                jnp.where(lanes == LANES - 1, pltpu.roll(right, LANES - 1 - lane, 1), pltpu.roll(row, LANES - 1, 1)),
+            )
+            for v in range(3):
+                block = shifted[v].astype(BF16)
+                for u in range(3):
+                    r = source - (u - 1)
+                    if 0 <= r < ROWS:
+                        zw[pl.ds((3 * u + v) * W + k * step, step), r * LANES : (r + 1) * LANES] = block
+    ids = lax.broadcasted_iota(jnp.int32, (16, CELLS), 0)
+    zw[9 * W :, :] = jnp.where(ids == 0, 1.0, 0.0).astype(BF16)
+
+
+def send_kernel(blocks, scale, acc_ref, x_ref, h2_ref, b_ref, h_ref, r0_ref, r1_ref, k0_ref, k1_ref, a_ref, out_ref, zh, zw, tmp, total):
+    stack_fields(0, x_ref, h_ref, tmp)
+    z_windows(tmp, r0_ref, r1_ref, k0_ref, k1_ref, zw)
+    total[...] = acc_ref[...] + lax.dot_general(zw[...], a_ref[...], CONTRACT_LANES, preferred_element_type=F32)
+    stack_fields(1, x_ref, h2_ref, tmp)
     for tap, got in halo_taps(tmp, b_ref, zh):
         rows = slice(tap * W, tap * W + got.shape[0])
-        total[rows, :] = (acc_ref[rows, :] + got) * scale
-    bias = acc_ref[9 * W : 9 * W + 8, :] * scale
+        total[rows, :] += got
+    bias = total[9 * W : 9 * W + 8, :] * scale
     high = jnp.broadcast_to(bias[0:1], (8, Q)).astype(BF16).astype(F32)
     low = jnp.broadcast_to(bias[0:1], (8, Q)) - high
     ids = lax.broadcasted_iota(jnp.int32, (8, Q), 0)
     tail = jnp.where(ids == 0, high, jnp.where(ids == 1, low, 0.0))
     size = 9 * W // blocks
     for c in range(blocks):
-        body = jnp.concatenate([total[c * size : (c + 1) * size, :], tail], axis=0)
+        body = jnp.concatenate([total[c * size : (c + 1) * size, :] * scale, tail], axis=0)
         out_ref[c * (size + 8) : (c + 1) * (size + 8), :] = body.astype(BF16)
 
 
@@ -439,91 +525,103 @@
     z3, zh = pltpu.VMEM((ZROWS, CELLS), BF16), pltpu.VMEM((3 * W, 3 * LANES), BF16)
     hbm = pl.BlockSpec(memory_space=pltpu.MemorySpace.HBM)
 
-    c1, c2, h1, h2, dc, a, p0, p1, ql, qr = call(
+    c1, c2, dc, a, p0, p1, ql, qr = call(
         forward_kernel,
-        (struct(field, F32), struct(field, F32), struct(field, BF16), struct(field, BF16), struct(field, F32)) + grads_out,
+        (struct(field, F32), struct(field, F32), struct(field, F32)) + grads_out,
         in_specs=[hbm] * 4,
-        out_specs=[whole()] * 10,
+        out_specs=[whole()] * 8,
         scratch=[
             scr,
             pltpu.VMEM((3, Q, ROWS, LANES), BF16),
             pltpu.VMEM(field, BF16),
             pltpu.VMEM(field, F32),
             pltpu.VMEM((ROWS, LANES), jnp.int32),
-            pltpu.SemaphoreType.DMA((6,)),
+            pltpu.SemaphoreType.DMA((13,)),
         ],
     )(*(in_hbm(x) for x in (gate_pre, cotangent, cell_init, land_mask)))
 
+    h1, h2 = call(hidden_kernel, (struct(field, BF16),) * 2, in_specs=[whole()] * 4, out_specs=[whole()] * 2)(gate_pre, c1, c2, land_mask)
     cells = [cell_init, c1, c2]
     hiddens = [hidden_init, h1, h2]
-    gi_shape = struct((3,) + field, BF16)
     interior, halo = struct((3 * Q, CELLS), BF16), struct((3 * Q, 3 * LANES), BF16)
-    acc_shape = struct((ZROWS + 6 * W, Q), F32)
-
-    def accumulate(t, acc, b, bh):
-        head = [] if acc is None else [acc]
-        rest = [b] if bh is None else [b, bh]
+    acc_shape = struct((9 * W + 16, Q), F32)
+
+    def corner(with_z, r0, r1, ql, qr):
+        out = call(functools.partial(corner_kernel, with_z), (edge, edge), in_specs=[whole()] * 4, out_specs=[whole()] * 2)
+        return out(r0, r1, ql, qr)
+
+    def inside(a):
         return call(
-            functools.partial(accumulate_kernel, acc is not None, bh is not None),
-            acc_shape,
-            in_specs=[whole()] * len(head) + [at_step(t, field)] + [whole()] * (1 + len(rest)),
-            out_specs=whole(),
-            scratch=[z3, zh, tmp],
-            aliases={0: 0} if head else {},
-        )(*head, inputs, hiddens[t], *rest)
-
-    gi = acc = weights = b = bh = None
-    for t in (2, 1, 0):
-        r0, r1 = swaps(p0, p1, "row")
-        if t == 2:
-            weights = call(weights_kernel, struct((3 * W, 3 * Q), BF16), in_specs=[whole()], out_specs=whole())(kernel)
-            r0, r1, weights = lax.optimization_barrier((r0, r1, weights))
-        else:
-            acc = accumulate(t + 1, acc, b, bh)
-            r0, r1, acc = lax.optimization_barrier((r0, r1, acc))
-        k0, k1 = call(corner_kernel, (edge, edge), in_specs=[whole()] * 4, out_specs=[whole()] * 2)(r0, r1, ql, qr)
-        k0, k1 = swaps(k0, k1, "col")
-        b, y = call(
             interior_kernel,
             (interior, struct((W, CELLS), F32)),
             in_specs=[whole()] * 2,
             out_specs=[whole()] * 2,
             scratch=[pltpu.VMEM((3 * W, CELLS), F32)],
         )(a, weights)
-        if t > 0:
-            head = [] if gi is None else [gi]
-            gi, bh, dc, a, p0, p1, ql, qr = call(
-                functools.partial(backward_kernel, gi is not None),
-                (gi_shape, halo, struct(field, F32)) + grads_out,
-                in_specs=[pl.BlockSpec(memory_space=pl.ANY)] * len(head)
-                + [whole()] * 6
-                + [at_step(t - 1, (Q, ROWS, LANES)), at_step(t - 1, field)]
-                + [whole()] * 4,
-                out_specs=[at_step(t, field)] + [whole()] * 7,
-                scratch=[y3, tmp, scr],
-                aliases={0: 0} if head else {},
-            )(*head, r0, r1, k0, k1, weights, y, gate_pre, cotangent, cells[t - 1], cells[t], land_mask, dc)
-    acc = accumulate(0, acc, b, None)
+
+    def backward(t, edges, r0, r1, k0, k1, y, dc):
+        pay = struct((Q + W, LANES), BF16) if edges else edge
+        return call(
+            functools.partial(backward_kernel, t - 1, bool(edges)),
+            (struct(field, BF16), halo, struct(field, F32), struct((Q, CELLS), BF16), pay, pay, edge, edge),
+            in_specs=[whole()] * (len(edges) + 12),
+            out_specs=[whole()] * 8,
+            scratch=[y3, tmp, scr],
+        )(*edges, r0, r1, k0, k1, weights, y, gate_pre, cotangent, cells[t - 1], cells[t], land_mask, dc)
+
+    def accumulate(t, acc, b, bh):
+        head = [] if acc is None else [acc]
+        rest = [b] if bh is None else [b, bh]
+        return call(
+            functools.partial(accumulate_kernel, t, acc is not None, bh is not None),
+            acc_shape,
+            in_specs=[whole()] * (len(head) + 2 + len(rest)),
+            out_specs=whole(),
+            scratch=[z3, zh, tmp],
+            aliases={0: 0} if head else {},
+        )(*head, inputs, hiddens[t], *rest)
+
+    r0, r1 = swaps(p0, p1, "row")
+    weights = call(weights_kernel, struct((3 * W, 3 * Q), BF16), in_specs=[whole()], out_specs=whole())(kernel)
+    zedge = struct((W, LANES), BF16)
+    edges = call(
+        z_edges_kernel, (zedge,) * 4, in_specs=[whole()] * 2, out_specs=[whole()] * 4, scratch=[tmp]
+    )(inputs, hidden_init)
+    r0, r1, weights, edges = lax.optimization_barrier((r0, r1, weights, edges))
+    k0, k1 = swaps(*corner(False, r0, r1, ql, qr), "col")
+    b, y = inside(a)
+    gi2, bh, dc, a, p0, p1, ql, qr = backward(2, edges, r0, r1, k0, k1, y, dc)
+    r0, r1 = swaps(p0, p1, "row")
+    acc = accumulate(2, None, b, bh)
+    r0, r1, acc = lax.optimization_barrier((r0, r1, acc))
+    k0, k1 = swaps(*corner(True, r0, r1, ql, qr), "col")
+    b, y = inside(a)
+    acc = accumulate(1, acc, b, None)
+    gi1, bh, dc, a, p0, p1, ql, qr = backward(1, [], r0, r1, k0, k1, y, dc)
     size = 9 * W // ncol + 8
-    send, bh = call(
+    send = call(
         functools.partial(send_kernel, ncol, scale),
-        (struct((ncol * size, Q), BF16), halo),
-        in_specs=[whole(), at_step(0, field)] + [whole()] * 5,
-        out_specs=[whole()] * 2,
-        scratch=[zh, tmp, pltpu.VMEM((9 * W, Q), F32)],
-    )(acc, inputs, hiddens[0], r0, r1, k0, k1)
+        struct((ncol * size, Q), BF16),
+        in_specs=[whole()] * 10,
+        out_specs=whole(),
+        scratch=[zh, pltpu.VMEM((9 * W + 16, CELLS), BF16), tmp, pltpu.VMEM((9 * W + 16, Q), F32)],
+    )(acc, inputs, hiddens[1], bh, hiddens[0], r0, r1, k0, k1, a)
+    r0, r1 = swaps(p0, p1, "row")
     got = lax.all_to_all(send, "col", 0, 0, tiled=True)
+    c0, c1 = corner(False, r0, r1, ql, qr)
+    k0, k1 = swaps(c0, c1, "col")
+    b, y = inside(a)
+    got, c0, y = lax.optimization_barrier((got, c0, y))
     folded = call(functools.partial(fold_kernel, ncol), struct((Q, size), F32), in_specs=[whole()], out_specs=whole())(got)
     got = lax.all_to_all(folded, "row", 0, 0, tiled=True)
     y, folded = lax.optimization_barrier((y, folded))
-    gi, grad_hidden = call(
+    gi, grad_hidden, grad_cell = call(
         last_kernel,
-        (gi_shape, struct(field, F32)),
-        in_specs=[pl.BlockSpec(memory_space=pl.ANY)] + [whole()] * 3,
-        out_specs=[at_step(0, field), whole()],
-        scratch=[y3, tmp],
-        aliases={0: 0},
-    )(gi, weights, y, bh)
+        (struct((3,) + field, BF16), struct(field, F32), struct(field, F32)),
+        in_specs=[whole()] * 9,
+        out_specs=[whole()] * 3,
+        scratch=[pltpu.VMEM((3 * Q, 3 * LANES), BF16), y3, tmp],
+    )(gi1, gi2, dc, r0, r1, k0, k1, weights, y)
     count = Q // nrow // ncol
     grad_kernel, grad_bias = call(
         functools.partial(result_kernel, nrow),
@@ -532,7 +630,7 @@
         out_specs=[whole()] * 2,
         scratch=[pltpu.VMEM((Q // nrow, LANES), F32)],
     )(got)
-    return (gi, grad_hidden, dc, grad_kernel, grad_bias.reshape(count))
+    return (gi, grad_hidden, grad_cell, grad_kernel, grad_bias.reshape(count))
 
 
 def solution(mesh):

time: 87.2 us -> 75.3 us (0.86)
  blocking collectives: 15.6 us -> 0 us
  starting transfers between devices: 31.8 us -> 34.9 us
    all_to_all x1 -> x0, blocking collectives: 15.6 us -> none  [shards(): got = lax.all_to_all(send, 'col', 0, 0, tiled=True)]
    all_to_all x1, waiting for transfers between devices: 7.36 us -> 0.33 us  [shards(): got = lax.all_to_all(folded, 'row', 0, 0, tiled=True)]
    all_to_all x0 -> x1, starting transfers between devices: none -> 5.48 us  [shards(): got = lax.all_to_all(send, 'col', 0, 0, tiled=True)]
    ppermute x6, waiting for transfers between devices: 11.7 us -> 15.7 us  [swaps(): lax.ppermute(second, axis, odd_swap(count))]
    all_to_all x0 -> x1, waiting for transfers between devices: none -> 3.48 us  [shards(): got = lax.all_to_all(send, 'col', 0, 0, tiled=True)]
    ppermute x6, starting transfers between devices: 12 us -> 8.94 us  [swaps(): lax.ppermute(second, axis, odd_swap(count))]
    pallas_call x13 -> x14, Pallas kernels: 14.2 us -> 14.8 us  [the longest x3 3.79 us: inside(): call(interior_kernel, (interior, struct((W, CELLS), F32)), in_specs=[whol...]
  transfers between devices with their start and end apart: 13 -> 14, of which waited for: 8 -> 9; matrix products, arithmetic and copies ran while one was open for 0% -> 0% of each run, Pallas kernels for 9% -> 12%
where the time goes in v3:
time: 75.3 us; the launch traced here: 75 us
  starting transfers between devices  34.9 us (46%)
  waiting for transfers between devices  19.9 us (26%)
  Pallas kernels  19.4 us (26%)
  between operations  0.86 us (1%)
    ppermute x6, waiting for transfers between devices, swaps(): lax.ppermute(second, axis, odd_swap(count))  15.7 us
    ppermute x6, starting transfers between devices, swaps(): lax.ppermute(first, axis, even_swap(count))  11.2 us
    all_to_all x1, starting transfers between devices, shards(): got = lax.all_to_all(folded, 'row', 0, 0, tiled=True)  9.23 us
    ppermute x6, starting transfers between devices, swaps(): lax.ppermute(second, axis, odd_swap(count))  8.94 us
    all_to_all x1, starting transfers between devices, shards(): got = lax.all_to_all(send, 'col', 0, 0, tiled=True)  5.48 us
    pallas_call x3, Pallas kernels, inside(): call(interior_kernel, (interior, struct((W, CELLS), F32)), in_specs=[whol...  3.79 us
    pallas_call x2, Pallas kernels, backward(): call(functools.partial(backward_kernel, t - 1, bool(edges)), (struct(fiel...  3.52 us
    all_to_all x1, waiting for transfers between devices, shards(): got = lax.all_to_all(send, 'col', 0, 0, tiled=True)  3.48 us
  transfers between devices with their start and end apart: 14, of which 9 were waited for; matrix products, arithmetic and copies ran while one was open for 0% of the time, Pallas kernels for 12%

profile of v3, /device:TPU:1, one launch (start us, length us, event | category | flops | bytes accessed | tf_op | source)
XLA Modules:
  0.0 75.0 jit_solution(5577964119885733485)
XLA Ops:
  0.7 2.9 %shard_map.110 = (f32[64,8,128]{2,1,0:T(8,128)S(1)}, f32[64,8,128]{2,1,0:T(8,128)S(1)}, f32[64,8,128]{2,1,0:T(8,128)S(1)}, bf16[256,1024]{1,0:T(8,128)(2,1)S(1)}...) custom-call(bf16[3,256,8,128]{3,2,1,0:T(8,128)(2,1)} %refs_6_.1, ...), custom_call_target="tpu_custom_call" | custom-call | tf_op jit(solution)/shard_map/pallas_call | solution.py:528
  3.6 3.3 %collective-permute-start = (bf16[256,128]{1,0:T(8,128)(2,1)S(1)}, bf16[256,128]{1,0:T(8,128)(2,1)S(1)}, u32[]{:S(2)}, u32[]{:S(2)}) collective-permute-start(bf16[256,128]{1,0:T(8,128)(2,1)S(1)} %get-tuple-element.64), channel_id=1, source_target_pairs={{0,16},{16,0},{32,48},{48,32},{64,80},{80,64},{96,112},{112,96},{1... | collective-permute-start | bytes 196616 | tf_op jit(solution)/shard_map/ppermute | solution.py:509
  7.1 0.3 shard_map.112
  7.4 0.4 collective-permute-done.r0_ref.refs_4_
  7.8 2.8 %collective-permute-done.1.r1_ref.refs_5_ = bf16[256,128]{1,0:T(8,128)(2,1)S(1)} collective-permute-done((bf16[256,128]{1,0:T(8,128)(2,1)S(1)}, bf16[256,128]{1,0:T(8,128)(2,1)S(1)}, u32[]{:S(2)}, u32[]{:S(2)}) %collective-permute-start.1) | collective-permute-done | bytes 65568 | tf_op jit(solution)/shard_map/ppermute | solution.py:509
  10.8 3.7 %collective-permute-start.3 = (bf16[256,128]{1,0:T(8,128)(2,1)S(1)}, bf16[256,128]{1,0:T(8,128)(2,1)S(1)}, u32[]{:S(2)}, u32[]{:S(2)}) collective-permute-start(bf16[256,128]{1,0:T(8,128)(2,1)S(1)} %get-tuple-element.79), channel_id=1, source_target_pairs={{0,15},{1,2},{2,1},{3,4},{4,3},{5,6},{6,5},{7,8},{8,7},{9,10},{10,... | collective-permute-start | bytes 196616 | tf_op jit(solution)/shard_map/ppermute | solution.py:509
  14.5 1.0 %shard_map.114 = (bf16[768,1024]{1,0:T(8,128)(2,1)S(1)}, f32[128,1024]{1,0:T(8,128)S(1)}) custom-call(bf16[256,1024]{1,0:T(8,128)(2,1)S(1)} %get-tuple-element.81.a_ref, bf16[384,768]{1,0:T(8,128)(2,1)S(1)} %shard_map.111.w_ref.refs_8_.refs_4_), custom_call_target="tpu_custom_call" | custom-call | tf_op jit(solution)/shard_map/pallas_call | solution.py:554
  15.5 1.9 %collective-permute-done.3.refs_7_ = bf16[256,128]{1,0:T(8,128)(2,1)S(1)} collective-permute-done((bf16[256,128]{1,0:T(8,128)(2,1)S(1)}, bf16[256,128]{1,0:T(8,128)(2,1)S(1)}, u32[]{:S(2)}, u32[]{:S(2)}) %collective-permute-start.3) | collective-permute-done | bytes 65568 | tf_op jit(solution)/shard_map/ppermute | solution.py:509
  17.4 1.8 %shard_map.115 = (bf16[64,8,128]{2,1,0:T(8,128)(2,1)S(1)}, bf16[768,384]{1,0:T(8,128)(2,1)S(1)}, f32[64,8,128]{2,1,0:T(8,128)S(1)}, bf16[256,1024]{1,0:T(8,128)(...) custom-call(bf16[128,128]{1,0:T(8,128)(2,1)S(1)} %get-tuple-element., ...), custom_call_target="tpu_custom_call" | custom-call | tf_op jit(solution)/shard_map/pallas_call | solution.py:564
  19.1 5.2 %collective-permute-start.4 = (bf16[384,128]{1,0:T(8,128)(2,1)S(1)}, bf16[384,128]{1,0:T(8,128)(2,1)S(1)}, u32[]{:S(2)}, u32[]{:S(2)}) collective-permute-start(bf16[384,128]{1,0:T(8,128)(2,1)S(1)} %get-tuple-element.86), channel_id=1, source_target_pairs={{0,16},{16,0},{32,48},{48,32},{64,80},{80,64},{96,112},{112,96},{1... | collective-permute-start | bytes 294920 | tf_op jit(solution)/shard_map/ppermute | solution.py:509
  24.4 0.5 shard_map.116
  24.9 1.2 %shard_map.117.refs_0_ = f32[1168,256]{1,0:T(8,128)S(1)} custom-call(bf16[3,64,8,128]{3,2,1,0:T(8,128)(2,1)S(1)} %copy-done.1, bf16[64,8,128]{2,1,0:T(8,128)(2,1)S(1)} %get-tuple-element.88.refs_1_, bf16[768,1024]{1,0:T(8,128)(2,1)S(1)} %get-tuple-element.89.refs_2_, bf16[768,384]{1,0:T(8,128)(2,1)S(1)} %get-tuple-element.90.refs_3_), custom_call_target="tpu_custom_call" | custom-call | tf_op jit(solution)/shard_map/pallas_call | solution.py:575
  26.1 2.6 %collective-permute-done.5.r1_ref.refs_1_ = bf16[384,128]{1,0:T(8,128)(2,1)S(1)} collective-permute-done((bf16[384,128]{1,0:T(8,128)(2,1)S(1)}, bf16[384,128]{1,0:T(8,128)(2,1)S(1)}, u32[]{:S(2)}, u32[]{:S(2)}) %collective-permute-start.5) | collective-permute-done | bytes 98336 | tf_op jit(solution)/shard_map/ppermute | solution.py:509
  28.7 0.2 shard_map.118
  29.1 4.4 %collective-permute-start.7 = (bf16[256,128]{1,0:T(8,128)(2,1)S(1)}, bf16[256,128]{1,0:T(8,128)(2,1)S(1)}, u32[]{:S(2)}, u32[]{:S(2)}) collective-permute-start(bf16[256,128]{1,0:T(8,128)(2,1)S(1)} %get-tuple-element.96), channel_id=1, source_target_pairs={{0,15},{1,2},{2,1},{3,4},{4,3},{5,6},{6,5},{7,8},{8,7},{9,10},{10,... | collective-permute-start | bytes 196616 | tf_op jit(solution)/shard_map/ppermute | solution.py:509
  33.4 1.0 %shard_map.119 = (bf16[768,1024]{1,0:T(8,128)(2,1)S(1)}, f32[128,1024]{1,0:T(8,128)S(1)}) custom-call(bf16[256,1024]{1,0:T(8,128)(2,1)S(1)} %get-tuple-element.97.a_ref, bf16[384,768]{1,0:T(8,128)(2,1)S(1)} %shard_map.111.w_ref.refs_8_.refs_4_), custom_call_target="tpu_custom_call" | custom-call | tf_op jit(solution)/shard_map/pallas_call | solution.py:554
  34.4 0.9 %shard_map.122.acc_ref = f32[1168,256]{1,0:T(8,128)S(1)} custom-call(f32[1168,256]{1,0:T(8,128)S(1)} %shard_map.117.refs_0_, bf16[3,64,8,128]{3,2,1,0:T(8,128)(2,1)S(1)} %copy-done.1, bf16[64,8,128]{2,1,0:T(8,128)(2,1)S(1)} %get-tuple-element.110.refs_2_.h2_ref, bf16[768,1024]{1,0:T(8,128)(2,1)S(1)} %get-tuple-element.111.refs_3_), custom_call_target="tpu_custom_call", output_to_operand_aliasing={{}: (0, {})} | custom-call | tf_op jit(solution)/shard_map/pallas_call | solution.py:575
  35.3 0.4 collective-permute-done.7.refs_3_.k1_ref
  35.8 1.7 %shard_map.120 = (bf16[64,8,128]{2,1,0:T(8,128)(2,1)S(1)}, bf16[768,384]{1,0:T(8,128)(2,1)S(1)}, f32[64,8,128]{2,1,0:T(8,128)S(1)}, bf16[256,1024]{1,0:T(8,128)(...) custom-call(bf16[384,128]{1,0:T(8,128)(2,1)S(1)} %collective-permute, ...), custom_call_target="tpu_custom_call" | custom-call | tf_op jit(solution)/shard_map/pallas_call | solution.py:564
  37.5 2.2 %shard_map.123 = bf16[1280,256]{1,0:T(8,128)(2,1)} custom-call(f32[1168,256]{1,0:T(8,128)S(1)} %shard_map.122.acc_ref, bf16[3,64,8,128]{3,2,1,0:T(8,128)(2,1)S(1)} %copy-done.1, bf16[64,8,128]{2,1,0:T(8,128)(2,1)S(1)} %get-tuple-element.110.refs_2_.h2_ref, bf16[768,384]{1,0:T(8,128)(2,1)S(1)} %get-tuple-element.112.b_ref, bf16[64,8,128]{2,1,0:T(8,128)(2,1)S(1)} %copy-done.5, ...), custom_call_target="tpu_custom_call" | custom-call | tf_op jit(solution)/shard_map/pallas_call | solution.py:602
  39.8 5.5 %all-to-all-start = ((bf16[16,80,256]{2,1,0:T(8,128)(2,1)}), bf16[16,80,256]{2,1,0:T(8,128)(2,1)S(1)}, u32[]{:S(2)}, u32[]{:S(2)}) async-start(bf16[16,80,256]{2,1,0:T(8,128)(2,1)} %bitcast), calls=%async_computation | async-start | bytes 1310720 | tf_op jit(solution)/shard_map/all_to_all | solution.py:610
  45.2 2.5 %collective-permute-start.8 = (bf16[256,128]{1,0:T(8,128)(2,1)S(1)}, bf16[256,128]{1,0:T(8,128)(2,1)S(1)}, u32[]{:S(2)}, u32[]{:S(2)}) collective-permute-start(bf16[256,128]{1,0:T(8,128)(2,1)S(1)} %get-tuple-element.103), channel_id=1, source_target_pairs={{0,16},{16,0},{32,48},{48,32},{64,80},{80,64},{96,112},{112,96},{1... | collective-permute-start | bytes 196616 | tf_op jit(solution)/shard_map/ppermute | solution.py:509
  47.8 1.8 %shard_map.124 = (bf16[768,1024]{1,0:T(8,128)(2,1)}, f32[128,1024]{1,0:T(8,128)S(1)}) custom-call(bf16[256,1024]{1,0:T(8,128)(2,1)S(1)} %get-tuple-element.113.a_ref, bf16[384,768]{1,0:T(8,128)(2,1)S(1)} %shard_map.111.w_ref.refs_8_.refs_4_), custom_call_target="tpu_custom_call" | custom-call | tf_op jit(solution)/shard_map/pallas_call | solution.py:554
  49.6 2.1 %collective-permute-done.9.r1_ref = bf16[256,128]{1,0:T(8,128)(2,1)S(1)} collective-permute-done((bf16[256,128]{1,0:T(8,128)(2,1)S(1)}, bf16[256,128]{1,0:T(8,128)(2,1)S(1)}, u32[]{:S(2)}, u32[]{:S(2)}) %collective-permute-start.9) | collective-permute-done | bytes 65568 | tf_op jit(solution)/shard_map/ppermute | solution.py:509
  51.9 3.5 %all-to-all-done = bf16[16,80,256]{2,1,0:T(8,128)(2,1)S(1)} async-done(((bf16[16,80,256]{2,1,0:T(8,128)(2,1)}), bf16[16,80,256]{2,1,0:T(8,128)(2,1)S(1)}, u32[]{:S(2)}, u32[]{:S(2)}) %all-to-all-start) | async-done | bytes 655392 | tf_op jit(solution)/shard_map/all_to_all | solution.py:610
  55.4 0.8 %shard_map.125 = f32[256,80]{1,0:T(8,128)} custom-call(bf16[1280,256]{1,0:T(8,128)(2,1)S(1)} %bitcast.5), custom_call_target="tpu_custom_call" | custom-call | tf_op jit(solution)/shard_map/pallas_call | solution.py:615
  56.2 9.2 %all-to-all-start.1 = ((f32[16,16,80]{2,1,0:T(8,128)}), f32[16,16,80]{2,1,0:T(8,128)S(1)}, u32[]{:S(2)}, u32[]{:S(2)}) async-start(f32[16,16,80]{2,1,0:T(8,128)} %bitcast.2), calls=%async_computation.1 | async-start | bytes 262144 | tf_op jit(solution)/shard_map/all_to_all | solution.py:616
  65.5 0.9 %collective-permute-start.11 = (bf16[256,128]{1,0:T(8,128)(2,1)S(1)}, bf16[256,128]{1,0:T(8,128)(2,1)S(1)}, u32[]{:S(2)}, u32[]{:S(2)}) collective-permute-start(bf16[256,128]{1,0:T(8,128)(2,1)S(1)} %get-tuple-element.108), channel_id=1, source_target_pairs={{0,15},{1,2},{2,1},{3,4},{4,3},{5,6},{6,5},{7,8},{8,7},{9,10},{10,... | collective-permute-start | bytes 196616 | tf_op jit(solution)/shard_map/ppermute | solution.py:509
  66.4 5.9 %collective-permute-done.11.k1_ref = bf16[256,128]{1,0:T(8,128)(2,1)S(1)} collective-permute-done((bf16[256,128]{1,0:T(8,128)(2,1)S(1)}, bf16[256,128]{1,0:T(8,128)(2,1)S(1)}, u32[]{:S(2)}, u32[]{:S(2)}) %collective-permute-start.11) | collective-permute-done | bytes 65568 | tf_op jit(solution)/shard_map/ppermute | solution.py:509
  72.3 1.8 %shard_map.126 = (bf16[3,64,8,128]{3,2,1,0:T(8,128)(2,1)}, f32[64,8,128]{2,1,0:T(8,128)}, f32[64,8,128]{2,1,0:T(8,128)}) custom-call(bf16[64,8,128]{2,1,0:T(8,128)(2,1)S(1)} %get-tuple-element.100.gi1_ref, bf16[64,8,128]{2,1,0:T(8,128)(2,1)S(1)} %get-tuple-element.101.gi2_ref, f32[64,8,128]{2,1,0:T(8,128)S(1)} %get-tuple-element.102.dc_ref, ...), custom_call_target="tpu_custom_call" | custom-call | tf_op jit(solution)/shard_map/pallas_call | solution.py:618
  74.0 0.3 all-to-all-done.1
  74.4 0.7 shard_map.127
  (28 shorter events, 0.8 us)
Async XLA Ops:
  0.6 6.2 %copy-start.4 = (bf16[256,1152]{1,0:T(8,128)(2,1)S(1)}, bf16[256,1152]{1,0:T(8,128)(2,1)}, u32[]{:S(2)}) copy-start(bf16[256,1152]{1,0:T(8,128)(2,1)} %k_ref.1) | copy-start | bytes 1769476
  0.6 6.5 %copy-start.1 = (bf16[3,64,8,128]{3,2,1,0:T(8,128)(2,1)S(1)}, bf16[3,64,8,128]{3,2,1,0:T(8,128)(2,1)}, u32[]{:S(2)}) copy-start(bf16[3,64,8,128]{3,2,1,0:T(8,128)(2,1)} %x_ref.3) | copy-start | bytes 1179652
  0.7 6.5 %copy-start.5 = (bf16[64,8,128]{2,1,0:T(8,128)(2,1)S(1)}, bf16[64,8,128]{2,1,0:T(8,128)(2,1)}, u32[]{:S(2)}) copy-start(bf16[64,8,128]{2,1,0:T(8,128)(2,1)} %h_ref.3) | copy-start | bytes 393220
  3.5 13.8 %copy-start = (bf16[3,256,8,128]{3,2,1,0:T(8,128)(2,1)S(1)}, bf16[3,256,8,128]{3,2,1,0:T(8,128)(2,1)}, u32[]{:S(2)}) copy-start(bf16[3,256,8,128]{3,2,1,0:T(8,128)(2,1)} %refs_6_.1) | copy-start | bytes 4718596
  3.6 13.8 %copy-start.2 = (bf16[3,64,8,128]{3,2,1,0:T(8,128)(2,1)S(1)}, bf16[3,64,8,128]{3,2,1,0:T(8,128)(2,1)}, u32[]{:S(2)}) copy-start(bf16[3,64,8,128]{3,2,1,0:T(8,128)(2,1)} %refs_7_.1) | copy-start | bytes 1179652
  3.6 13.8 %copy-start.6 = (s32[8,128]{1,0:T(8,128)S(1)}, s32[8,128]{1,0:T(8,128)}, u32[]{:S(2)}) copy-start(s32[8,128]{1,0:T(8,128)} %refs_10_.3) | copy-start | bytes 12292
  3.6 4.2 %collective-permute-start = (bf16[256,128]{1,0:T(8,128)(2,1)S(1)}, bf16[256,128]{1,0:T(8,128)(2,1)S(1)}, u32[]{:S(2)}, u32[]{:S(2)}) collective-permute-start(bf16[256,128]{1,0:T(8,128)(2,1)S(1)} %get-tuple-element.64), channel_id=1, source_target_pairs={{0,16},{16,0},{32,48},{48,32},{64,80},{80,64},{96,112},{112,96},{1... | collective-permute-start | bytes 196616 | tf_op jit(solution)/shard_map/ppermute | solution.py:509
  6.9 3.7 %collective-permute-start.1 = (bf16[256,128]{1,0:T(8,128)(2,1)S(1)}, bf16[256,128]{1,0:T(8,128)(2,1)S(1)}, u32[]{:S(2)}, u32[]{:S(2)}) collective-permute-start(bf16[256,128]{1,0:T(8,128)(2,1)S(1)} %get-tuple-element.65), channel_id=1, source_target_pairs={{0,240},{16,32},{32,16},{48,64},{64,48},{80,96},{96,80},{112,128},... | collective-permute-start | bytes 196616 | tf_op jit(solution)/shard_map/ppermute | solution.py:509
  10.7 4.8 %collective-permute-start.2 = (bf16[256,128]{1,0:T(8,128)(2,1)S(1)}, bf16[256,128]{1,0:T(8,128)(2,1)S(1)}, u32[]{:S(2)}, u32[]{:S(2)}) collective-permute-start(bf16[256,128]{1,0:T(8,128)(2,1)S(1)} %get-tuple-element.78), channel_id=1, source_target_pairs={{0,1},{1,0},{2,3},{3,2},{4,5},{5,4},{6,7},{7,6},{8,9},{9,8},{10,11... | collective-permute-start | bytes 196616 | tf_op jit(solution)/shard_map/ppermute | solution.py:509
  10.8 6.5 %collective-permute-start.3 = (bf16[256,128]{1,0:T(8,128)(2,1)S(1)}, bf16[256,128]{1,0:T(8,128)(2,1)S(1)}, u32[]{:S(2)}, u32[]{:S(2)}) collective-permute-start(bf16[256,128]{1,0:T(8,128)(2,1)S(1)} %get-tuple-element.79), channel_id=1, source_target_pairs={{0,15},{1,2},{2,1},{3,4},{4,3},{5,6},{6,5},{7,8},{8,7},{9,10},{10,... | collective-permute-start | bytes 196616 | tf_op jit(solution)/shard_map/ppermute | solution.py:509
  19.1 7.0 %collective-permute-start.4 = (bf16[384,128]{1,0:T(8,128)(2,1)S(1)}, bf16[384,128]{1,0:T(8,128)(2,1)S(1)}, u32[]{:S(2)}, u32[]{:S(2)}) collective-permute-start(bf16[384,128]{1,0:T(8,128)(2,1)S(1)} %get-tuple-element.86), channel_id=1, source_target_pairs={{0,16},{16,0},{32,48},{48,32},{64,80},{80,64},{96,112},{112,96},{1... | collective-permute-start | bytes 294920 | tf_op jit(solution)/shard_map/ppermute | solution.py:509
  24.4 4.3 %collective-permute-start.5 = (bf16[384,128]{1,0:T(8,128)(2,1)S(1)}, bf16[384,128]{1,0:T(8,128)(2,1)S(1)}, u32[]{:S(2)}, u32[]{:S(2)}) collective-permute-start(bf16[384,128]{1,0:T(8,128)(2,1)S(1)} %get-tuple-element.87), channel_id=1, source_target_pairs={{0,240},{16,32},{32,16},{48,64},{64,48},{80,96},{96,80},{112,128},... | collective-permute-start | bytes 294920 | tf_op jit(solution)/shard_map/ppermute | solution.py:509
  29.0 6.4 %collective-permute-start.6 = (bf16[256,128]{1,0:T(8,128)(2,1)S(1)}, bf16[256,128]{1,0:T(8,128)(2,1)S(1)}, u32[]{:S(2)}, u32[]{:S(2)}) collective-permute-start(bf16[256,128]{1,0:T(8,128)(2,1)S(1)} %get-tuple-element.95), channel_id=1, source_target_pairs={{0,1},{1,0},{2,3},{3,2},{4,5},{5,4},{6,7},{7,6},{8,9},{9,8},{10,11... | collective-permute-start | bytes 196616 | tf_op jit(solution)/shard_map/ppermute | solution.py:509
  29.1 6.7 %collective-permute-start.7 = (bf16[256,128]{1,0:T(8,128)(2,1)S(1)}, bf16[256,128]{1,0:T(8,128)(2,1)S(1)}, u32[]{:S(2)}, u32[]{:S(2)}) collective-permute-start(bf16[256,128]{1,0:T(8,128)(2,1)S(1)} %get-tuple-element.96), channel_id=1, source_target_pairs={{0,15},{1,2},{2,1},{3,4},{4,3},{5,6},{6,5},{7,8},{8,7},{9,10},{10,... | collective-permute-start | bytes 196616 | tf_op jit(solution)/shard_map/ppermute | solution.py:509
  34.4 1.4 %copy-start.3 = (f32[64,8,128]{2,1,0:T(8,128)S(1)}, f32[64,8,128]{2,1,0:T(8,128)}, u32[]{:S(2)}) copy-start(f32[64,8,128]{2,1,0:T(8,128)} %refs_8_.1) | copy-start | bytes 786436
  39.8 15.7 %all-to-all-start = ((bf16[16,80,256]{2,1,0:T(8,128)(2,1)}), bf16[16,80,256]{2,1,0:T(8,128)(2,1)S(1)}, u32[]{:S(2)}, u32[]{:S(2)}) async-start(bf16[16,80,256]{2,1,0:T(8,128)(2,1)} %bitcast), calls=%async_computation | async-start | bytes 1310720 | tf_op jit(solution)/shard_map/all_to_all | solution.py:610
  45.2 4.4 %collective-permute-start.8 = (bf16[256,128]{1,0:T(8,128)(2,1)S(1)}, bf16[256,128]{1,0:T(8,128)(2,1)S(1)}, u32[]{:S(2)}, u32[]{:S(2)}) collective-permute-start(bf16[256,128]{1,0:T(8,128)(2,1)S(1)} %get-tuple-element.103), channel_id=1, source_target_pairs={{0,16},{16,0},{32,48},{48,32},{64,80},{80,64},{96,112},{112,96},{1... | collective-permute-start | bytes 196616 | tf_op jit(solution)/shard_map/ppermute | solution.py:509
  47.8 4.0 %collective-permute-start.9 = (bf16[256,128]{1,0:T(8,128)(2,1)S(1)}, bf16[256,128]{1,0:T(8,128)(2,1)S(1)}, u32[]{:S(2)}, u32[]{:S(2)}) collective-permute-start(bf16[256,128]{1,0:T(8,128)(2,1)S(1)} %get-tuple-element.104), channel_id=1, source_target_pairs={{0,240},{16,32},{32,16},{48,64},{64,48},{80,96},{96,80},{112,128},... | collective-permute-start | bytes 196616 | tf_op jit(solution)/shard_map/ppermute | solution.py:509
  56.2 18.1 %all-to-all-start.1 = ((f32[16,16,80]{2,1,0:T(8,128)}), f32[16,16,80]{2,1,0:T(8,128)S(1)}, u32[]{:S(2)}, u32[]{:S(2)}) async-start(f32[16,16,80]{2,1,0:T(8,128)} %bitcast.2), calls=%async_computation.1 | async-start | bytes 262144 | tf_op jit(solution)/shard_map/all_to_all | solution.py:616
  65.5 6.8 %collective-permute-start.11 = (bf16[256,128]{1,0:T(8,128)(2,1)S(1)}, bf16[256,128]{1,0:T(8,128)(2,1)S(1)}, u32[]{:S(2)}, u32[]{:S(2)}) collective-permute-start(bf16[256,128]{1,0:T(8,128)(2,1)S(1)} %get-tuple-element.108), channel_id=1, source_target_pairs={{0,15},{1,2},{2,1},{3,4},{4,3},{5,6},{6,5},{7,8},{8,7},{9,10},{10,... | collective-permute-start | bytes 196616 | tf_op jit(solution)/shard_map/ppermute | solution.py:509
  66.4 5.9 %collective-permute-start.10 = (bf16[256,128]{1,0:T(8,128)(2,1)S(1)}, bf16[256,128]{1,0:T(8,128)(2,1)S(1)}, u32[]{:S(2)}, u32[]{:S(2)}) collective-permute-start(bf16[256,128]{1,0:T(8,128)(2,1)S(1)} %get-tuple-element.107), channel_id=1, source_target_pairs={{0,1},{1,0},{2,3},{3,2},{4,5},{5,4},{6,7},{7,6},{8,9},{9,8},{10,11... | collective-permute-start | bytes 196616 | tf_op jit(solution)/shard_map/ppermute | solution.py:509

commit v4 on v3

--- a/solution.py
+++ b/solution.py
@@ -95,8 +95,7 @@
         p1_ref[rows, :] = bottom
 
 
-def emit_grads(scr, a_ref, p0_ref, p1_ref, ql_ref, qr_ref):
-    par = parity("row")
+def emit_grads(scr, a_ref, p0_ref, p1_ref, packs=None):
     step = 32
     lanes = lane_ids(step)
     for k in range(Q // step):
@@ -106,17 +105,16 @@
         for r in range(ROWS):
             row = scr[pl.ds(k * step * ROWS + r, step, stride=ROWS), :]
             a_ref[own, r * LANES : (r + 1) * LANES] = row.astype(BF16)
-            ql = jnp.where(lanes == r + 1, pltpu.roll(row, r + 1, 1), ql)
-            qr = jnp.where(lanes == r + 1, pltpu.roll(row, r + 2, 1), qr)
-        ql_ref[own, :] = ql.astype(BF16)
-        qr_ref[own, :] = qr.astype(BF16)
-    top = a_ref[:, 0:LANES]
-    bottom = a_ref[:, (ROWS - 1) * LANES :]
-
-    by_parity(par, top, bottom, p0_ref, p1_ref, 0)
-
-
-def forward_kernel(pre_hbm, cot_hbm, c0_hbm, mask_hbm, c1_ref, c2_ref, dc_ref, a_ref, p0_ref, p1_ref, ql_ref, qr_ref, scr, pre_ref, cot_ref, c0_ref, mask_ref, sems):
+            if packs:
+                ql = jnp.where(lanes == r + 1, pltpu.roll(row, r + 1, 1), ql)
+                qr = jnp.where(lanes == r + 1, pltpu.roll(row, r + 2, 1), qr)
+        if packs:
+            packs[0][own, :] = ql.astype(BF16)
+            packs[1][own, :] = qr.astype(BF16)
+    by_parity(parity("row"), a_ref[:, 0:LANES], a_ref[:, (ROWS - 1) * LANES :], p0_ref, p1_ref, 0)
+
+
+def forward_kernel(pre_hbm, cot_hbm, c0_hbm, mask_hbm, c1_ref, c2_ref, dc_ref, a_ref, p0_ref, p1_ref, scr, pre_ref, cot_ref, c0_ref, mask_ref, sems):
     pairs = [(c0_hbm, c0_ref), (mask_hbm, mask_ref), (cot_hbm.at[2], cot_ref)]
     for t, g in ((0, 1), (0, 0), (0, 3), (1, 1), (1, 0), (1, 3), (2, 1), (2, 0), (2, 3), (2, 2)):
         own = pl.ds(g * CH, CH)
@@ -159,7 +157,7 @@
         return carry
 
     lax.fori_loop(0, CH // step, chunk, 0)
-    emit_grads(scr, a_ref, p0_ref, p1_ref, ql_ref, qr_ref)
+    emit_grads(scr, a_ref, p0_ref, p1_ref)
 
 
 def hidden_kernel(pre_ref, c1_ref, c2_ref, mask_ref, h1_ref, h2_ref):
@@ -192,27 +190,27 @@
     return above, below
 
 
-ZLANE = 16
-
-
-def corner_kernel(with_z, r0_ref, r1_ref, ql_ref, qr_ref, c0_ref, c1_ref):
+SECOND, PRE, STATE, ZLANE = 16, 32, 48, 64
+CORNER = Q + W
+
+
+def move(x, source, target):
+    shift = (target - source) % LANES
+    return pltpu.roll(x, shift, 1) if shift else x
+
+
+def corner_kernel(wide, r0_ref, r1_ref, ql_ref, qr_ref, c0_ref, c1_ref):
     par = parity("col").astype(F32)
     step = 32
     lanes = lane_ids(step)
     for k in range(Q // step):
         own = pl.ds(k * step, step)
         above, below = halo_rows(r0_ref, r1_ref, own)
-        left = jnp.where(lanes == 0, above, ql_ref[own, :].astype(F32))
-        left = jnp.where(lanes == SLABS - 1, pltpu.roll(below, SLABS - 1, 1), left)
-        right = jnp.where(lanes == 0, pltpu.roll(above, 1, 1), qr_ref[own, :].astype(F32))
-        right = jnp.where(lanes == SLABS - 1, pltpu.roll(below, SLABS, 1), right)
-        if with_z and k < W // step:
-            above, below = halo_rows(r0_ref, r1_ref, pl.ds(Q + k * step, step))
-            far = ZLANE + SLABS - 1
-            left = jnp.where(lanes == ZLANE, pltpu.roll(above, ZLANE, 1), left)
-            left = jnp.where(lanes == far, pltpu.roll(below, far, 1), left)
-            right = jnp.where(lanes == ZLANE, pltpu.roll(above, ZLANE + 1, 1), right)
-            right = jnp.where(lanes == far, pltpu.roll(below, far + 1, 1), right)
+        left, right = ql_ref[own, :].astype(F32), qr_ref[own, :].astype(F32)
+        for depth in range(2 if wide else 1):
+            for row, lane in ((above, depth * SECOND), (below, depth * SECOND + SLABS - 1)):
+                left = jnp.where(lanes == lane, move(row, depth, lane), left)
+                right = jnp.where(lanes == lane, move(row, LANES - 1 - depth, lane), right)
         c0_ref[own, :] = (right * (1.0 - par) + left * par).astype(BF16)
         c1_ref[own, :] = (left * (1.0 - par) + right * par).astype(BF16)
 
@@ -226,23 +224,40 @@
     return left, right
 
 
-def z_edges_kernel(x_ref, h_ref, p0_ref, p1_ref, zl_ref, zr_ref, tmp):
+def edges_kernel(a_ref, pre_ref, cot_ref, cell_ref, dc_ref, mask_ref, x_ref, h_ref, p0_ref, p1_ref, ql_ref, qr_ref, pre_tmp, state, tmp):
     stack_fields(0, x_ref, h_ref, tmp)
     top = tmp[pl.ds(0, W, stride=ROWS), :].astype(BF16)
     bottom = tmp[pl.ds(ROWS - 1, W, stride=ROWS), :].astype(BF16)
     by_parity(parity("row"), top, bottom, p0_ref, p1_ref, 0)
-    step = 32
-    lanes = lane_ids(step)
-    for k in range(W // step):
-        zl = jnp.zeros((step, LANES), F32)
-        zr = jnp.zeros((step, LANES), F32)
+    land = mask_ref[...][None] > 0
+    size = CH * ROWS
+    for g in range(4):
+        block = pre_ref[1, g * CH : (g + 1) * CH].astype(F32)
+        if g == 2:
+            block = jnp.where(land, block, -64.0)
+        pre_tmp[g * size : (g + 1) * size, :] = block.reshape(size, LANES)
+    state[0:size, :] = cot_ref[1].astype(F32).reshape(size, LANES)
+    state[size : 2 * size, :] = cell_ref[...].reshape(size, LANES)
+    state[2 * size :, :] = dc_ref[...].reshape(size, LANES)
+    step = 32
+    lanes = lane_ids(step)
+    for k in range(Q // step):
+        left = jnp.zeros((step, LANES), F32)
+        right = jnp.zeros((step, LANES), F32)
         for r in range(ROWS):
-            row = tmp[pl.ds(k * step * ROWS + r, step, stride=ROWS), :]
-            lane = ZLANE + r + 1
-            zl = jnp.where(lanes == lane, pltpu.roll(row, lane, 1), zl)
-            zr = jnp.where(lanes == lane, pltpu.roll(row, lane + 1, 1), zr)
-        zl_ref[pl.ds(k * step, step), :] = zl.astype(BF16)
-        zr_ref[pl.ds(k * step, step), :] = zr.astype(BF16)
+            own = pl.ds(k * step * ROWS + r, step, stride=ROWS)
+            row = a_ref[pl.ds(k * step, step), r * LANES : (r + 1) * LANES].astype(F32)
+            pieces = [(row, 0, 0), (row, 1, SECOND), (pre_tmp[own, :], 0, PRE)]
+            if k < 3 * CH // step:
+                pieces.append((state[own, :], 0, STATE))
+            if k < W // step:
+                pieces.append((tmp[own, :], 0, ZLANE))
+            for piece, depth, slot in pieces:
+                lane = slot + r + 1
+                left = jnp.where(lanes == lane, move(piece, depth, lane), left)
+                right = jnp.where(lanes == lane, move(piece, LANES - 1 - depth, lane), right)
+        ql_ref[pl.ds(k * step, step), :] = left.astype(BF16)
+        qr_ref[pl.ds(k * step, step), :] = right.astype(BF16)
 
 
 def interior_kernel(a_ref, w_ref, b_ref, y_ref, y3):
@@ -268,15 +283,39 @@
         y_ref[:, r * LANES : (r + 1) * LANES] = total
 
 
-def build_halo(r0_ref, r1_ref, c0_ref, c1_ref, b_ref):
+def travelled(r0_ref, r1_ref, c0_ref, c1_ref):
+    def source(k, step):
+        own = pl.ds(k * step, step)
+        return halo_rows(r0_ref, r1_ref, own) + halo_columns(c0_ref, c1_ref, own)
+
+    return source
+
+
+def corner_lanes(lanes, r0_ref, r1_ref, group, left, right, first):
+    above, below = halo_rows(r0_ref, r1_ref, pl.ds(CORNER, 32))
+    for row, lane in ((above, first), (below, first + SLABS - 1)):
+        right = jnp.where(lanes == lane, move(row, 2 * group, lane), right)
+        left = jnp.where(lanes == lane, move(row, 2 * group + 1, lane), left)
+    return left, right
+
+
+def computed(r0_ref, r1_ref, pack_ref):
+    def source(k, step):
+        own = pl.ds(k * step, step)
+        pack = pack_ref[own, :].astype(F32)
+        columns = corner_lanes(lane_ids(step), r0_ref, r1_ref, k, pltpu.roll(pack, LANES // 2, 1), pack, 0)
+        return halo_rows(r0_ref, r1_ref, own) + columns
+
+    return source
+
+
+def build_halo(source, b_ref):
     step = 32
     lanes = lane_ids(step)
     inside = (lanes >= 1) & (lanes <= ROWS)
     last = SLABS - 1
     for k in range(Q // step):
-        own = pl.ds(k * step, step)
-        above, below = halo_rows(r0_ref, r1_ref, own)
-        left, right = halo_columns(c0_ref, c1_ref, own)
+        above, below, left, right = source(k, step)
         for n, (row, s) in enumerate(((above, 0), (below, last))):
             span = slice(n * LANES, (n + 1) * LANES)
             minus = jnp.where(lanes == LANES - 1, pltpu.roll(right, LANES - 1 - s, 1), pltpu.roll(row, LANES - 1, 1))
@@ -297,7 +336,7 @@
     for k in range(W // step):
         side = 0.0
         for u in range(3):
-            piece = y3[pl.ds(u * W + k * step, step), 2 * LANES :]
+            piece = y3[pl.ds(u * W + k * step, step), 2 * LANES : 3 * LANES]
             side = side + (piece if u == 2 else pltpu.roll(piece, LANES + u - 2, 1))
         for r in range(ROWS):
             total = y_ref[pl.ds(k * step, step), r * LANES : (r + 1) * LANES]
@@ -310,13 +349,7 @@
             scr[pl.ds(k * step * ROWS + r, step, stride=ROWS), :] = total + left
 
 
-def backward_kernel(t, with_z, *refs):
-    edges = refs[:4] if with_z else None
-    refs = refs[4:] if with_z else refs
-    (r0_ref, r1_ref, k0_ref, k1_ref, w_ref, y_ref, pre_ref, cot_ref, before_ref, cell_ref, mask_ref, dc_in,
-     gi_ref, b_ref, dc_ref, a_ref, p0_ref, p1_ref, ql_ref, qr_ref, y3, yscr, scr) = refs
-    build_halo(r0_ref, r1_ref, k0_ref, k1_ref, b_ref)
-    finish_y(w_ref, b_ref, y_ref, y3, yscr)
+def step_grads(t, pre_ref, cot_ref, before_ref, cell_ref, mask_ref, dc_in, gi_ref, dc_ref, yscr, scr):
     step = 4
     mask = mask_ref[...].astype(F32)[None]
 
@@ -337,17 +370,80 @@
         return carry
 
     lax.fori_loop(0, CH // step, chunk, 0)
-    emit_grads(scr, a_ref, p0_ref, p1_ref, ql_ref, qr_ref)
-    if with_z:
-        z0_ref, z1_ref, zl_ref, zr_ref = edges
-        p0_ref[Q:, :] = z0_ref[...]
-        p1_ref[Q:, :] = z1_ref[...]
-        ql_ref[0:W, :] = (ql_ref[0:W, :].astype(F32) + zl_ref[...].astype(F32)).astype(BF16)
-        qr_ref[0:W, :] = (qr_ref[0:W, :].astype(F32) + zr_ref[...].astype(F32)).astype(BF16)
+
+
+def third_kernel(r0_ref, r1_ref, k0_ref, k1_ref, s0_ref, s1_ref, z0_ref, z1_ref, w_ref, y_ref, pre_ref, cot_ref, before_ref, cell_ref, mask_ref, dc_in,
+                 gi_ref, bh_ref, dc_ref, a_ref, p0_ref, p1_ref, pack_ref, b_ref, y3, yscr, scr):
+    build_halo(travelled(r0_ref, r1_ref, k0_ref, k1_ref), b_ref)
+    par = parity("col").astype(F32)
+    step = 32
+    half = LANES // 2
+    lanes = lane_ids(step)
+    first, second = lanes < SLABS, (lanes >= half) & (lanes < half + SLABS)
+    for k in range(Q // step):
+        own = pl.ds(k * step, step)
+        left, right = halo_columns(k0_ref, k1_ref, own)
+        sent0, sent1 = s0_ref[own, :].astype(F32), s1_ref[own, :].astype(F32)
+        my_right = sent0 * (1.0 - par) + sent1 * par
+        my_left = sent1 * (1.0 - par) + sent0 * par
+        pairs = (
+            (move(right, SECOND, 0), move(my_left, 0, half)),
+            (right, move(left, 0, half)),
+            (my_right, move(left, SECOND, half)),
+        )
+        for v, (low, high) in enumerate(pairs):
+            b_ref[pl.ds(v * Q + k * step, step), 3 * LANES :] = jnp.where(first, low, jnp.where(second, high, 0.0)).astype(BF16)
+    bh_ref[...] = b_ref[:, 0 : 3 * LANES]
+    finish_y(w_ref, b_ref, y_ref, y3, yscr)
+    step_grads(1, pre_ref, cot_ref, before_ref, cell_ref, mask_ref, dc_in, gi_ref, dc_ref, yscr, scr)
+    low, high = edge_flags("col")
+    valid = jnp.where((lanes >= 1) & (lanes <= ROWS), high, jnp.where((lanes > half) & (lanes <= half + ROWS), low, 0.0))
+    for j in range(CH // step):
+
+        def border(start, slot):
+            left, right = halo_columns(k0_ref, k1_ref, pl.ds(start + j * step, step))
+            return jnp.where(lanes < half, move(right, slot, 0), move(left, slot, half))
+
+        dh = 0.0
+        for u in range(3):
+            dh = dh + move(y3[pl.ds(u * W + CH + j * step, step), 3 * LANES :], 1, u)
+        gates = [border(g * CH, PRE) for g in range(4)]
+        cot, before, dc = (border(m * CH, STATE) for m in range(3))
+        pre = (sigmoid(gates[0]), sigmoid(gates[1]), sigmoid(gates[2]), jnp.tanh(gates[3]))
+        tanh_cell = jnp.tanh(pre[1] * before + pre[0] * pre[3])
+        part = [None] * 4
+        gate_grads(pre, part, cot, dh, valid, before, tanh_cell, dc * valid)
+        for g in range(4):
+            pack_ref[pl.ds(g * CH + j * step, step), :] = part[g].astype(BF16)
+    emit_grads(scr, a_ref, p0_ref, p1_ref)
+    p0_ref[Q:CORNER, :] = z0_ref[...]
+    p1_ref[Q:CORNER, :] = z1_ref[...]
+    corners = []
+    for r in (0, ROWS - 1):
+        block = jnp.zeros((step, LANES), F32)
+        for k in range(Q // step):
+            pack = pack_ref[pl.ds(k * step, step), :].astype(F32)
+            block = jnp.where(lanes == 2 * k, move(pack, r + 1, 2 * k), block)
+            block = jnp.where(lanes == 2 * k + 1, move(pack, half + r + 1, 2 * k + 1), block)
+        for k in range(W // step):
+            left, right = halo_columns(k0_ref, k1_ref, pl.ds(k * step, step))
+            lane = 2 * (Q // step + k)
+            block = jnp.where(lanes == lane, move(right, ZLANE + r + 1, lane), block)
+            block = jnp.where(lanes == lane + 1, move(left, ZLANE + r + 1, lane + 1), block)
+        corners.append(block.astype(BF16))
+    by_parity(parity("row"), corners[0], corners[1], p0_ref, p1_ref, CORNER)
+
+
+def second_kernel(r0_ref, r1_ref, pack_ref, w_ref, y_ref, pre_ref, cot_ref, before_ref, cell_ref, mask_ref, dc_in,
+                  gi_ref, b_ref, dc_ref, a_ref, p0_ref, p1_ref, ql_ref, qr_ref, y3, yscr, scr):
+    build_halo(computed(r0_ref, r1_ref, pack_ref), b_ref)
+    finish_y(w_ref, b_ref, y_ref, y3, yscr)
+    step_grads(0, pre_ref, cot_ref, before_ref, cell_ref, mask_ref, dc_in, gi_ref, dc_ref, yscr, scr)
+    emit_grads(scr, a_ref, p0_ref, p1_ref, (ql_ref, qr_ref))
 
 
 def last_kernel(gi1_ref, gi2_ref, dc_ref, r0_ref, r1_ref, k0_ref, k1_ref, w_ref, y_ref, gi_ref, dh_ref, cell_ref, b_ref, y3, yscr):
-    build_halo(r0_ref, r1_ref, k0_ref, k1_ref, b_ref)
+    build_halo(travelled(r0_ref, r1_ref, k0_ref, k1_ref), b_ref)
     finish_y(w_ref, b_ref, y_ref, y3, yscr)
     gi_ref[0] = yscr[0 : CH * ROWS, :].reshape(CH, ROWS, LANES).astype(BF16)
     gi_ref[1] = gi1_ref[...]
@@ -434,6 +530,7 @@
     for k in range(W // step):
         above, below = halo_rows(r0_ref, r1_ref, pl.ds(Q + k * step, step))
         left, right = halo_columns(k0_ref, k1_ref, pl.ds(k * step, step))
+        left, right = corner_lanes(lanes, r0_ref, r1_ref, Q // step + k, left, right, ZLANE)
         for source in range(-1, ROWS + 1):
             if source < 0:
                 row = above
@@ -518,18 +615,18 @@
     nrow, ncol = lax.axis_size("row"), lax.axis_size("col")
     scale = 1.0 / math.sqrt(ROWS * LANES * nrow * ncol)
     edge = struct((Q, LANES), BF16)
-    grads_out = (struct((Q, CELLS), BF16), edge, edge, edge, edge)
+    grads_out = (struct((Q, CELLS), BF16), edge, edge)
     scr = pltpu.VMEM((Q * ROWS, LANES), F32)
     y3 = pltpu.VMEM((3 * W, 3 * LANES), F32)
     tmp = pltpu.VMEM((W * ROWS, LANES), F32)
     z3, zh = pltpu.VMEM((ZROWS, CELLS), BF16), pltpu.VMEM((3 * W, 3 * LANES), BF16)
     hbm = pl.BlockSpec(memory_space=pltpu.MemorySpace.HBM)
 
-    c1, c2, dc, a, p0, p1, ql, qr = call(
+    c1, c2, dc, a, p0, p1 = call(
         forward_kernel,
         (struct(field, F32), struct(field, F32), struct(field, F32)) + grads_out,
         in_specs=[hbm] * 4,
-        out_specs=[whole()] * 8,
+        out_specs=[whole()] * 6,
         scratch=[
             scr,
             pltpu.VMEM((3, Q, ROWS, LANES), BF16),
@@ -546,8 +643,8 @@
     interior, halo = struct((3 * Q, CELLS), BF16), struct((3 * Q, 3 * LANES), BF16)
     acc_shape = struct((9 * W + 16, Q), F32)
 
-    def corner(with_z, r0, r1, ql, qr):
-        out = call(functools.partial(corner_kernel, with_z), (edge, edge), in_specs=[whole()] * 4, out_specs=[whole()] * 2)
+    def corner(wide, r0, r1, ql, qr):
+        out = call(functools.partial(corner_kernel, wide), (edge, edge), in_specs=[whole()] * 4, out_specs=[whole()] * 2)
         return out(r0, r1, ql, qr)
 
     def inside(a):
@@ -558,16 +655,6 @@
             out_specs=[whole()] * 2,
             scratch=[pltpu.VMEM((3 * W, CELLS), F32)],
         )(a, weights)
-
-    def backward(t, edges, r0, r1, k0, k1, y, dc):
-        pay = struct((Q + W, LANES), BF16) if edges else edge
-        return call(
-            functools.partial(backward_kernel, t - 1, bool(edges)),
-            (struct(field, BF16), halo, struct(field, F32), struct((Q, CELLS), BF16), pay, pay, edge, edge),
-            in_specs=[whole()] * (len(edges) + 12),
-            out_specs=[whole()] * 8,
-            scratch=[y3, tmp, scr],
-        )(*edges, r0, r1, k0, k1, weights, y, gate_pre, cotangent, cells[t - 1], cells[t], land_mask, dc)
 
     def accumulate(t, acc, b, bh):
         head = [] if acc is None else [acc]
@@ -584,20 +671,37 @@
     r0, r1 = swaps(p0, p1, "row")
     weights = call(weights_kernel, struct((3 * W, 3 * Q), BF16), in_specs=[whole()], out_specs=whole())(kernel)
     zedge = struct((W, LANES), BF16)
-    edges = call(
-        z_edges_kernel, (zedge,) * 4, in_specs=[whole()] * 2, out_specs=[whole()] * 4, scratch=[tmp]
-    )(inputs, hidden_init)
-    r0, r1, weights, edges = lax.optimization_barrier((r0, r1, weights, edges))
-    k0, k1 = swaps(*corner(False, r0, r1, ql, qr), "col")
+    z0, z1, ql, qr = call(
+        edges_kernel,
+        (zedge, zedge, edge, edge),
+        in_specs=[whole()] * 8,
+        out_specs=[whole()] * 4,
+        scratch=[scr, pltpu.VMEM((3 * CH * ROWS, LANES), F32), tmp],
+    )(a, gate_pre, cotangent, c1, dc, land_mask, inputs, hidden_init)
+    r0, r1, weights, ql, qr = lax.optimization_barrier((r0, r1, weights, ql, qr))
+    s0, s1 = corner(True, r0, r1, ql, qr)
+    k0, k1 = swaps(s0, s1, "col")
     b, y = inside(a)
-    gi2, bh, dc, a, p0, p1, ql, qr = backward(2, edges, r0, r1, k0, k1, y, dc)
+    pay = struct((CORNER + 32, LANES), BF16)
+    gi2, bh, dc, a, p0, p1, pack = call(
+        third_kernel,
+        (struct(field, BF16), halo, struct(field, F32), struct((Q, CELLS), BF16), pay, pay, edge),
+        in_specs=[whole()] * 16,
+        out_specs=[whole()] * 7,
+        scratch=[pltpu.VMEM((3 * Q, 4 * LANES), BF16), pltpu.VMEM((3 * W, 4 * LANES), F32), tmp, scr],
+    )(r0, r1, k0, k1, s0, s1, z0, z1, weights, y, gate_pre, cotangent, cells[1], cells[2], land_mask, dc)
     r0, r1 = swaps(p0, p1, "row")
     acc = accumulate(2, None, b, bh)
-    r0, r1, acc = lax.optimization_barrier((r0, r1, acc))
-    k0, k1 = swaps(*corner(True, r0, r1, ql, qr), "col")
     b, y = inside(a)
     acc = accumulate(1, acc, b, None)
-    gi1, bh, dc, a, p0, p1, ql, qr = backward(1, [], r0, r1, k0, k1, y, dc)
+    r0, r1, acc, y = lax.optimization_barrier((r0, r1, acc, y))
+    gi1, bh, dc, a, p0, p1, ql, qr = call(
+        second_kernel,
+        (struct(field, BF16), halo, struct(field, F32)) + grads_out + (edge, edge),
+        in_specs=[whole()] * 11,
+        out_specs=[whole()] * 8,
+        scratch=[y3, tmp, scr],
+    )(r0, r1, pack, weights, y, gate_pre, cotangent, cells[0], cells[1], land_mask, dc)
     size = 9 * W // ncol + 8
     send = call(
         functools.partial(send_kernel, ncol, scale),

time: 75.3 us -> 69.9 us (0.928)
  starting transfers between devices: 34.9 us -> 28.5 us
  waiting for transfers between devices: 19.9 us -> 16.4 us
  local copies, waits for them, and re-layouts: 0.04 us -> 2.68 us
  Pallas kernels: 19.4 us -> 21.2 us
    ppermute x6 -> x5, waiting for transfers between devices: 15.7 us -> 10.1 us  [swaps(): lax.ppermute(second, axis, odd_swap(count))]
    ppermute x6 -> x5, starting transfers between devices: 8.94 us -> 5 us  [swaps(): lax.ppermute(second, axis, odd_swap(count))]
    all_to_all x1, starting transfers between devices: 9.23 us -> 6.01 us  [shards(): got = lax.all_to_all(folded, 'row', 0, 0, tiled=True)]
    unnamed x14 -> x18, local copies, waits for them, and re-layouts: 0.04 us -> 2.68 us
    all_to_all x1, waiting for transfers between devices: 3.48 us -> 5.91 us  [shards(): got = lax.all_to_all(send, 'col', 0, 0, tiled=True)]
    pallas_call x3, Pallas kernels: 3.79 us -> 5.58 us  [the longest x1 2.11 us: shards(): call(third_kernel, (struct(field, BF16), halo, struct(field, F32), struct...]
    ppermute x6 -> x5, starting transfers between devices: 11.2 us -> 12 us  [swaps(): lax.ppermute(first, axis, even_swap(count))]
  transfers between devices with their start and end apart: 14 -> 12, of which waited for: 9 -> 6; matrix products, arithmetic and copies ran while one was open for 0% -> 0% of each run, Pallas kernels for 12% -> 14%
where the time goes in v4:
time: 69.9 us; the launch traced here: 69.6 us
  starting transfers between devices  28.5 us (41%)
  Pallas kernels  21.2 us (30%)
  waiting for transfers between devices  16.4 us (23%)
  local copies, waits for them, and re-layouts  2.68 us (4%)
  between operations  0.85 us (1%)
    ppermute x5, starting transfers between devices, swaps(): lax.ppermute(first, axis, even_swap(count))  12 us
    ppermute x5, waiting for transfers between devices, swaps(): lax.ppermute(second, axis, odd_swap(count))  10.1 us
    all_to_all x1, starting transfers between devices, shards(): got = lax.all_to_all(folded, 'row', 0, 0, tiled=True)  6.01 us
    all_to_all x1, waiting for transfers between devices, shards(): got = lax.all_to_all(send, 'col', 0, 0, tiled=True)  5.91 us
    all_to_all x1, starting transfers between devices, shards(): got = lax.all_to_all(send, 'col', 0, 0, tiled=True)  5.47 us
    ppermute x5, starting transfers between devices, swaps(): lax.ppermute(second, axis, odd_swap(count))  5 us
    pallas_call x3, Pallas kernels, inside(): call(interior_kernel, (interior, struct((W, CELLS), F32)), in_specs=[whol...  3.8 us
    pallas_call x1, Pallas kernels, shards(): call(forward_kernel, (struct(field, F32), struct(field, F32), struct(fiel...  2.76 us
  transfers between devices with their start and end apart: 12, of which 6 were waited for; matrix products, arithmetic and copies ran while one was open for 0% of the time, Pallas kernels for 14%

profile of v4, /device:TPU:1, one launch (start us, length us, event | category | flops | bytes accessed | tf_op | source)
XLA Modules:
  0.0 69.6 jit_solution(14155855542944389726)
XLA Ops:
  0.7 2.8 %shard_map.110 = (f32[64,8,128]{2,1,0:T(8,128)S(1)}, f32[64,8,128]{2,1,0:T(8,128)S(1)}, f32[64,8,128]{2,1,0:T(8,128)S(1)}, bf16[256,1024]{1,0:T(8,128)(2,1)S(1)}...) custom-call(bf16[3,256,8,128]{3,2,1,0:T(8,128)(2,1)} %pre_ref.7, bf16[3,64,8,128]{3,2,1,0:T(8,128)(2,1)} %cot_ref.5, ...), custom_call_target="tpu_custom_call" | custom-call | tf_op jit(solution)/shard_map/pallas_call | solution.py:625
  3.4 3.3 %collective-permute-start = (bf16[256,128]{1,0:T(8,128)(2,1)S(1)}, bf16[256,128]{1,0:T(8,128)(2,1)S(1)}, u32[]{:S(2)}, u32[]{:S(2)}) collective-permute-start(bf16[256,128]{1,0:T(8,128)(2,1)S(1)} %get-tuple-element.58), channel_id=1, source_target_pairs={{0,16},{16,0},{32,48},{48,32},{64,80},{80,64},{96,112},{112,96},{1... | collective-permute-start | bytes 196616 | tf_op jit(solution)/shard_map/ppermute | solution.py:606
  6.7 1.1 %copy-done.4 = bf16[256,1152]{1,0:T(8,128)(2,1)S(1)} copy-done((bf16[256,1152]{1,0:T(8,128)(2,1)S(1)}, bf16[256,1152]{1,0:T(8,128)(2,1)}, u32[]{:S(2)}) %copy-start.4) | copy-done | bytes 589848
  8.1 0.9 %copy-done.5 = bf16[64,8,128]{2,1,0:T(8,128)(2,1)S(1)} copy-done((bf16[64,8,128]{2,1,0:T(8,128)(2,1)S(1)}, bf16[64,8,128]{2,1,0:T(8,128)(2,1)}, u32[]{:S(2)}) %copy-start.5) | copy-done | bytes 131096
  9.0 0.7 copy-done.7
  9.6 1.4 %shard_map.112 = (bf16[128,128]{1,0:T(8,128)(2,1)S(1)}, bf16[128,128]{1,0:T(8,128)(2,1)S(1)}, bf16[256,128]{1,0:T(8,128)(2,1)S(1)}, bf16[256,128]{1,0:T(8,128)(2,1)S(1)}) custom-call(bf16[256,1024]{1,0:T(8,128)(2,1)S(1)} %get-tuple-element.60.a_ref, bf16[3,256,8,128]{3,2,1,0:T(8,128)(2,1)S(1)} %copy-done, bf16[3,64,8,128]{3,2,1,0:T(8,128)(2,1)S(1)} %copy-done.1, ...), custom_call_target="tpu_custom_call" | custom-call | tf_op jit(solution)/shard_map/pallas_call | solution.py:674
  11.0 0.3 shard_map.113
  11.4 1.3 %collective-permute-start.2 = (bf16[256,128]{1,0:T(8,128)(2,1)S(1)}, bf16[256,128]{1,0:T(8,128)(2,1)S(1)}, u32[]{:S(2)}, u32[]{:S(2)}) collective-permute-start(bf16[256,128]{1,0:T(8,128)(2,1)S(1)} %get-tuple-element.69.s0_ref), channel_id=1, source_target_pairs={{0,1},{1,0},{2,3},{3,2},{4,5},{5,4},{6,7},{7,6},{8,9},{9,8},{10,11... | collective-permute-start | bytes 196616 | tf_op jit(solution)/shard_map/ppermute | solution.py:606
  12.7 4.1 %collective-permute-start.3 = (bf16[256,128]{1,0:T(8,128)(2,1)S(1)}, bf16[256,128]{1,0:T(8,128)(2,1)S(1)}, u32[]{:S(2)}, u32[]{:S(2)}) collective-permute-start(bf16[256,128]{1,0:T(8,128)(2,1)S(1)} %get-tuple-element.70.s1_ref), channel_id=1, source_target_pairs={{0,15},{1,2},{2,1},{3,4},{4,3},{5,6},{6,5},{7,8},{8,7},{9,10},{10,... | collective-permute-start | bytes 196616 | tf_op jit(solution)/shard_map/ppermute | solution.py:606
  16.8 1.0 %shard_map.114 = (bf16[768,1024]{1,0:T(8,128)(2,1)S(1)}, f32[128,1024]{1,0:T(8,128)S(1)}) custom-call(bf16[256,1024]{1,0:T(8,128)(2,1)S(1)} %get-tuple-element.60.a_ref, bf16[384,768]{1,0:T(8,128)(2,1)S(1)} %shard_map.111.w_ref), custom_call_target="tpu_custom_call" | custom-call | tf_op jit(solution)/shard_map/pallas_call | solution.py:651
  17.8 1.4 %collective-permute-done.3.k1_ref = bf16[256,128]{1,0:T(8,128)(2,1)S(1)} collective-permute-done((bf16[256,128]{1,0:T(8,128)(2,1)S(1)}, bf16[256,128]{1,0:T(8,128)(2,1)S(1)}, u32[]{:S(2)}, u32[]{:S(2)}) %collective-permute-start.3) | collective-permute-done | bytes 65568 | tf_op jit(solution)/shard_map/ppermute | solution.py:606
  19.1 2.1 %shard_map.115 = (bf16[64,8,128]{2,1,0:T(8,128)(2,1)S(1)}, bf16[768,384]{1,0:T(8,128)(2,1)S(1)}, f32[64,8,128]{2,1,0:T(8,128)S(1)}, bf16[256,1024]{1,0:T(8,128)(...) custom-call(bf16[256,128]{1,0:T(8,128)(2,1)S(1)} %collective-permute-done.r0_ref,, ...), custom_call_target="tpu_custom_call" | custom-call | tf_op jit(solution)/shard_map/pallas_call | solution.py:686
  21.2 5.9 %collective-permute-start.4 = (bf16[416,128]{1,0:T(8,128)(2,1)S(1)}, bf16[416,128]{1,0:T(8,128)(2,1)S(1)}, u32[]{:S(2)}, u32[]{:S(2)}) collective-permute-start(bf16[416,128]{1,0:T(8,128)(2,1)S(1)} %get-tuple-element.76), channel_id=1, source_target_pairs={{0,16},{16,0},{32,48},{48,32},{64,80},{80,64},{96,112},{112,96},{1... | collective-permute-start | bytes 319496 | tf_op jit(solution)/shard_map/ppermute | solution.py:606
  27.1 0.5 shard_map.116
  27.6 1.0 %shard_map.118 = (bf16[768,1024]{1,0:T(8,128)(2,1)S(1)}, f32[128,1024]{1,0:T(8,128)S(1)}) custom-call(bf16[256,1024]{1,0:T(8,128)(2,1)S(1)} %get-tuple-element.82.a_ref, bf16[384,768]{1,0:T(8,128)(2,1)S(1)} %shard_map.111.w_ref), custom_call_target="tpu_custom_call" | custom-call | tf_op jit(solution)/shard_map/pallas_call | solution.py:651
  28.6 1.2 %shard_map.117.refs_0_ = f32[1168,256]{1,0:T(8,128)S(1)} custom-call(bf16[3,64,8,128]{3,2,1,0:T(8,128)(2,1)S(1)} %copy-done.2, bf16[64,8,128]{2,1,0:T(8,128)(2,1)S(1)} %get-tuple-element.78.refs_1_, bf16[768,1024]{1,0:T(8,128)(2,1)S(1)} %get-tuple-element.79.refs_2_, bf16[768,384]{1,0:T(8,128)(2,1)S(1)} %get-tuple-element.80.refs_3_), custom_call_target="tpu_custom_call" | custom-call | tf_op jit(solution)/shard_map/pallas_call | solution.py:662
  29.8 0.9 %shard_map.119.acc_ref = f32[1168,256]{1,0:T(8,128)S(1)} custom-call(f32[1168,256]{1,0:T(8,128)S(1)} %shard_map.117.refs_0_, bf16[3,64,8,128]{3,2,1,0:T(8,128)(2,1)S(1)} %copy-done.2, bf16[64,8,128]{2,1,0:T(8,128)(2,1)S(1)} %get-tuple-element.81.refs_2_.h2_ref, bf16[768,1024]{1,0:T(8,128)(2,1)S(1)} %get-tuple-element.83.refs_3_), custom_call_target="tpu_custom_call", output_to_operand_aliasing={{}: (0, {})} | custom-call | tf_op jit(solution)/shard_map/pallas_call | solution.py:662
  30.7 0.8 %collective-permute-done.5.r1_ref = bf16[416,128]{1,0:T(8,128)(2,1)S(1)} collective-permute-done((bf16[416,128]{1,0:T(8,128)(2,1)S(1)}, bf16[416,128]{1,0:T(8,128)(2,1)S(1)}, u32[]{:S(2)}, u32[]{:S(2)}) %collective-permute-start.5) | collective-permute-done | bytes 106528 | tf_op jit(solution)/shard_map/ppermute | solution.py:606
  31.5 2.1 %shard_map.120 = (bf16[64,8,128]{2,1,0:T(8,128)(2,1)S(1)}, bf16[768,384]{1,0:T(8,128)(2,1)S(1)}, f32[64,8,128]{2,1,0:T(8,128)S(1)}, bf16[256,1024]{1,0:T(8,128)(...) custom-call(bf16[416,128]{1,0:T(8,128)(2,1)S(1)} %collective-permute, ...), custom_call_target="tpu_custom_call" | custom-call | tf_op jit(solution)/shard_map/pallas_call | solution.py:698
  33.6 2.4 %shard_map.122 = bf16[1280,256]{1,0:T(8,128)(2,1)} custom-call(f32[1168,256]{1,0:T(8,128)S(1)} %shard_map.119.acc_ref, bf16[3,64,8,128]{3,2,1,0:T(8,128)(2,1)S(1)} %copy-done.2, bf16[64,8,128]{2,1,0:T(8,128)(2,1)S(1)} %get-tuple-element.81.refs_2_.h2_ref, bf16[768,384]{1,0:T(8,128)(2,1)S(1)} %get-tuple-element.100.b_ref, bf16[64,8,128]{2,1,0:T(8,128)(2,1)S(1)} %copy-done.6, ...), custom_call_target="tpu_custom_call" | custom-call | tf_op jit(solution)/shard_map/pallas_call | solution.py:706
  36.1 5.5 %all-to-all-start = ((bf16[16,80,256]{2,1,0:T(8,128)(2,1)}), bf16[16,80,256]{2,1,0:T(8,128)(2,1)S(1)}, u32[]{:S(2)}, u32[]{:S(2)}) async-start(bf16[16,80,256]{2,1,0:T(8,128)(2,1)} %bitcast), calls=%async_computation | async-start | bytes 1310720 | tf_op jit(solution)/shard_map/all_to_all | solution.py:714
  41.5 1.6 %collective-permute-start.6 = (bf16[256,128]{1,0:T(8,128)(2,1)S(1)}, bf16[256,128]{1,0:T(8,128)(2,1)S(1)}, u32[]{:S(2)}, u32[]{:S(2)}) collective-permute-start(bf16[256,128]{1,0:T(8,128)(2,1)S(1)} %get-tuple-element.93), channel_id=1, source_target_pairs={{0,16},{16,0},{32,48},{48,32},{64,80},{80,64},{96,112},{112,96},{1... | collective-permute-start | bytes 196616 | tf_op jit(solution)/shard_map/ppermute | solution.py:606
  43.1 1.9 %shard_map.123 = (bf16[768,1024]{1,0:T(8,128)(2,1)}, f32[128,1024]{1,0:T(8,128)S(1)}) custom-call(bf16[256,1024]{1,0:T(8,128)(2,1)S(1)} %get-tuple-element.101.a_ref, bf16[384,768]{1,0:T(8,128)(2,1)S(1)} %shard_map.111.w_ref), custom_call_target="tpu_custom_call" | custom-call | tf_op jit(solution)/shard_map/pallas_call | solution.py:651
  45.0 2.1 %collective-permute-done.7.r1_ref = bf16[256,128]{1,0:T(8,128)(2,1)S(1)} collective-permute-done((bf16[256,128]{1,0:T(8,128)(2,1)S(1)}, bf16[256,128]{1,0:T(8,128)(2,1)S(1)}, u32[]{:S(2)}, u32[]{:S(2)}) %collective-permute-start.7) | collective-permute-done | bytes 65568 | tf_op jit(solution)/shard_map/ppermute | solution.py:606
  47.3 5.9 %all-to-all-done = bf16[16,80,256]{2,1,0:T(8,128)(2,1)S(1)} async-done(((bf16[16,80,256]{2,1,0:T(8,128)(2,1)}), bf16[16,80,256]{2,1,0:T(8,128)(2,1)S(1)}, u32[]{:S(2)}, u32[]{:S(2)}) %all-to-all-start) | async-done | bytes 655392 | tf_op jit(solution)/shard_map/all_to_all | solution.py:714
  53.2 0.8 %shard_map.124 = f32[256,80]{1,0:T(8,128)} custom-call(bf16[1280,256]{1,0:T(8,128)(2,1)S(1)} %bitcast.5), custom_call_target="tpu_custom_call" | custom-call | tf_op jit(solution)/shard_map/pallas_call | solution.py:719
  54.0 6.0 %all-to-all-start.1 = ((f32[16,16,80]{2,1,0:T(8,128)}), f32[16,16,80]{2,1,0:T(8,128)S(1)}, u32[]{:S(2)}, u32[]{:S(2)}) async-start(f32[16,16,80]{2,1,0:T(8,128)} %bitcast.2), calls=%async_computation.1 | async-start | bytes 262144 | tf_op jit(solution)/shard_map/all_to_all | solution.py:720
  60.0 0.9 %collective-permute-start.9 = (bf16[256,128]{1,0:T(8,128)(2,1)S(1)}, bf16[256,128]{1,0:T(8,128)(2,1)S(1)}, u32[]{:S(2)}, u32[]{:S(2)}) collective-permute-start(bf16[256,128]{1,0:T(8,128)(2,1)S(1)} %get-tuple-element.98), channel_id=1, source_target_pairs={{0,15},{1,2},{2,1},{3,4},{4,3},{5,6},{6,5},{7,8},{8,7},{9,10},{10,... | collective-permute-start | bytes 196616 | tf_op jit(solution)/shard_map/ppermute | solution.py:606
  60.9 5.9 %collective-permute-done.9.k1_ref = bf16[256,128]{1,0:T(8,128)(2,1)S(1)} collective-permute-done((bf16[256,128]{1,0:T(8,128)(2,1)S(1)}, bf16[256,128]{1,0:T(8,128)(2,1)S(1)}, u32[]{:S(2)}, u32[]{:S(2)}) %collective-permute-start.9) | collective-permute-done | bytes 65568 | tf_op jit(solution)/shard_map/ppermute | solution.py:606
  66.8 1.8 %shard_map.125 = (bf16[3,64,8,128]{3,2,1,0:T(8,128)(2,1)}, f32[64,8,128]{2,1,0:T(8,128)}, f32[64,8,128]{2,1,0:T(8,128)}) custom-call(bf16[64,8,128]{2,1,0:T(8,128)(2,1)S(1)} %get-tuple-element.90.gi1_ref, bf16[64,8,128]{2,1,0:T(8,128)(2,1)S(1)} %get-tuple-element.91.gi2_ref, f32[64,8,128]{2,1,0:T(8,128)S(1)} %get-tuple-element.92.dc_ref, ...), custom_call_target="tpu_custom_call" | custom-call | tf_op jit(solution)/shard_map/pallas_call | solution.py:722
  68.6 0.3 all-to-all-done.1
  68.9 0.7 shard_map.126
  (27 shorter events, 0.5 us)
Async XLA Ops:
  0.6 7.4 %copy-start = (bf16[3,256,8,128]{3,2,1,0:T(8,128)(2,1)S(1)}, bf16[3,256,8,128]{3,2,1,0:T(8,128)(2,1)}, u32[]{:S(2)}) copy-start(bf16[3,256,8,128]{3,2,1,0:T(8,128)(2,1)} %pre_ref.7) | copy-start | bytes 4718596
  0.6 7.4 %copy-start.1 = (bf16[3,64,8,128]{3,2,1,0:T(8,128)(2,1)S(1)}, bf16[3,64,8,128]{3,2,1,0:T(8,128)(2,1)}, u32[]{:S(2)}) copy-start(bf16[3,64,8,128]{3,2,1,0:T(8,128)(2,1)} %cot_ref.5) | copy-start | bytes 1179652
  0.7 7.4 %copy-start.2 = (bf16[3,64,8,128]{3,2,1,0:T(8,128)(2,1)S(1)}, bf16[3,64,8,128]{3,2,1,0:T(8,128)(2,1)}, u32[]{:S(2)}) copy-start(bf16[3,64,8,128]{3,2,1,0:T(8,128)(2,1)} %x_ref.3) | copy-start | bytes 1179652
  3.4 7.6 %collective-permute-start = (bf16[256,128]{1,0:T(8,128)(2,1)S(1)}, bf16[256,128]{1,0:T(8,128)(2,1)S(1)}, u32[]{:S(2)}, u32[]{:S(2)}) collective-permute-start(bf16[256,128]{1,0:T(8,128)(2,1)S(1)} %get-tuple-element.58), channel_id=1, source_target_pairs={{0,16},{16,0},{32,48},{48,32},{64,80},{80,64},{96,112},{112,96},{1... | collective-permute-start | bytes 196616 | tf_op jit(solution)/shard_map/ppermute | solution.py:606
  6.7 4.3 %collective-permute-start.1 = (bf16[256,128]{1,0:T(8,128)(2,1)S(1)}, bf16[256,128]{1,0:T(8,128)(2,1)S(1)}, u32[]{:S(2)}, u32[]{:S(2)}) collective-permute-start(bf16[256,128]{1,0:T(8,128)(2,1)S(1)} %get-tuple-element.59), channel_id=1, source_target_pairs={{0,240},{16,32},{32,16},{48,64},{64,48},{80,96},{96,80},{112,128},... | collective-permute-start | bytes 196616 | tf_op jit(solution)/shard_map/ppermute | solution.py:606
  6.7 1.1 %copy-start.4 = (bf16[256,1152]{1,0:T(8,128)(2,1)S(1)}, bf16[256,1152]{1,0:T(8,128)(2,1)}, u32[]{:S(2)}) copy-start(bf16[256,1152]{1,0:T(8,128)(2,1)} %k_ref.1) | copy-start | bytes 1769476
  8.0 0.9 %copy-start.5 = (bf16[64,8,128]{2,1,0:T(8,128)(2,1)S(1)}, bf16[64,8,128]{2,1,0:T(8,128)(2,1)}, u32[]{:S(2)}) copy-start(bf16[64,8,128]{2,1,0:T(8,128)(2,1)} %h_ref.3) | copy-start | bytes 393220
  9.0 0.7 copy-start.7
  11.4 6.4 %collective-permute-start.2 = (bf16[256,128]{1,0:T(8,128)(2,1)S(1)}, bf16[256,128]{1,0:T(8,128)(2,1)S(1)}, u32[]{:S(2)}, u32[]{:S(2)}) collective-permute-start(bf16[256,128]{1,0:T(8,128)(2,1)S(1)} %get-tuple-element.69.s0_ref), channel_id=1, source_target_pairs={{0,1},{1,0},{2,3},{3,2},{4,5},{5,4},{6,7},{7,6},{8,9},{9,8},{10,11... | collective-permute-start | bytes 196616 | tf_op jit(solution)/shard_map/ppermute | solution.py:606
  12.7 6.4 %collective-permute-start.3 = (bf16[256,128]{1,0:T(8,128)(2,1)S(1)}, bf16[256,128]{1,0:T(8,128)(2,1)S(1)}, u32[]{:S(2)}, u32[]{:S(2)}) collective-permute-start(bf16[256,128]{1,0:T(8,128)(2,1)S(1)} %get-tuple-element.70.s1_ref), channel_id=1, source_target_pairs={{0,15},{1,2},{2,1},{3,4},{4,3},{5,6},{6,5},{7,8},{8,7},{9,10},{10,... | collective-permute-start | bytes 196616 | tf_op jit(solution)/shard_map/ppermute | solution.py:606
  21.2 9.5 %collective-permute-start.4 = (bf16[416,128]{1,0:T(8,128)(2,1)S(1)}, bf16[416,128]{1,0:T(8,128)(2,1)S(1)}, u32[]{:S(2)}, u32[]{:S(2)}) collective-permute-start(bf16[416,128]{1,0:T(8,128)(2,1)S(1)} %get-tuple-element.76), channel_id=1, source_target_pairs={{0,16},{16,0},{32,48},{48,32},{64,80},{80,64},{96,112},{112,96},{1... | collective-permute-start | bytes 319496 | tf_op jit(solution)/shard_map/ppermute | solution.py:606
  27.1 4.4 %collective-permute-start.5 = (bf16[416,128]{1,0:T(8,128)(2,1)S(1)}, bf16[416,128]{1,0:T(8,128)(2,1)S(1)}, u32[]{:S(2)}, u32[]{:S(2)}) collective-permute-start(bf16[416,128]{1,0:T(8,128)(2,1)S(1)} %get-tuple-element.77), channel_id=1, source_target_pairs={{0,240},{16,32},{32,16},{48,64},{64,48},{80,96},{96,80},{112,128},... | collective-permute-start | bytes 319496 | tf_op jit(solution)/shard_map/ppermute | solution.py:606
  29.8 1.7 %copy-start.3 = (f32[64,8,128]{2,1,0:T(8,128)S(1)}, f32[64,8,128]{2,1,0:T(8,128)}, u32[]{:S(2)}) copy-start(f32[64,8,128]{2,1,0:T(8,128)} %before_ref.1) | copy-start | bytes 786436
  29.8 1.7 %copy-start.8 = (s32[8,128]{1,0:T(8,128)S(1)}, s32[8,128]{1,0:T(8,128)}, u32[]{:S(2)}) copy-start(s32[8,128]{1,0:T(8,128)} %mask_ref.7) | copy-start | bytes 12292
  31.5 2.1 %copy-start.6 = (bf16[64,8,128]{2,1,0:T(8,128)(2,1)S(1)}, bf16[64,8,128]{2,1,0:T(8,128)(2,1)}, u32[]{:S(2)}) copy-start(bf16[64,8,128]{2,1,0:T(8,128)(2,1)} %h_ref.3) | copy-start | bytes 393220
  36.1 17.1 %all-to-all-start = ((bf16[16,80,256]{2,1,0:T(8,128)(2,1)}), bf16[16,80,256]{2,1,0:T(8,128)(2,1)S(1)}, u32[]{:S(2)}, u32[]{:S(2)}) async-start(bf16[16,80,256]{2,1,0:T(8,128)(2,1)} %bitcast), calls=%async_computation | async-start | bytes 1310720 | tf_op jit(solution)/shard_map/all_to_all | solution.py:714
  41.5 3.4 %collective-permute-start.6 = (bf16[256,128]{1,0:T(8,128)(2,1)S(1)}, bf16[256,128]{1,0:T(8,128)(2,1)S(1)}, u32[]{:S(2)}, u32[]{:S(2)}) collective-permute-start(bf16[256,128]{1,0:T(8,128)(2,1)S(1)} %get-tuple-element.93), channel_id=1, source_target_pairs={{0,16},{16,0},{32,48},{48,32},{64,80},{80,64},{96,112},{112,96},{1... | collective-permute-start | bytes 196616 | tf_op jit(solution)/shard_map/ppermute | solution.py:606
  43.1 4.0 %collective-permute-start.7 = (bf16[256,128]{1,0:T(8,128)(2,1)S(1)}, bf16[256,128]{1,0:T(8,128)(2,1)S(1)}, u32[]{:S(2)}, u32[]{:S(2)}) collective-permute-start(bf16[256,128]{1,0:T(8,128)(2,1)S(1)} %get-tuple-element.94), channel_id=1, source_target_pairs={{0,240},{16,32},{32,16},{48,64},{64,48},{80,96},{96,80},{112,128},... | collective-permute-start | bytes 196616 | tf_op jit(solution)/shard_map/ppermute | solution.py:606
  54.0 14.9 %all-to-all-start.1 = ((f32[16,16,80]{2,1,0:T(8,128)}), f32[16,16,80]{2,1,0:T(8,128)S(1)}, u32[]{:S(2)}, u32[]{:S(2)}) async-start(f32[16,16,80]{2,1,0:T(8,128)} %bitcast.2), calls=%async_computation.1 | async-start | bytes 262144 | tf_op jit(solution)/shard_map/all_to_all | solution.py:720
  60.0 6.8 %collective-permute-start.9 = (bf16[256,128]{1,0:T(8,128)(2,1)S(1)}, bf16[256,128]{1,0:T(8,128)(2,1)S(1)}, u32[]{:S(2)}, u32[]{:S(2)}) collective-permute-start(bf16[256,128]{1,0:T(8,128)(2,1)S(1)} %get-tuple-element.98), channel_id=1, source_target_pairs={{0,15},{1,2},{2,1},{3,4},{4,3},{5,6},{6,5},{7,8},{8,7},{9,10},{10,... | collective-permute-start | bytes 196616 | tf_op jit(solution)/shard_map/ppermute | solution.py:606
  60.9 5.9 %collective-permute-start.8 = (bf16[256,128]{1,0:T(8,128)(2,1)S(1)}, bf16[256,128]{1,0:T(8,128)(2,1)S(1)}, u32[]{:S(2)}, u32[]{:S(2)}) collective-permute-start(bf16[256,128]{1,0:T(8,128)(2,1)S(1)} %get-tuple-element.97), channel_id=1, source_target_pairs={{0,1},{1,0},{2,3},{3,2},{4,5},{5,4},{6,7},{7,6},{8,9},{9,8},{10,11... | collective-permute-start | bytes 196616 | tf_op jit(solution)/shard_map/ppermute | solution.py:606
